TPU v7x, 256 devices: a whole 4x4x8 slice. The times are simulated.
256 devices in a mesh: slab: 64 (over x, z, core), img: 4 (over y).
Axes of the slice: x: 4, y: 4, z: 8, core: 2. Of those that a mesh axis runs over, the one named last changes fastest.
Arguments:
- volume: bfloat16 [32768, 256], P('slab'), may hold values from -6 to 6
- interp: bfloat16 [4, 64, 16, 32768], P('img', None, None, 'slab'), may hold values from -0.09375 to 0.09375
- block_index: int32 [4, 64, 64], P('img'), may hold values from 0 to 7
- images: bfloat16 [4, 1024, 128, 256], P('img', 'slab'), may hold values from -6 to 6
- defocus: float32 [4, 1024], P('img', 'slab'), may hold values from 5000 to 25000
- orient: int32 [4, 1024, 4], P('img', 'slab'), may hold values from 0 to 63, all different within a row
Outputs:
- update: float32 [32768, 256], P('slab')
- weights: float32 [4, 1024, 64], P('img', 'slab')
Inputs may be any that keep to these rules, and one draw needn't show every extreme that they name: `orient`: each image lists 4 different orientations of its group.
All inputs are finite; a program needn't handle non-finite values.
Results may differ from a plain program's by a relative error of at most 0.0077.
Values may be sent and summed in bfloat16 or wider, within the bound.
A program may use at most 64 MiB of HBM per device.

v0:
```python
import math

import jax
import jax.numpy as jnp
from jax import lax
from jax.sharding import PartitionSpec as P

BOX = 256
NS = 16


wave_length = 0.0197
aberration = 27000000.0
amplitude = 0.1
grid_side = 4


def phase_tables(fourier, shifts, box):
    freq = (jnp.arange(fourier, dtype=jnp.int32) - fourier // 2).astype(jnp.float32)
    shift_steps = jnp.arange(shifts, dtype=jnp.int32)
    shift_x = (2 * (shift_steps // grid_side) - (grid_side - 1)).astype(jnp.float32)
    shift_y = (2 * (shift_steps % grid_side) - (grid_side - 1)).astype(jnp.float32)
    angle = 2.0 * math.pi / box * (freq[:, None, None] * shift_x + freq[None, :, None] * shift_y)
    forward = jnp.stack([jnp.cos(angle), jnp.sin(angle)], axis=1).reshape(
        2 * fourier * fourier, shifts
    )
    backward = jnp.stack([jnp.cos(angle), -jnp.sin(angle)], axis=1).reshape(
        2 * fourier * fourier, shifts
    )
    return (forward.astype(jnp.bfloat16), backward.T.astype(jnp.bfloat16))


def contrast(defocus_blk, fourier, box):
    freq = (jnp.arange(fourier, dtype=jnp.int32) - fourier // 2).astype(jnp.float32)
    wave_sq = (freq[:, None] * freq[:, None] + freq[None, :] * freq[None, :]) / (box * box)
    phase = math.pi * wave_length * defocus_blk[:, None, None] * wave_sq
    phase = phase - 0.5 * math.pi * aberration * wave_length**3 * wave_sq * wave_sq
    return -(math.sqrt(1.0 - amplitude * amplitude) * jnp.sin(phase) + amplitude * jnp.cos(phase))


def correlate(panels, image_blk, list_blk, defocus_blk, phase_fwd, phase_back, box):
    count = image_blk.shape[0]
    fourier = image_blk.shape[1]
    picks = list_blk.shape[1]
    shifts = phase_fwd.shape[1]
    ctf = contrast(defocus_blk, fourier, box)
    weighted = ctf[:, :, None, :] * image_blk.astype(jnp.float32).reshape(
        count, fourier, 2, fourier
    )
    real_u = weighted[:, None, :, 0]
    imag_u = weighted[:, None, :, 1]
    chosen = panels[list_blk].astype(jnp.float32).reshape(count, picks, fourier, 2, fourier)
    real_p = chosen[:, :, :, 0]
    imag_p = chosen[:, :, :, 1]
    product = jnp.stack(
        [real_p * real_u + imag_p * imag_u, real_p * imag_u - imag_p * real_u], axis=3
    )
    product = product.astype(jnp.bfloat16).reshape(count * picks, 2 * fourier * fourier)
    scores = jnp.dot(product, phase_fwd, preferred_element_type=jnp.float32) / fourier
    scores = scores.reshape(count, picks * shifts)
    squared = scores * scores
    weights = squared / (jnp.mean(squared, axis=1, keepdims=True) + 1e-05)
    rounded = weights.astype(jnp.bfloat16).reshape(count * picks, shifts)
    spread = jnp.dot(rounded, phase_back, preferred_element_type=jnp.float32)
    spread = spread.reshape(count, picks, fourier, 2, fourier)
    real_e = spread[:, :, :, 0]
    imag_e = spread[:, :, :, 1]
    backed = jnp.stack(
        [real_u * real_e - imag_u * imag_e, real_u * imag_e + imag_u * real_e], axis=3
    )
    backed = backed.astype(jnp.bfloat16).reshape(count * picks, 2 * fourier * fourier)
    return (weights, backed)


def on_device(volume, interp, block_index, images, defocus, orient):
    slab_count = lax.axis_size("slab")
    slab_index = lax.axis_index("slab")
    orient_count = interp.shape[1]
    ori_dev = orient_count // slab_count
    block_rows = interp.shape[2]
    fourier = images.shape[2]
    block_count = fourier // block_rows
    img_dev = images.shape[1]
    picks = orient.shape[2]
    levels = jnp.arange(block_count, dtype=jnp.int32)
    partial_value = jnp.einsum("jpr,rx->jpx", interp[0], volume, preferred_element_type=jnp.float32)
    own_blocks = lax.dynamic_index_in_dim(block_index[0], slab_index, axis=1, keepdims=False)
    owned_idx = lax.dynamic_slice_in_dim(block_index[0], slab_index * ori_dev, ori_dev, 0)
    chosen = (own_blocks[:, None] == levels[None, :]).astype(jnp.float32)
    summed = lax.psum_scatter(
        (chosen[:, :, None, None] * partial_value[:, None]).reshape(
            lax.axis_size("slab") * ori_dev, fourier, 2 * fourier
        ),
        "slab",
        scatter_dimension=0,
        tiled=True,
    )
    panels = lax.all_gather(summed.astype(jnp.bfloat16), "slab", axis=0, tiled=True)
    phase_fwd, phase_back = phase_tables(fourier, NS, BOX)
    blk = math.gcd(img_dev, 32)
    blk_total = img_dev // blk

    def per_block(pieces):
        image_blk, list_blk, defocus_blk = pieces
        return correlate(panels, image_blk, list_blk, defocus_blk, phase_fwd, phase_back, BOX)

    weights, backs = lax.map(
        per_block,
        (
            images[0].reshape(blk_total, blk, fourier, 2 * fourier),
            orient[0].reshape(blk_total, blk, picks),
            defocus[0].reshape(blk_total, blk),
        ),
    )
    all_slices = backs.reshape(img_dev * picks, 2 * fourier * fourier)
    member = (
        orient[0].reshape(-1)[:, None] == jnp.arange(orient_count, dtype=jnp.int32)[None, :]
    ).astype(jnp.bfloat16)
    back_own = lax.psum_scatter(
        lax.dot_general(
            member, all_slices, (((0,), (0,)), ((), ())), preferred_element_type=jnp.float32
        ),
        "slab",
        scatter_dimension=0,
        tiled=True,
    ).astype(jnp.bfloat16)
    back_own = back_own.reshape(ori_dev, block_count, block_rows, 2 * fourier)
    chosen_back = (owned_idx[:, :, None] == levels).astype(jnp.bfloat16)
    outgoing = jnp.einsum(
        "osb,obpx->sopx", chosen_back, back_own, preferred_element_type=jnp.float32
    )
    outgoing = outgoing.astype(jnp.bfloat16).reshape(slab_count * ori_dev, block_rows, 2 * fourier)
    incoming = lax.all_to_all(outgoing, "slab", split_axis=0, concat_axis=0, tiled=True)
    column = jnp.einsum("jpr,jpx->rx", interp[0], incoming, preferred_element_type=jnp.float32)
    summed_cols = lax.psum(column, "img")
    update = summed_cols / math.sqrt(img_dev * slab_count)
    return (update, weights)


def solution(mesh):
    return jax.shard_map(
        on_device,
        mesh=mesh,
        in_specs=(
            P("slab", None),
            P("img", None, None, "slab"),
            P("img", None, None),
            P("img", "slab", None, None),
            P("img", "slab"),
            P("img", "slab", None),
        ),
        out_specs=(P("slab", None), P("img", "slab", None)),
        check_vma=False,
    )
```

profile of v0, /device:TPU:6, one launch (start us, length us, event | category | flops | bytes accessed | tf_op | source)
XLA Modules:
  0.0 703.2 jit_solution(17142144156621512723)
XLA Ops:
  7.2 1.0 dynamic-slice_reduce_fusion
  8.4 1.4 fusion.7
  9.8 3.9 bitcast_multiply_fusion
  13.7 153.4 %reduce-scatter.2.cloned.1.call-done = f32[1,128,256]{2,1,0:T(8,128)} async-done(((f32[64,128,256]{2,1,0:T(8,128)}), f32[1,128,256]{2,1,0:T(8,128)}) %reduce-scatter.2.cloned.1.call-update) | async-done | bytes 131088 | tf_op jit(solution)/shard_map/reduce_scatter | solution.py:90
  167.1 1.5 convert_element_type.137
  168.9 0.1 reshape.431
  169.0 2.1 reshape.427
  171.2 0.1 copy.57
  171.3 5.4 fusion.10
  176.7 0.8 copy-done.2
  177.5 0.1 pad_maximum_fusion.3
  177.6 1.9 copy.58
  179.5 2.6 convert_element_type.143
  182.2 0.6 dynamic-slice.2
  182.8 0.7 dynamic-slice_bitcast_fusion
  183.6 3.9 add_negate_fusion
  187.5 1.2 copy_multiply_fusion
  188.7 1.1 slice_bitcast_fusion.1
  189.8 57.2 %all-gather.2.cloned.1.call-done = bf16[64,128,256]{2,1,0:T(8,128)(2,1)} async-done(((bf16[1,128,256]{2,1,0:T(8,128)(2,1)}), bf16[64,128,256]{2,1,0:T(8,128)(2,1)}) %all-gather.2.cloned.1.call-update) | async-done | bytes 4194320 | tf_op jit(solution)/shard_map/all_gather | solution.py:98
  247.0 4.9 gather_fusion
  251.9 7.0 copy.53
  258.9 7.8 %fusion.30 = (f32[16,4,128,1,128]{2,4,3,1,0:T(8,128)}, f32[16,4,128,1,128]{2,4,3,1,0:T(8,128)}) fusion(f32[16,4,128,2,128]{2,4,3,1,0:T(8,128)} %bitcast.54), kind=kLoop, calls=%fused_computation.71 | loop fusion | bytes 16777216 | tf_op jit(solution)/shard_map/while/body/eval_jaxpr/slice | solution.py:53
  266.7 5.5 copy.73
  272.2 5.5 copy.74
  277.6 4.9 add_convert_fusion.1
  282.5 0.4 pad_maximum_fusion
  282.9 6.6 copy.56
  289.5 7.8 %convert_element_type.140 = bf16[64,32768]{1,0:T(8,128)(2,1)} reshape(bf16[16,4,128,2,128]{4,3,2,1,0:T(2,128)(2,1)} %copy.56) | data formatting | bytes 8388608 | tf_op jit(solution)/shard_map/while/body/eval_jaxpr/convert_element_type | solution.py:58
  297.3 3.7 fusion.31
  301.1 0.1 reduce_sum.19
  301.3 0.1 div.68
  301.4 0.1 copy.59
  301.6 2.4 fusion.3
  303.9 1.5 subtract_convert_fusion
  305.4 0.4 pad_maximum_fusion.1
  305.8 6.5 copy.61
  312.3 7.9 %convert_element_type.145 = bf16[64,32768]{1,0:T(8,128)(2,1)} reshape(bf16[16,4,128,2,128]{4,3,2,1,0:T(2,128)(2,1)} %copy.61) | data formatting | bytes 8388608 | tf_op jit(solution)/shard_map/while/body/eval_jaxpr/convert_element_type | solution.py:71
  320.2 6.8 fusion.15
  327.0 258.8 %all-reduce.5 = bf16[64,32768]{1,0:T(8,128)(2,1)} all-reduce(f32[64,32768]{1,0:T(8,128)} %fusion.15), channel_id=3, replica_groups=mesh['slab'=64,'img'=4] {'slab'}, use_global_device_ids=true, to_apply=%region_3.4.clone | all-reduce | flops 2097152 | bytes 12582912
  585.7 2.1 fusion.12
  587.9 0.3 fusion
  588.2 0.3 copy.63
  588.5 59.0 %all_to_all.5 = bf16[64,16,256]{2,1,0:T(8,128)(2,1)S(1)} all-to-all(bf16[64,16,256]{2,1,0:T(8,128)(2,1)S(1)} %copy.63), channel_id=1, replica_groups=mesh['slab'=64,'img'=4] {'slab'}, dimensions={0} | all-to-all | bytes 1048576 | tf_op jit(solution)/shard_map/all_to_all | solution.py:133
  647.5 1.2 convolution_bitcast_fusion
  648.9 0.7 broadcast_divide_fusion
  649.6 45.0 %all-reduce.4.cloned.1.call-done = f32[512,256]{0,1:T(8,128)} async-done(((f32[512,256]{0,1:T(8,128)}), f32[512,256]{0,1:T(8,128)}) %all-reduce.4.cloned.1.call-update) | async-done | bytes 524304 | tf_op jit(solution)/shard_map/psum | solution.py:135
  694.6 1.1 broadcast_multiply_fusion
  695.7 1.0 copy.67
  (40 shorter events, 1.1 us)
Async XLA Ops:
  7.2 1.2 copy-start
  7.2 159.9 %reduce-scatter.2.cloned.1.call-start = ((), (), s32[]{:S(2)}) async-start(), calls=%async_computation.2 | async-start | bytes 8519680 | tf_op jit(solution)/shard_map/reduce_scatter | solution.py:90
  13.7 155.1 %copy-start.4 = (s32[1,16,4]{1,2,0:T(4,128)S(1)}, s32[1,16,4]{1,2,0:T(4,128)}, u32[]{:S(2)}) copy-start(s32[1,16,4]{1,2,0:T(4,128)} %param.11) | copy-start | bytes 772
  13.7 233.3 %all-gather.2.cloned.1.call-start = ((), (), s32[]{:S(2)}) async-start(), calls=%async_computation.3 | async-start | bytes 4259840 | tf_op jit(solution)/shard_map/all_gather | solution.py:98
  168.7 526.0 %all-reduce.4.cloned.1.call-start = ((), (), s32[]{:S(2)}) async-start(), calls=%async_computation.4 | async-start | bytes 1048576 | tf_op jit(solution)/shard_map/psum | solution.py:135
  171.1 11.1 %copy-start.6 = (u32[256]{0:T(256)S(1)}, u32[256]{0:T(256)}, u32[]{:S(2)}) copy-start(u32[256]{0:T(256)} %constant.117) | copy-start | bytes 3076
  171.1 12.4 %copy-start.5 = (f32[1,16]{1,0:T(1,128)S(1)}, f32[1,16]{1,0:T(1,128)}, u32[]{:S(2)}) copy-start(f32[1,16]{1,0:T(1,128)} %param.10) | copy-start | bytes 196
  176.7 0.8 copy-start.2
  297.3 4.3 copy-start.3
  301.6 2.4 copy-start.1
Sparse Core Ops, SparseCore 0:
  13.8 153.2 reduce-scatter.1
  170.3 76.6 all-gather.1
  648.9 45.6 all-reduce.3
where the time goes:
time: 704 us; the launch traced here: 703 us
  blocking collectives  318 us (45%)
  waiting for transfers between devices  256 us (36%)
  local copies, waits for them, and re-layouts  74.8 us (11%)
  other arithmetic  25.2 us (4%)
  matrix products  15.8 us (2%)
  between operations  14 us (2%)
    unnamed x1, blocking collectives  259 us
    reduce_scatter x1, waiting for transfers between devices, on_device(): lax.psum_scatter((chosen[:, :, None, None] * partial_value[:, None]).resh...  153 us
    all_to_all x1, blocking collectives, on_device(): lax.all_to_all(outgoing, 'slab', split_axis=0, concat_axis=0, tiled=True)  59 us
    all_gather x1, waiting for transfers between devices, on_device(): lax.all_gather(summed.astype(jnp.bfloat16), 'slab', axis=0, tiled=True)  57.2 us
    psum x1, waiting for transfers between devices, on_device(): summed_cols = lax.psum(column, 'img')  45 us
  transfers between devices with their start and end apart: 3, of which 3 were waited for; matrix products, arithmetic and copies ran while one was open for 3% of the time, Pallas kernels for 0%

commit v1 on v0

--- a/solution.py
+++ b/solution.py
@@ -84,17 +84,19 @@
     picks = orient.shape[2]
     levels = jnp.arange(block_count, dtype=jnp.int32)
     partial_value = jnp.einsum("jpr,rx->jpx", interp[0], volume, preferred_element_type=jnp.float32)
-    own_blocks = lax.dynamic_index_in_dim(block_index[0], slab_index, axis=1, keepdims=False)
     owned_idx = lax.dynamic_slice_in_dim(block_index[0], slab_index * ori_dev, ori_dev, 0)
-    chosen = (own_blocks[:, None] == levels[None, :]).astype(jnp.float32)
-    summed = lax.psum_scatter(
-        (chosen[:, :, None, None] * partial_value[:, None]).reshape(
-            lax.axis_size("slab") * ori_dev, fourier, 2 * fourier
-        ),
+    received = lax.all_to_all(
+        partial_value.reshape(slab_count, ori_dev * block_rows, 2 * fourier),
         "slab",
-        scatter_dimension=0,
+        split_axis=0,
+        concat_axis=0,
         tiled=True,
-    )
+    ).reshape(slab_count, ori_dev, block_rows, 2 * fourier)
+    place = (owned_idx[:, :, None] == levels).astype(jnp.float32)
+    summed = jnp.einsum(
+        "osb,sopx->obpx", place, received, precision=lax.Precision.HIGHEST,
+        preferred_element_type=jnp.float32,
+    ).reshape(ori_dev, fourier, 2 * fourier)
     panels = lax.all_gather(summed.astype(jnp.bfloat16), "slab", axis=0, tiled=True)
     phase_fwd, phase_back = phase_tables(fourier, NS, BOX)
     blk = math.gcd(img_dev, 32)
@@ -116,14 +118,10 @@
     member = (
         orient[0].reshape(-1)[:, None] == jnp.arange(orient_count, dtype=jnp.int32)[None, :]
     ).astype(jnp.bfloat16)
-    back_own = lax.psum_scatter(
-        lax.dot_general(
-            member, all_slices, (((0,), (0,)), ((), ())), preferred_element_type=jnp.float32
-        ),
-        "slab",
-        scatter_dimension=0,
-        tiled=True,
-    ).astype(jnp.bfloat16)
+    contrib = lax.dot_general(
+        member, all_slices, (((0,), (0,)), ((), ())), preferred_element_type=jnp.float32
+    ).reshape(orient_count, fourier, 2 * fourier)
+    back_own = lax.psum_scatter(contrib, "slab", scatter_dimension=0, tiled=True).astype(jnp.bfloat16)
     back_own = back_own.reshape(ori_dev, block_count, block_rows, 2 * fourier)
     chosen_back = (owned_idx[:, :, None] == levels).astype(jnp.bfloat16)
     outgoing = jnp.einsum(

time: 704 us -> 445 us (0.63)
  blocking collectives: 318 us -> 25.1 us
  waiting for transfers between devices: 256 us -> 277 us
  starting transfers between devices: 0.12 us -> 12.5 us
    unnamed x1 -> x0, blocking collectives: 259 us -> none
    all_to_all x1, blocking collectives: 59 us -> 25.1 us  [on_device(): lax.all_to_all(outgoing, 'slab', split_axis=0, concat_axis=0, tiled=True)]
    all_to_all x0 -> x1, waiting for transfers between devices: none -> 25.9 us  [on_device(): lax.all_to_all(partial_value.reshape(slab_count, ori_dev * block_rows, 2...]
    all_to_all x0 -> x1, starting transfers between devices: none -> 12.2 us  [on_device(): lax.all_to_all(partial_value.reshape(slab_count, ori_dev * block_rows, 2...]
    dot_general x0 -> x1, local copies, waits for them, and re-layouts: none -> 8.08 us  [on_device(): lax.dot_general(member, all_slices, (((0,), (0,)), ((), ())), preferred_e...]
  transfers between devices with their start and end apart: 3 -> 4, of which waited for: 3 -> 4; matrix products, arithmetic and copies ran while one was open for 3% -> 5% of each run, Pallas kernels for 0% -> 0%
where the time goes in v1:
time: 445 us; the launch traced here: 444 us
  waiting for transfers between devices  277 us (62%)
  local copies, waits for them, and re-layouts  80.9 us (18%)
  blocking collectives  25.1 us (6%)
  other arithmetic  20.7 us (5%)
  matrix products  14.5 us (3%)
  between operations  14 us (3%)
  starting transfers between devices  12.5 us (3%)
    reduce_scatter x1, waiting for transfers between devices, on_device(): lax.psum_scatter(contrib, 'slab', scatter_dimension=0, tiled=True)  149 us
    all_gather x1, waiting for transfers between devices, on_device(): lax.all_gather(summed.astype(jnp.bfloat16), 'slab', axis=0, tiled=True)  56.5 us
    psum x1, waiting for transfers between devices, on_device(): summed_cols = lax.psum(column, 'img')  44.8 us
    all_to_all x1, waiting for transfers between devices, on_device(): lax.all_to_all(partial_value.reshape(slab_count, ori_dev * block_rows, 2...  25.9 us
    all_to_all x1, blocking collectives, on_device(): lax.all_to_all(outgoing, 'slab', split_axis=0, concat_axis=0, tiled=True)  25.1 us
    unnamed x16, local copies, waits for them, and re-layouts  14.1 us
    all_to_all x1, starting transfers between devices, on_device(): lax.all_to_all(partial_value.reshape(slab_count, ori_dev * block_rows, 2...  12.2 us
    another operation x3, other arithmetic  11.8 us
  transfers between devices with their start and end apart: 4, of which 4 were waited for; matrix products, arithmetic and copies ran while one was open for 5% of the time, Pallas kernels for 0%

profile of v1, /device:TPU:6, one launch (start us, length us, event | category | flops | bytes accessed | tf_op | source)
XLA Modules:
  0.0 444.2 jit_solution(18430927952869716344)
XLA Ops:
  7.2 1.2 copy-done
  8.4 2.4 fusion.10
  10.8 12.2 %all-to-all-start = ((f32[64,16,256]{2,1,0:T(8,128)}), f32[64,16,256]{2,1,0:T(8,128)S(1)}, u32[]{:S(2)}, u32[]{:S(2)}) async-start(f32[64,16,256]{2,1,0:T(8,128)} %fusion.10), calls=%async_computation | async-start | bytes 2097152 | tf_op jit(solution)/shard_map/all_to_all | solution.py:88
  23.0 0.7 dynamic-slice_bitcast_fusion
  23.7 25.9 %all-to-all-done = f32[64,16,256]{2,1,0:T(8,128)S(1)} async-done(((f32[64,16,256]{2,1,0:T(8,128)}), f32[64,16,256]{2,1,0:T(8,128)S(1)}, u32[]{:S(2)}, u32[]{:S(2)}) %all-to-all-start) | async-done | bytes 1048608 | tf_op jit(solution)/shard_map/all_to_all | solution.py:88
  49.6 1.0 convolution_convert_fusion.1
  50.6 0.6 copy.62
  51.3 0.2 reduce-scatter.2.cloned.1.call-start
  51.8 2.1 reshape.430
  54.0 0.1 copy.68
  54.1 5.4 %fusion.14 = (bf16[128,1,128,16]{2,3,1,0:T(8,128)(2,1)S(1)}, bf16[128,1,128,16]{2,3,1,0:T(8,128)(2,1)}, bf16[128,1,128,16]{2,3,1,0:T(8,128)(2,1)S(1)}) fusion(f32[128,16]{0,1:T(8,128)S(1)} %get-tuple-element.51, f32[128,16]{1,0:T(8,128)S(1)} %copy.68), kind=kLoop, calls=%fused_computation.32 | loop fusion | flops 1572864 | bytes 1589248 | tf_op jit(solution)/shard_map/convert.7
  59.5 0.8 copy-done.2
  60.4 1.9 copy.69
  62.3 2.6 convert_element_type.148
  65.1 3.9 add_negate_fusion
  69.0 1.2 copy_multiply_fusion
  70.2 1.1 slice_bitcast_fusion.1
  71.4 56.5 %all-gather.2.cloned.1.call-done = bf16[64,128,256]{2,1,0:T(8,128)(2,1)} async-done(((bf16[1,128,256]{2,1,0:T(8,128)(2,1)}), bf16[64,128,256]{2,1,0:T(8,128)(2,1)}) %all-gather.2.cloned.1.call-update) | async-done | bytes 4194320 | tf_op jit(solution)/shard_map/all_gather | solution.py:100
  127.9 5.0 %gather_fusion = bf16[64,128,256]{2,1,0:T(8,128)(2,1)} fusion(bf16[64,128,256]{2,1,0:T(8,128)(2,1)} %all-gather.2.cloned.1.call-done, s32[1024]{0:T(1024)S(1)} %pad_clamp_fusion), kind=kCustom, calls=%fused_computation | custom fusion | bytes 8388864 | tf_op jit(solution)/shard_map/while/body/eval_jaxpr/gather | solution.py:52
  132.8 7.0 %copy.64 = f32[64,128,256]{1,2,0:T(8,128)} copy(bf16[64,128,256]{2,1,0:T(8,128)(2,1)} %gather_fusion) | data formatting | bytes 12582912 | tf_op jit(solution)/shard_map/while/body/eval_jaxpr/convert_element_type | solution.py:52
  139.9 7.8 %fusion.36 = (f32[16,4,128,1,128]{2,4,3,1,0:T(8,128)}, f32[16,4,128,1,128]{2,4,3,1,0:T(8,128)}) fusion(f32[16,4,128,2,128]{2,4,3,1,0:T(8,128)} %bitcast.62), kind=kLoop, calls=%fused_computation.73 | loop fusion | bytes 16777216 | tf_op jit(solution)/shard_map/while/body/eval_jaxpr/slice | solution.py:53
  147.7 5.5 %copy.84 = f32[16,4,128,1,128]{4,0,3,2,1:T(8,128)} copy(f32[16,4,128,1,128]{2,4,3,1,0:T(8,128)} %get-tuple-element.41) | data formatting | bytes 8388608
  153.1 5.5 %copy.85 = f32[16,4,128,1,128]{4,0,3,2,1:T(8,128)} copy(f32[16,4,128,1,128]{2,4,3,1,0:T(8,128)} %get-tuple-element.42) | data formatting | bytes 8388608
  158.6 4.9 %add_convert_fusion.1 = (bf16[16,4,128,1,128]{4,0,3,2,1:T(8,128)(2,1)S(1)}, bf16[16,4,128,1,128]{4,0,3,2,1:T(8,128)(2,1)S(1)}) fusion(f32[16,4,128,1,128]{4,0,3,2,1:T(8,128)} %copy.85, f32[16,4,128,1,128]{4,0,3,2,1:T(8,128)} %copy.84, f32[16,128,128]{2,0,1:T(8,128)} %get-tuple-element.44, f32[16,128,128]{2,0,1:T(8,128)S(1)} %get-tuple-element.43), kind=kLoop, calls=%fused_computation.9 | loop fusion | flops 8388608 | bytes 14680064 | tf_op jit(solution)/shard_map/convert.8
  163.5 0.4 pad_maximum_fusion
  163.9 6.6 %copy.67 = bf16[16,4,128,2,128]{4,3,2,1,0:T(2,128)(2,1)} copy(bf16[16,4,128,2,128]{4,0,3,2,1:T(8,128)(2,1)S(1)} %pad_maximum_fusion) | data formatting | bytes 8388608 | tf_op jit(solution)/shard_map/while/body/eval_jaxpr/stack | solution.py:55
  170.5 7.8 %convert_element_type.145 = bf16[64,32768]{1,0:T(8,128)(2,1)} reshape(bf16[16,4,128,2,128]{4,3,2,1,0:T(2,128)(2,1)} %copy.67) | data formatting | bytes 8388608 | tf_op jit(solution)/shard_map/while/body/eval_jaxpr/convert_element_type | solution.py:58
  178.3 3.7 fusion.37
  182.1 0.1 reduce_sum.19
  182.3 0.1 div.68
  182.4 0.1 copy.70
  182.5 2.4 fusion.6
  184.9 1.5 subtract_convert_fusion
  186.4 0.4 pad_maximum_fusion.1
  186.8 6.6 %copy.72 = bf16[16,4,128,2,128]{4,3,2,1,0:T(2,128)(2,1)} copy(bf16[16,4,128,2,128]{4,0,3,2,1:T(8,128)(2,1)S(1)} %pad_maximum_fusion.1) | data formatting | bytes 8388608 | tf_op jit(solution)/shard_map/while/body/eval_jaxpr/stack | solution.py:68
  193.4 7.8 %convert_element_type.150 = bf16[64,32768]{1,0:T(8,128)(2,1)} reshape(bf16[16,4,128,2,128]{4,3,2,1,0:T(2,128)(2,1)} %copy.72) | data formatting | bytes 8388608 | tf_op jit(solution)/shard_map/while/body/eval_jaxpr/convert_element_type | solution.py:71
  201.2 3.4 fusion
  204.6 8.1 %copy.74 = f32[64,128,256]{2,1,0:T(8,128)} copy(f32[64,128,256]{2,0,1:T(8,128)S(1)} %fusion) | data formatting | bytes 16777216 | tf_op jit(solution)/shard_map/dot_general | solution.py:121
  212.8 149.2 %reduce-scatter.2.cloned.1.call-done = f32[1,128,256]{2,1,0:T(8,128)} async-done(((f32[64,128,256]{2,1,0:T(8,128)}), f32[1,128,256]{2,1,0:T(8,128)}) %reduce-scatter.2.cloned.1.call-update) | async-done | bytes 131088 | tf_op jit(solution)/shard_map/reduce_scatter | solution.py:124
  362.0 0.9 convert_element_type.151
  362.9 0.3 fusion.3
  363.3 0.3 copy.76
  363.6 25.1 %all_to_all.10 = bf16[64,16,256]{2,1,0:T(8,128)(2,1)S(1)} all-to-all(bf16[64,16,256]{2,1,0:T(8,128)(2,1)S(1)} %copy.76), channel_id=1, replica_groups=mesh['slab'=64,'img'=4] {'slab'}, dimensions={0} | all-to-all | bytes 1048576 | tf_op jit(solution)/shard_map/all_to_all | solution.py:131
  388.7 1.2 convolution_bitcast_fusion
  390.1 0.7 broadcast_divide_fusion
  390.8 44.8 %all-reduce.2.cloned.1.call-done = f32[512,256]{0,1:T(8,128)} async-done(((f32[512,256]{0,1:T(8,128)}), f32[512,256]{0,1:T(8,128)}) %all-reduce.2.cloned.1.call-update) | async-done | bytes 524304 | tf_op jit(solution)/shard_map/psum | solution.py:133
  435.6 1.1 broadcast_multiply_fusion
  436.7 1.0 copy.78
  (34 shorter events, 1.1 us)
Async XLA Ops:
  7.2 1.2 copy-start
  7.2 44.3 %copy-start.4 = (s32[1,16,4]{1,2,0:T(4,128)S(1)}, s32[1,16,4]{1,2,0:T(4,128)}, u32[]{:S(2)}) copy-start(s32[1,16,4]{1,2,0:T(4,128)} %param.11) | copy-start | bytes 772
  10.8 38.8 %all-to-all-start = ((f32[64,16,256]{2,1,0:T(8,128)}), f32[64,16,256]{2,1,0:T(8,128)S(1)}, u32[]{:S(2)}, u32[]{:S(2)}) async-start(f32[64,16,256]{2,1,0:T(8,128)} %fusion.10), calls=%async_computation | async-start | bytes 2097152 | tf_op jit(solution)/shard_map/all_to_all | solution.py:88
  22.9 104.9 %all-gather.2.cloned.1.call-start = ((), (), s32[]{:S(2)}) async-start(), calls=%async_computation.3 | async-start | bytes 4259840 | tf_op jit(solution)/shard_map/all_gather | solution.py:100
  51.3 310.7 %reduce-scatter.2.cloned.1.call-start = ((), (), s32[]{:S(2)}) async-start(), calls=%async_computation.4 | async-start | bytes 8519680 | tf_op jit(solution)/shard_map/reduce_scatter | solution.py:124
  53.9 11.1 %copy-start.5 = (f32[1,16]{1,0:T(1,128)S(1)}, f32[1,16]{1,0:T(1,128)}, u32[]{:S(2)}) copy-start(f32[1,16]{1,0:T(1,128)} %param.10) | copy-start | bytes 196
  59.5 0.8 copy-start.2
  178.3 4.3 copy-start.3
  182.5 2.4 copy-start.1
  212.7 222.9 %all-reduce.2.cloned.1.call-start = ((), (), s32[]{:S(2)}) async-start(), calls=%async_computation.5 | async-start | bytes 1048576 | tf_op jit(solution)/shard_map/psum | solution.py:133
Sparse Core Ops, SparseCore 0:
  51.4 76.4 all-gather.1
  212.9 149.1 reduce-scatter.1
  390.1 45.5 all-reduce.1

commit v2 on v1

--- a/solution.py
+++ b/solution.py
@@ -121,7 +121,9 @@
     contrib = lax.dot_general(
         member, all_slices, (((0,), (0,)), ((), ())), preferred_element_type=jnp.float32
     ).reshape(orient_count, fourier, 2 * fourier)
-    back_own = lax.psum_scatter(contrib, "slab", scatter_dimension=0, tiled=True).astype(jnp.bfloat16)
+    back_own = lax.psum_scatter(
+        contrib.astype(jnp.bfloat16), "slab", scatter_dimension=0, tiled=True
+    )
     back_own = back_own.reshape(ori_dev, block_count, block_rows, 2 * fourier)
     chosen_back = (owned_idx[:, :, None] == levels).astype(jnp.bfloat16)
     outgoing = jnp.einsum(

time: 445 us -> 434 us (0.975)
  waiting for transfers between devices: 277 us -> 269 us
    dot_general x1 -> x0, local copies, waits for them, and re-layouts: 8.08 us -> none  [on_device(): lax.dot_general(member, all_slices, (((0,), (0,)), ((), ())), preferred_e...]
    reduce_scatter x1, waiting for transfers between devices: 149 us -> 142 us  [on_device(): lax.psum_scatter(contrib.astype(jnp.bfloat16), 'slab', scatter_dimension=...]
where the time goes in v2:
time: 434 us; the launch traced here: 433 us
  waiting for transfers between devices  269 us (62%)
  local copies, waits for them, and re-layouts  77.2 us (18%)
  blocking collectives  25.1 us (6%)
  other arithmetic  19.8 us (5%)
  matrix products  15.4 us (4%)
  between operations  14 us (3%)
  starting transfers between devices  12.5 us (3%)
    reduce_scatter x1, waiting for transfers between devices, on_device(): lax.psum_scatter(contrib.astype(jnp.bfloat16), 'slab', scatter_dimension=...  142 us
    all_gather x1, waiting for transfers between devices, on_device(): lax.all_gather(summed.astype(jnp.bfloat16), 'slab', axis=0, tiled=True)  56.5 us
    psum x1, waiting for transfers between devices, on_device(): summed_cols = lax.psum(column, 'img')  44.9 us
    all_to_all x1, waiting for transfers between devices, on_device(): lax.all_to_all(partial_value.reshape(slab_count, ori_dev * block_rows, 2...  25.9 us
    all_to_all x1, blocking collectives, on_device(): lax.all_to_all(outgoing, 'slab', split_axis=0, concat_axis=0, tiled=True)  25.1 us
    unnamed x16, local copies, waits for them, and re-layouts  14.1 us
    all_to_all x1, starting transfers between devices, on_device(): lax.all_to_all(partial_value.reshape(slab_count, ori_dev * block_rows, 2...  12.2 us
    another operation x3, other arithmetic  11.8 us
  transfers between devices with their start and end apart: 4, of which 4 were waited for; matrix products, arithmetic and copies ran while one was open for 5% of the time, Pallas kernels for 0%

profile of v2, /device:TPU:6, one launch (start us, length us, event | category | flops | bytes accessed | tf_op | source)
XLA Modules:
  0.0 433.0 jit_solution(10198420405480891421)
XLA Ops:
  7.2 1.2 copy-done
  8.4 2.4 fusion.13
  10.8 12.2 %all-to-all-start = ((f32[64,16,256]{2,1,0:T(8,128)}), f32[64,16,256]{2,1,0:T(8,128)S(1)}, u32[]{:S(2)}, u32[]{:S(2)}) async-start(f32[64,16,256]{2,1,0:T(8,128)} %fusion.13), calls=%async_computation | async-start | bytes 2097152 | tf_op jit(solution)/shard_map/all_to_all | solution.py:88
  23.0 0.7 dynamic-slice_bitcast_fusion
  23.7 25.9 %all-to-all-done = f32[64,16,256]{2,1,0:T(8,128)S(1)} async-done(((f32[64,16,256]{2,1,0:T(8,128)}), f32[64,16,256]{2,1,0:T(8,128)S(1)}, u32[]{:S(2)}, u32[]{:S(2)}) %all-to-all-start) | async-done | bytes 1048608 | tf_op jit(solution)/shard_map/all_to_all | solution.py:88
  49.6 1.0 convolution_convert_fusion.1
  50.6 0.6 copy.62
  51.3 0.2 reduce-scatter.2.cloned.1.call-start
  51.8 2.1 reshape.430
  54.0 0.1 copy.68
  54.1 5.4 %fusion.17 = (bf16[128,1,128,16]{2,3,1,0:T(8,128)(2,1)S(1)}, bf16[128,1,128,16]{2,3,1,0:T(8,128)(2,1)}, bf16[128,1,128,16]{2,3,1,0:T(8,128)(2,1)S(1)}) fusion(f32[128,16]{0,1:T(8,128)S(1)} %get-tuple-element.51, f32[128,16]{1,0:T(8,128)S(1)} %copy.68), kind=kLoop, calls=%fused_computation.33 | loop fusion | flops 1572864 | bytes 1589248 | tf_op jit(solution)/shard_map/convert.7
  59.5 0.8 copy-done.2
  60.3 0.1 pad_maximum_fusion.3
  60.4 1.9 copy.69
  62.3 2.6 convert_element_type.148
  65.1 3.9 add_negate_fusion
  69.0 1.2 copy_multiply_fusion
  70.2 1.1 slice_bitcast_fusion.1
  71.4 56.5 %all-gather.2.cloned.1.call-done = bf16[64,128,256]{2,1,0:T(8,128)(2,1)} async-done(((bf16[1,128,256]{2,1,0:T(8,128)(2,1)}), bf16[64,128,256]{2,1,0:T(8,128)(2,1)}) %all-gather.2.cloned.1.call-update) | async-done | bytes 4194320 | tf_op jit(solution)/shard_map/all_gather | solution.py:100
  127.9 5.0 %gather_fusion = bf16[64,128,256]{2,1,0:T(8,128)(2,1)} fusion(bf16[64,128,256]{2,1,0:T(8,128)(2,1)} %all-gather.2.cloned.1.call-done, s32[1024]{0:T(1024)S(1)} %pad_clamp_fusion), kind=kCustom, calls=%fused_computation | custom fusion | bytes 8388864 | tf_op jit(solution)/shard_map/while/body/eval_jaxpr/gather | solution.py:52
  132.8 7.0 %copy.64 = f32[64,128,256]{1,2,0:T(8,128)} copy(bf16[64,128,256]{2,1,0:T(8,128)(2,1)} %gather_fusion) | data formatting | bytes 12582912 | tf_op jit(solution)/shard_map/while/body/eval_jaxpr/convert_element_type | solution.py:52
  139.9 7.8 %fusion.39 = (f32[16,4,128,1,128]{2,4,3,1,0:T(8,128)}, f32[16,4,128,1,128]{2,4,3,1,0:T(8,128)}) fusion(f32[16,4,128,2,128]{2,4,3,1,0:T(8,128)} %bitcast.64), kind=kLoop, calls=%fused_computation.74 | loop fusion | bytes 16777216 | tf_op jit(solution)/shard_map/while/body/eval_jaxpr/slice | solution.py:53
  147.7 5.5 %copy.84 = f32[16,4,128,1,128]{4,0,3,2,1:T(8,128)} copy(f32[16,4,128,1,128]{2,4,3,1,0:T(8,128)} %get-tuple-element.41) | data formatting | bytes 8388608
  153.1 5.5 %copy.85 = f32[16,4,128,1,128]{4,0,3,2,1:T(8,128)} copy(f32[16,4,128,1,128]{2,4,3,1,0:T(8,128)} %get-tuple-element.42) | data formatting | bytes 8388608
  158.6 4.9 %add_convert_fusion.1 = (bf16[16,4,128,1,128]{4,0,3,2,1:T(8,128)(2,1)S(1)}, bf16[16,4,128,1,128]{4,0,3,2,1:T(8,128)(2,1)S(1)}) fusion(f32[16,4,128,1,128]{4,0,3,2,1:T(8,128)} %copy.85, f32[16,4,128,1,128]{4,0,3,2,1:T(8,128)} %copy.84, f32[16,128,128]{2,0,1:T(8,128)} %get-tuple-element.44, f32[16,128,128]{2,0,1:T(8,128)S(1)} %get-tuple-element.43), kind=kLoop, calls=%fused_computation.9 | loop fusion | flops 8388608 | bytes 14680064 | tf_op jit(solution)/shard_map/convert.8
  163.5 0.4 pad_maximum_fusion
  163.9 6.6 %copy.67 = bf16[16,4,128,2,128]{4,3,2,1,0:T(2,128)(2,1)} copy(bf16[16,4,128,2,128]{4,0,3,2,1:T(8,128)(2,1)S(1)} %pad_maximum_fusion) | data formatting | bytes 8388608 | tf_op jit(solution)/shard_map/while/body/eval_jaxpr/stack | solution.py:55
  170.5 7.8 %convert_element_type.145 = bf16[64,32768]{1,0:T(8,128)(2,1)} reshape(bf16[16,4,128,2,128]{4,3,2,1,0:T(2,128)(2,1)} %copy.67) | data formatting | bytes 8388608 | tf_op jit(solution)/shard_map/while/body/eval_jaxpr/convert_element_type | solution.py:58
  178.3 3.7 fusion.40
  182.1 0.1 reduce_sum.19
  182.3 0.1 div.68
  182.4 0.1 copy.70
  182.5 2.4 fusion.9
  184.9 1.5 subtract_convert_fusion
  186.4 0.4 pad_maximum_fusion.1
  186.8 6.6 %copy.72 = bf16[16,4,128,2,128]{4,3,2,1,0:T(2,128)(2,1)} copy(bf16[16,4,128,2,128]{4,0,3,2,1:T(8,128)(2,1)S(1)} %pad_maximum_fusion.1) | data formatting | bytes 8388608 | tf_op jit(solution)/shard_map/while/body/eval_jaxpr/stack | solution.py:68
  193.4 7.8 %convert_element_type.150 = bf16[64,32768]{1,0:T(8,128)(2,1)} reshape(bf16[16,4,128,2,128]{4,3,2,1,0:T(2,128)(2,1)} %copy.72) | data formatting | bytes 8388608 | tf_op jit(solution)/shard_map/while/body/eval_jaxpr/convert_element_type | solution.py:71
  201.2 3.4 fusion.3
  204.6 4.4 %copy.74 = bf16[64,128,256]{2,1,0:T(8,128)(2,1)} copy(bf16[64,128,256]{2,0,1:T(8,128)(2,1)S(1)} %fusion.3) | data formatting | bytes 8388608 | tf_op jit(solution)/shard_map/convert_element_type | solution.py:125
  209.1 141.8 %reduce-scatter.2.cloned.1.call-done = bf16[1,128,256]{2,1,0:T(8,128)(2,1)} async-done(((bf16[64,128,256]{2,1,0:T(8,128)(2,1)}), bf16[1,128,256]{2,1,0:T(8,128)(2,1)}) %reduce-scatter.2.cloned.1.call-update) | async-done | bytes 65552 | tf_op jit(solution)/shard_map/reduce_scatter | solution.py:124
  350.9 1.2 fusion.6
  352.1 0.3 copy.76
  352.4 25.1 %all_to_all.10 = bf16[64,16,256]{2,1,0:T(8,128)(2,1)S(1)} all-to-all(bf16[64,16,256]{2,1,0:T(8,128)(2,1)S(1)} %copy.76), channel_id=1, replica_groups=mesh['slab'=64,'img'=4] {'slab'}, dimensions={0} | all-to-all | bytes 1048576 | tf_op jit(solution)/shard_map/all_to_all | solution.py:133
  377.5 1.2 convolution_bitcast_fusion
  378.9 0.7 broadcast_divide_fusion
  379.6 44.9 %all-reduce.2.cloned.1.call-done = f32[512,256]{0,1:T(8,128)} async-done(((f32[512,256]{0,1:T(8,128)}), f32[512,256]{0,1:T(8,128)}) %all-reduce.2.cloned.1.call-update) | async-done | bytes 524304 | tf_op jit(solution)/shard_map/psum | solution.py:135
  424.4 1.1 broadcast_multiply_fusion
  425.5 1.0 copy.78
  (33 shorter events, 1.0 us)
Async XLA Ops:
  7.2 1.2 copy-start
  7.2 44.3 %copy-start.4 = (s32[1,16,4]{1,2,0:T(4,128)S(1)}, s32[1,16,4]{1,2,0:T(4,128)}, u32[]{:S(2)}) copy-start(s32[1,16,4]{1,2,0:T(4,128)} %param.11) | copy-start | bytes 772
  10.8 38.8 %all-to-all-start = ((f32[64,16,256]{2,1,0:T(8,128)}), f32[64,16,256]{2,1,0:T(8,128)S(1)}, u32[]{:S(2)}, u32[]{:S(2)}) async-start(f32[64,16,256]{2,1,0:T(8,128)} %fusion.13), calls=%async_computation | async-start | bytes 2097152 | tf_op jit(solution)/shard_map/all_to_all | solution.py:88
  22.9 104.9 %all-gather.2.cloned.1.call-start = ((), (), s32[]{:S(2)}) async-start(), calls=%async_computation.3 | async-start | bytes 4259840 | tf_op jit(solution)/shard_map/all_gather | solution.py:100
  51.3 299.6 %reduce-scatter.2.cloned.1.call-start = ((), (), s32[]{:S(2)}) async-start(), calls=%async_computation.4 | async-start | bytes 4259840 | tf_op jit(solution)/shard_map/reduce_scatter | solution.py:124
  53.9 11.1 %copy-start.5 = (f32[1,16]{1,0:T(1,128)S(1)}, f32[1,16]{1,0:T(1,128)}, u32[]{:S(2)}) copy-start(f32[1,16]{1,0:T(1,128)} %param.10) | copy-start | bytes 196
  59.5 0.8 copy-start.2
  178.3 4.3 copy-start.3
  182.5 2.4 copy-start.1
  209.0 215.4 %all-reduce.2.cloned.1.call-start = ((), (), s32[]{:S(2)}) async-start(), calls=%async_computation.5 | async-start | bytes 1048576 | tf_op jit(solution)/shard_map/psum | solution.py:135
Sparse Core Ops, SparseCore 0:
  51.4 76.4 all-gather.1
  209.2 141.6 reduce-scatter.1
  378.9 45.5 all-reduce.1

commit v3 on v1

--- a/solution.py
+++ b/solution.py
@@ -121,7 +121,10 @@
     contrib = lax.dot_general(
         member, all_slices, (((0,), (0,)), ((), ())), preferred_element_type=jnp.float32
     ).reshape(orient_count, fourier, 2 * fourier)
-    back_own = lax.psum_scatter(contrib, "slab", scatter_dimension=0, tiled=True).astype(jnp.bfloat16)
+    gathered = lax.all_to_all(
+        contrib.astype(jnp.bfloat16), "slab", split_axis=0, concat_axis=0, tiled=True
+    ).reshape(slab_count, ori_dev, fourier, 2 * fourier)
+    back_own = jnp.sum(gathered.astype(jnp.float32), axis=0).astype(jnp.bfloat16)
     back_own = back_own.reshape(ori_dev, block_count, block_rows, 2 * fourier)
     chosen_back = (owned_idx[:, :, None] == levels).astype(jnp.bfloat16)
     outgoing = jnp.einsum(

time: 445 us -> 394 us (0.89)
  waiting for transfers between devices: 277 us -> 127 us
  blocking collectives: 25.1 us -> 127 us
  local copies, waits for them, and re-layouts: 80.9 us -> 75.3 us
    reduce_scatter x1 -> x0, waiting for transfers between devices: 149 us -> none  [on_device(): lax.psum_scatter(contrib, 'slab', scatter_dimension=0, tiled=True)]
    all_to_all x0 -> x1, blocking collectives: none -> 102 us  [on_device(): lax.all_to_all(contrib.astype(jnp.bfloat16), 'slab', split_axis=0, concat...]
    dot_general x1 -> x0, local copies, waits for them, and re-layouts: 8.08 us -> none  [on_device(): lax.dot_general(member, all_slices, (((0,), (0,)), ((), ())), preferred_e...]
  transfers between devices with their start and end apart: 4 -> 3, of which waited for: 4 -> 3; matrix products, arithmetic and copies ran while one was open for 5% -> 5% of each run, Pallas kernels for 0% -> 0%
where the time goes in v3:
time: 394 us; the launch traced here: 393 us
  waiting for transfers between devices  127 us (32%)
  blocking collectives  127 us (32%)
  local copies, waits for them, and re-layouts  75.3 us (19%)
  other arithmetic  22.6 us (6%)
  matrix products  14.5 us (4%)
  between operations  14.3 us (4%)
  starting transfers between devices  12.4 us (3%)
    all_to_all x1, blocking collectives, on_device(): lax.all_to_all(contrib.astype(jnp.bfloat16), 'slab', split_axis=0, concat...  102 us
    all_gather x1, waiting for transfers between devices, on_device(): lax.all_gather(summed.astype(jnp.bfloat16), 'slab', axis=0, tiled=True)  56.5 us
    psum x1, waiting for transfers between devices, on_device(): summed_cols = lax.psum(column, 'img')  44.9 us
    all_to_all x1, waiting for transfers between devices, on_device(): lax.all_to_all(partial_value.reshape(slab_count, ori_dev * block_rows, 2...  25.9 us
    all_to_all x1, blocking collectives, on_device(): lax.all_to_all(outgoing, 'slab', split_axis=0, concat_axis=0, tiled=True)  24.6 us
    unnamed x16, local copies, waits for them, and re-layouts  14.1 us
    all_to_all x1, starting transfers between devices, on_device(): lax.all_to_all(partial_value.reshape(slab_count, ori_dev * block_rows, 2...  12.2 us
    another operation x3, other arithmetic  11.8 us
  transfers between devices with their start and end apart: 3, of which 3 were waited for; matrix products, arithmetic and copies ran while one was open for 5% of the time, Pallas kernels for 0%

profile of v3, /device:TPU:6, one launch (start us, length us, event | category | flops | bytes accessed | tf_op | source)
XLA Modules:
  0.0 393.0 jit_solution(16889548143787505688)
XLA Ops:
  7.2 1.2 copy-done
  8.4 2.4 fusion.13
  10.8 12.2 %all-to-all-start = ((f32[64,16,256]{2,1,0:T(8,128)}), f32[64,16,256]{2,1,0:T(8,128)S(1)}, u32[]{:S(2)}, u32[]{:S(2)}) async-start(f32[64,16,256]{2,1,0:T(8,128)} %fusion.13), calls=%async_computation | async-start | bytes 2097152 | tf_op jit(solution)/shard_map/all_to_all | solution.py:88
  23.0 0.7 dynamic-slice_bitcast_fusion
  23.7 25.9 %all-to-all-done = f32[64,16,256]{2,1,0:T(8,128)S(1)} async-done(((f32[64,16,256]{2,1,0:T(8,128)}), f32[64,16,256]{2,1,0:T(8,128)S(1)}, u32[]{:S(2)}, u32[]{:S(2)}) %all-to-all-start) | async-done | bytes 1048608 | tf_op jit(solution)/shard_map/all_to_all | solution.py:88
  49.6 1.0 convolution_convert_fusion.1
  50.6 0.6 copy.61
  51.3 0.2 all-reduce.2.cloned.1.call-start
  51.8 2.1 reshape.433
  54.0 0.1 copy.67
  54.1 5.4 %fusion.17 = (bf16[128,1,128,16]{2,3,1,0:T(8,128)(2,1)S(1)}, bf16[128,1,128,16]{2,3,1,0:T(8,128)(2,1)}, bf16[128,1,128,16]{2,3,1,0:T(8,128)(2,1)S(1)}) fusion(f32[128,16]{0,1:T(8,128)S(1)} %get-tuple-element.51, f32[128,16]{1,0:T(8,128)S(1)} %copy.67), kind=kLoop, calls=%fused_computation.33 | loop fusion | flops 1572864 | bytes 1589248 | tf_op jit(solution)/shard_map/convert.8
  59.4 0.8 copy-done.2
  60.3 1.9 copy.68
  62.3 2.6 convert_element_type.150
  65.1 3.9 add_negate_fusion
  69.0 1.2 copy_multiply_fusion
  70.2 1.1 slice_bitcast_fusion.1
  71.3 56.5 %all-gather.2.cloned.1.call-done = bf16[64,128,256]{2,1,0:T(8,128)(2,1)} async-done(((bf16[1,128,256]{2,1,0:T(8,128)(2,1)}), bf16[64,128,256]{2,1,0:T(8,128)(2,1)}) %all-gather.2.cloned.1.call-update) | async-done | bytes 4194320 | tf_op jit(solution)/shard_map/all_gather | solution.py:100
  127.9 5.0 %gather_fusion = bf16[64,128,256]{2,1,0:T(8,128)(2,1)} fusion(bf16[64,128,256]{2,1,0:T(8,128)(2,1)} %all-gather.2.cloned.1.call-done, s32[1024]{0:T(1024)S(1)} %pad_clamp_fusion), kind=kCustom, calls=%fused_computation | custom fusion | bytes 8388864 | tf_op jit(solution)/shard_map/while/body/eval_jaxpr/gather | solution.py:52
  132.8 7.0 %copy.63 = f32[64,128,256]{1,2,0:T(8,128)} copy(bf16[64,128,256]{2,1,0:T(8,128)(2,1)} %gather_fusion) | data formatting | bytes 12582912 | tf_op jit(solution)/shard_map/while/body/eval_jaxpr/convert_element_type | solution.py:52
  139.8 7.8 %fusion.39 = (f32[16,4,128,1,128]{2,4,3,1,0:T(8,128)}, f32[16,4,128,1,128]{2,4,3,1,0:T(8,128)}) fusion(f32[16,4,128,2,128]{2,4,3,1,0:T(8,128)} %bitcast.64), kind=kLoop, calls=%fused_computation.74 | loop fusion | bytes 16777216 | tf_op jit(solution)/shard_map/while/body/eval_jaxpr/slice | solution.py:53
  147.6 5.5 %copy.83 = f32[16,4,128,1,128]{4,0,3,2,1:T(8,128)} copy(f32[16,4,128,1,128]{2,4,3,1,0:T(8,128)} %get-tuple-element.41) | data formatting | bytes 8388608
  153.1 5.5 %copy.84 = f32[16,4,128,1,128]{4,0,3,2,1:T(8,128)} copy(f32[16,4,128,1,128]{2,4,3,1,0:T(8,128)} %get-tuple-element.42) | data formatting | bytes 8388608
  158.6 4.9 %add_convert_fusion.1 = (bf16[16,4,128,1,128]{4,0,3,2,1:T(8,128)(2,1)S(1)}, bf16[16,4,128,1,128]{4,0,3,2,1:T(8,128)(2,1)S(1)}) fusion(f32[16,4,128,1,128]{4,0,3,2,1:T(8,128)} %copy.84, f32[16,4,128,1,128]{4,0,3,2,1:T(8,128)} %copy.83, f32[16,128,128]{2,0,1:T(8,128)} %get-tuple-element.44, f32[16,128,128]{2,0,1:T(8,128)S(1)} %get-tuple-element.43), kind=kLoop, calls=%fused_computation.9 | loop fusion | flops 8388608 | bytes 14680064 | tf_op jit(solution)/shard_map/convert.9
  163.5 0.4 pad_maximum_fusion
  163.9 6.6 %copy.66 = bf16[16,4,128,2,128]{4,3,2,1,0:T(2,128)(2,1)} copy(bf16[16,4,128,2,128]{4,0,3,2,1:T(8,128)(2,1)S(1)} %pad_maximum_fusion) | data formatting | bytes 8388608 | tf_op jit(solution)/shard_map/while/body/eval_jaxpr/stack | solution.py:55
  170.4 7.8 %convert_element_type.147 = bf16[64,32768]{1,0:T(8,128)(2,1)} reshape(bf16[16,4,128,2,128]{4,3,2,1,0:T(2,128)(2,1)} %copy.66) | data formatting | bytes 8388608 | tf_op jit(solution)/shard_map/while/body/eval_jaxpr/convert_element_type | solution.py:58
  178.2 3.7 fusion.40
  182.1 0.1 reduce_sum.31
  182.3 0.1 div.68
  182.4 0.1 copy.69
  182.5 2.3 fusion.9
  184.9 1.5 subtract_convert_fusion
  186.4 0.4 pad_maximum_fusion.1
  186.8 6.6 %copy.71 = bf16[16,4,128,2,128]{4,3,2,1,0:T(2,128)(2,1)} copy(bf16[16,4,128,2,128]{4,0,3,2,1:T(8,128)(2,1)S(1)} %pad_maximum_fusion.1) | data formatting | bytes 8388608 | tf_op jit(solution)/shard_map/while/body/eval_jaxpr/stack | solution.py:68
  193.3 7.9 %convert_element_type.152 = bf16[64,32768]{1,0:T(8,128)(2,1)} reshape(bf16[16,4,128,2,128]{4,3,2,1,0:T(2,128)(2,1)} %copy.71) | data formatting | bytes 8388608 | tf_op jit(solution)/shard_map/while/body/eval_jaxpr/convert_element_type | solution.py:71
  201.2 3.4 fusion.3
  204.6 2.4 copy.73
  207.0 101.9 %all_to_all.15 = bf16[64,128,256]{2,1,0:T(8,128)(2,1)} all-to-all(bf16[64,128,256]{2,1,0:T(8,128)(2,1)S(1)} %copy.73), channel_id=1, replica_groups=mesh['slab'=64,'img'=4] {'slab'}, dimensions={0} | all-to-all | bytes 8388608 | tf_op jit(solution)/shard_map/all_to_all | solution.py:124
  309.0 2.8 reduce_sum.32
  311.8 0.3 fusion.6
  312.1 0.3 copy.75
  312.4 24.6 %all_to_all.16 = bf16[64,16,256]{2,1,0:T(8,128)(2,1)S(1)} all-to-all(bf16[64,16,256]{2,1,0:T(8,128)(2,1)S(1)} %copy.75), channel_id=1, replica_groups=mesh['slab'=64,'img'=4] {'slab'}, dimensions={0} | all-to-all | bytes 1048576 | tf_op jit(solution)/shard_map/all_to_all | solution.py:134
  337.1 1.2 convolution_bitcast_fusion
  338.5 0.7 broadcast_divide_fusion
  339.2 44.9 %all-reduce.2.cloned.1.call-done = f32[512,256]{0,1:T(8,128)} async-done(((f32[512,256]{0,1:T(8,128)}), f32[512,256]{0,1:T(8,128)}) %all-reduce.2.cloned.1.call-update) | async-done | bytes 524304 | tf_op jit(solution)/shard_map/psum | solution.py:136
  384.1 1.1 broadcast_multiply_fusion
  385.2 1.0 copy.77
  (32 shorter events, 1.0 us)
Async XLA Ops:
  7.2 1.2 copy-start
  7.2 44.3 %copy-start.4 = (s32[1,16,4]{1,2,0:T(4,128)S(1)}, s32[1,16,4]{1,2,0:T(4,128)}, u32[]{:S(2)}) copy-start(s32[1,16,4]{1,2,0:T(4,128)} %param.11) | copy-start | bytes 772
  10.8 38.8 %all-to-all-start = ((f32[64,16,256]{2,1,0:T(8,128)}), f32[64,16,256]{2,1,0:T(8,128)S(1)}, u32[]{:S(2)}, u32[]{:S(2)}) async-start(f32[64,16,256]{2,1,0:T(8,128)} %fusion.13), calls=%async_computation | async-start | bytes 2097152 | tf_op jit(solution)/shard_map/all_to_all | solution.py:88
  22.9 104.9 %all-gather.2.cloned.1.call-start = ((), (), s32[]{:S(2)}) async-start(), calls=%async_computation.3 | async-start | bytes 4259840 | tf_op jit(solution)/shard_map/all_gather | solution.py:100
  51.3 332.8 %all-reduce.2.cloned.1.call-start = ((), (), s32[]{:S(2)}) async-start(), calls=%async_computation.4 | async-start | bytes 1048576 | tf_op jit(solution)/shard_map/psum | solution.py:136
  53.9 11.1 %copy-start.5 = (f32[1,16]{1,0:T(1,128)S(1)}, f32[1,16]{1,0:T(1,128)}, u32[]{:S(2)}) copy-start(f32[1,16]{1,0:T(1,128)} %param.10) | copy-start | bytes 196
  59.4 0.8 copy-start.2
  178.2 4.3 %copy-start.3 = (bf16[128,1,128,16]{2,3,1,0:T(8,128)(2,1)S(1)}, bf16[128,1,128,16]{2,3,1,0:T(8,128)(2,1)}, u32[]{:S(2)}) copy-start(bf16[128,1,128,16]{2,3,1,0:T(8,128)(2,1)} %copy-done.2) | copy-start | bytes 1572868
  182.5 2.4 copy-start.1
Sparse Core Ops, SparseCore 0:
  51.4 76.4 all-gather.1
  338.5 45.5 all-reduce.1

commit v4 on v1

--- a/solution.py
+++ b/solution.py
@@ -3,6 +3,8 @@
 import jax
 import jax.numpy as jnp
 from jax import lax
+from jax.experimental import pallas as pl
+from jax.experimental.pallas import tpu as pltpu
 from jax.sharding import PartitionSpec as P
 
 BOX = 256
@@ -70,6 +72,74 @@
     )
     backed = backed.astype(jnp.bfloat16).reshape(count * picks, 2 * fourier * fourier)
     return (weights, backed)
+
+
+def _a2a_kernel(x_ref, o_ref, send_sems, recv_sems, local_sem):
+    count = x_ref.shape[0]
+    me = lax.axis_index("slab")
+    grp = lax.axis_index("img")
+    mesh_ids = pl.DeviceIdType.MESH
+    barrier = pltpu.get_barrier_semaphore()
+
+    def greet(i, carry):
+        peer = lax.rem(me + 1 + i, count)
+        pl.semaphore_signal(barrier, inc=1, device_id=(peer, grp), device_id_type=mesh_ids)
+        return carry
+
+    lax.fori_loop(0, count - 1, greet, 0)
+    pl.semaphore_wait(barrier, count - 1)
+    local = pltpu.make_async_copy(x_ref.at[me], o_ref.at[me], local_sem)
+    local.start()
+
+    def outgoing(peer):
+        return pltpu.make_async_remote_copy(
+            src_ref=x_ref.at[peer],
+            dst_ref=o_ref.at[me],
+            send_sem=send_sems.at[peer],
+            recv_sem=recv_sems.at[me],
+            device_id=(peer, grp),
+            device_id_type=mesh_ids,
+        )
+
+    def incoming(src):
+        return pltpu.make_async_remote_copy(
+            src_ref=x_ref.at[src],
+            dst_ref=o_ref.at[src],
+            send_sem=send_sems.at[src],
+            recv_sem=recv_sems.at[src],
+            device_id=(src, grp),
+            device_id_type=mesh_ids,
+        )
+
+    def send(i, carry):
+        outgoing(lax.rem(me + 1 + i, count)).start()
+        return carry
+
+    lax.fori_loop(0, count - 1, send, 0)
+
+    def finish(i, carry):
+        outgoing(lax.rem(me + 1 + i, count)).wait_send()
+        incoming(lax.rem(me + count - 1 - i, count)).wait_recv()
+        return carry
+
+    lax.fori_loop(0, count - 1, finish, 0)
+    local.wait()
+
+
+def slab_all_to_all(x, cid):
+    count = x.shape[0]
+    return pl.pallas_call(
+        _a2a_kernel,
+        out_shape=jax.ShapeDtypeStruct(x.shape, x.dtype),
+        in_specs=[pl.BlockSpec(memory_space=pl.ANY)],
+        out_specs=pl.BlockSpec(memory_space=pl.ANY),
+        scratch_shapes=[
+            pltpu.SemaphoreType.DMA((count,)),
+            pltpu.SemaphoreType.DMA((count,)),
+            pltpu.SemaphoreType.DMA,
+        ],
+        compiler_params=pltpu.CompilerParams(collective_id=cid, has_side_effects=True),
+    )(x)
 
 
 def on_device(volume, interp, block_index, images, defocus, orient):
@@ -121,7 +191,8 @@
     contrib = lax.dot_general(
         member, all_slices, (((0,), (0,)), ((), ())), preferred_element_type=jnp.float32
     ).reshape(orient_count, fourier, 2 * fourier)
-    back_own = lax.psum_scatter(contrib, "slab", scatter_dimension=0, tiled=True).astype(jnp.bfloat16)
+    gathered = slab_all_to_all(contrib.astype(jnp.bfloat16), 0).reshape(slab_count, ori_dev, fourier, 2 * fourier)
+    back_own = jnp.sum(gathered.astype(jnp.float32), axis=0).astype(jnp.bfloat16)
     back_own = back_own.reshape(ori_dev, block_count, block_rows, 2 * fourier)
     chosen_back = (owned_idx[:, :, None] == levels).astype(jnp.bfloat16)
     outgoing = jnp.einsum(

time: 445 us -> 405 us (0.910)
  waiting for transfers between devices: 277 us -> 127 us
  Pallas kernels: 0 us -> 102 us
  blocking collectives: 25.1 us -> 33.3 us
    reduce_scatter x1 -> x0, waiting for transfers between devices: 149 us -> none  [on_device(): lax.psum_scatter(contrib, 'slab', scatter_dimension=0, tiled=True)]
    pallas_call x0 -> x1, Pallas kernels: none -> 102 us  [slab_all_to_all(): pl.pallas_call(_a2a_kernel, out_shape=jax.ShapeDtypeStruct(x.shape, x.dty...]
    all_to_all x1, blocking collectives: 25.1 us -> 33.3 us  [on_device(): lax.all_to_all(outgoing, 'slab', split_axis=0, concat_axis=0, tiled=True)]
  transfers between devices with their start and end apart: 4 -> 3, of which waited for: 4 -> 3; matrix products, arithmetic and copies ran while one was open for 5% -> 5% of each run, Pallas kernels for 0% -> 0%
where the time goes in v4:
time: 405 us; the launch traced here: 404 us
  waiting for transfers between devices  127 us (31%)
  Pallas kernels  102 us (25%)
  local copies, waits for them, and re-layouts  77.2 us (19%)
  blocking collectives  33.3 us (8%)
  other arithmetic  22.6 us (6%)
  matrix products  14.5 us (4%)
  between operations  14.3 us (4%)
  starting transfers between devices  12.4 us (3%)
    pallas_call x1, Pallas kernels, slab_all_to_all(): pl.pallas_call(_a2a_kernel, out_shape=jax.ShapeDtypeStruct(x.shape, x.dty...  102 us
    all_gather x1, waiting for transfers between devices, on_device(): lax.all_gather(summed.astype(jnp.bfloat16), 'slab', axis=0, tiled=True)  56.5 us
    psum x1, waiting for transfers between devices, on_device(): summed_cols = lax.psum(column, 'img')  45 us
    all_to_all x1, blocking collectives, on_device(): lax.all_to_all(outgoing, 'slab', split_axis=0, concat_axis=0, tiled=True)  33.3 us
    all_to_all x1, waiting for transfers between devices, on_device(): lax.all_to_all(partial_value.reshape(slab_count, ori_dev * block_rows, 2...  25.9 us
    unnamed x16, local copies, waits for them, and re-layouts  14.1 us
    all_to_all x1, starting transfers between devices, on_device(): lax.all_to_all(partial_value.reshape(slab_count, ori_dev * block_rows, 2...  12.2 us
    another operation x3, other arithmetic  11.8 us
  transfers between devices with their start and end apart: 3, of which 3 were waited for; matrix products, arithmetic and copies ran while one was open for 5% of the time, Pallas kernels for 0%

profile of v4, /device:TPU:6, one launch (start us, length us, event | category | flops | bytes accessed | tf_op | source)
XLA Modules:
  0.0 403.6 jit_solution(16877168443449616803)
XLA Ops:
  7.2 1.2 copy-done
  8.4 2.4 fusion.10
  10.8 12.2 %all-to-all-start = ((f32[64,16,256]{2,1,0:T(8,128)}), f32[64,16,256]{2,1,0:T(8,128)S(1)}, u32[]{:S(2)}, u32[]{:S(2)}) async-start(f32[64,16,256]{2,1,0:T(8,128)} %fusion.10), calls=%async_computation | async-start | bytes 2097152 | tf_op jit(solution)/shard_map/all_to_all | solution.py:158
  23.0 0.7 dynamic-slice_bitcast_fusion
  23.7 25.9 %all-to-all-done = f32[64,16,256]{2,1,0:T(8,128)S(1)} async-done(((f32[64,16,256]{2,1,0:T(8,128)}), f32[64,16,256]{2,1,0:T(8,128)S(1)}, u32[]{:S(2)}, u32[]{:S(2)}) %all-to-all-start) | async-done | bytes 1048608 | tf_op jit(solution)/shard_map/all_to_all | solution.py:158
  49.6 1.0 convolution_convert_fusion.1
  50.6 0.6 copy.63
  51.3 0.2 all-reduce.2.cloned.1.call-start
  51.8 2.1 reshape.433
  54.0 0.1 copy.69
  54.1 5.4 %fusion.14 = (bf16[128,1,128,16]{2,3,1,0:T(8,128)(2,1)S(1)}, bf16[128,1,128,16]{2,3,1,0:T(8,128)(2,1)}, bf16[128,1,128,16]{2,3,1,0:T(8,128)(2,1)S(1)}) fusion(f32[128,16]{0,1:T(8,128)S(1)} %get-tuple-element.51, f32[128,16]{1,0:T(8,128)S(1)} %copy.69), kind=kLoop, calls=%fused_computation.33 | loop fusion | flops 1572864 | bytes 1589248 | tf_op jit(solution)/shard_map/convert.8
  59.4 0.8 copy-done.2
  60.3 1.9 copy.70
  62.3 2.6 convert_element_type.150
  65.1 3.9 add_negate_fusion
  69.0 1.2 copy_multiply_fusion
  70.2 1.1 slice_bitcast_fusion.1
  71.3 56.5 %all-gather.2.cloned.1.call-done = bf16[64,128,256]{2,1,0:T(8,128)(2,1)} async-done(((bf16[1,128,256]{2,1,0:T(8,128)(2,1)}), bf16[64,128,256]{2,1,0:T(8,128)(2,1)}) %all-gather.2.cloned.1.call-update) | async-done | bytes 4194320 | tf_op jit(solution)/shard_map/all_gather | solution.py:170
  127.9 5.0 %gather_fusion = bf16[64,128,256]{2,1,0:T(8,128)(2,1)} fusion(bf16[64,128,256]{2,1,0:T(8,128)(2,1)} %all-gather.2.cloned.1.call-done, s32[1024]{0:T(1024)S(1)} %pad_clamp_fusion), kind=kCustom, calls=%fused_computation | custom fusion | bytes 8388864 | tf_op jit(solution)/shard_map/while/body/eval_jaxpr/gather | solution.py:54
  132.8 7.0 %copy.65 = f32[64,128,256]{1,2,0:T(8,128)} copy(bf16[64,128,256]{2,1,0:T(8,128)(2,1)} %gather_fusion) | data formatting | bytes 12582912 | tf_op jit(solution)/shard_map/while/body/eval_jaxpr/convert_element_type | solution.py:54
  139.8 7.8 %fusion.36 = (f32[16,4,128,1,128]{2,4,3,1,0:T(8,128)}, f32[16,4,128,1,128]{2,4,3,1,0:T(8,128)}) fusion(f32[16,4,128,2,128]{2,4,3,1,0:T(8,128)} %bitcast.62), kind=kLoop, calls=%fused_computation.74 | loop fusion | bytes 16777216 | tf_op jit(solution)/shard_map/while/body/eval_jaxpr/slice | solution.py:55
  147.6 5.5 %copy.85 = f32[16,4,128,1,128]{4,0,3,2,1:T(8,128)} copy(f32[16,4,128,1,128]{2,4,3,1,0:T(8,128)} %get-tuple-element.41) | data formatting | bytes 8388608
  153.1 5.5 %copy.86 = f32[16,4,128,1,128]{4,0,3,2,1:T(8,128)} copy(f32[16,4,128,1,128]{2,4,3,1,0:T(8,128)} %get-tuple-element.42) | data formatting | bytes 8388608
  158.6 4.9 %add_convert_fusion.1 = (bf16[16,4,128,1,128]{4,0,3,2,1:T(8,128)(2,1)S(1)}, bf16[16,4,128,1,128]{4,0,3,2,1:T(8,128)(2,1)S(1)}) fusion(f32[16,4,128,1,128]{4,0,3,2,1:T(8,128)} %copy.86, f32[16,4,128,1,128]{4,0,3,2,1:T(8,128)} %copy.85, f32[16,128,128]{2,0,1:T(8,128)} %get-tuple-element.44, f32[16,128,128]{2,0,1:T(8,128)S(1)} %get-tuple-element.43), kind=kLoop, calls=%fused_computation.10 | loop fusion | flops 8388608 | bytes 14680064 | tf_op jit(solution)/shard_map/convert.9
  163.5 0.4 pad_maximum_fusion
  163.9 6.6 %copy.68 = bf16[16,4,128,2,128]{4,3,2,1,0:T(2,128)(2,1)} copy(bf16[16,4,128,2,128]{4,0,3,2,1:T(8,128)(2,1)S(1)} %pad_maximum_fusion) | data formatting | bytes 8388608 | tf_op jit(solution)/shard_map/while/body/eval_jaxpr/stack | solution.py:57
  170.4 7.8 %convert_element_type.147 = bf16[64,32768]{1,0:T(8,128)(2,1)} reshape(bf16[16,4,128,2,128]{4,3,2,1,0:T(2,128)(2,1)} %copy.68) | data formatting | bytes 8388608 | tf_op jit(solution)/shard_map/while/body/eval_jaxpr/convert_element_type | solution.py:60
  178.2 3.7 fusion.37
  182.1 0.1 reduce_sum.31
  182.3 0.1 div.68
  182.4 0.1 copy.71
  182.5 2.3 fusion.6
  184.9 1.5 subtract_convert_fusion
  186.4 0.4 pad_maximum_fusion.1
  186.8 6.6 %copy.73 = bf16[16,4,128,2,128]{4,3,2,1,0:T(2,128)(2,1)} copy(bf16[16,4,128,2,128]{4,0,3,2,1:T(8,128)(2,1)S(1)} %pad_maximum_fusion.1) | data formatting | bytes 8388608 | tf_op jit(solution)/shard_map/while/body/eval_jaxpr/stack | solution.py:70
  193.3 7.9 %convert_element_type.152 = bf16[64,32768]{1,0:T(8,128)(2,1)} reshape(bf16[16,4,128,2,128]{4,3,2,1,0:T(2,128)(2,1)} %copy.73) | data formatting | bytes 8388608 | tf_op jit(solution)/shard_map/while/body/eval_jaxpr/convert_element_type | solution.py:73
  201.2 3.4 fusion
  204.6 4.4 %copy.100.x_ref = bf16[64,128,256]{2,1,0:T(8,128)(2,1)} copy(bf16[64,128,256]{2,0,1:T(8,128)(2,1)S(1)} %fusion) | data formatting | bytes 8388608 | tf_op jit(solution)/shard_map/dot_general | solution.py:191
  209.0 101.9 %shard_map.77 = bf16[64,128,256]{2,1,0:T(8,128)(2,1)} custom-call(bf16[64,128,256]{2,1,0:T(8,128)(2,1)} %copy.100.x_ref), custom_call_target="tpu_custom_call" | custom-call | tf_op jit(solution)/shard_map/pallas_call | solution.py:131
  310.9 2.8 reduce_sum.32
  313.7 0.3 fusion.3
  314.1 0.3 copy.77
  314.4 33.3 %all_to_all.10 = bf16[64,16,256]{2,1,0:T(8,128)(2,1)S(1)} all-to-all(bf16[64,16,256]{2,1,0:T(8,128)(2,1)S(1)} %copy.77), channel_id=1, replica_groups=mesh['slab'=64,'img'=4] {'slab'}, dimensions={0} | all-to-all | bytes 1048576 | tf_op jit(solution)/shard_map/all_to_all | solution.py:202
  347.6 1.2 convolution_bitcast_fusion
  349.1 0.7 broadcast_divide_fusion
  349.7 45.0 %all-reduce.2.cloned.1.call-done = f32[512,256]{0,1:T(8,128)} async-done(((f32[512,256]{0,1:T(8,128)}), f32[512,256]{0,1:T(8,128)}) %all-reduce.2.cloned.1.call-update) | async-done | bytes 524304 | tf_op jit(solution)/shard_map/psum | solution.py:204
  394.7 1.1 broadcast_multiply_fusion
  395.8 1.0 copy.79
  (32 shorter events, 1.0 us)
Async XLA Ops:
  7.2 1.2 copy-start
  7.2 44.3 %copy-start.4 = (s32[1,16,4]{1,2,0:T(4,128)S(1)}, s32[1,16,4]{1,2,0:T(4,128)}, u32[]{:S(2)}) copy-start(s32[1,16,4]{1,2,0:T(4,128)} %param.11) | copy-start | bytes 772
  10.8 38.8 %all-to-all-start = ((f32[64,16,256]{2,1,0:T(8,128)}), f32[64,16,256]{2,1,0:T(8,128)S(1)}, u32[]{:S(2)}, u32[]{:S(2)}) async-start(f32[64,16,256]{2,1,0:T(8,128)} %fusion.10), calls=%async_computation | async-start | bytes 2097152 | tf_op jit(solution)/shard_map/all_to_all | solution.py:158
  22.9 104.9 %all-gather.2.cloned.1.call-start = ((), (), s32[]{:S(2)}) async-start(), calls=%async_computation.2 | async-start | bytes 4259840 | tf_op jit(solution)/shard_map/all_gather | solution.py:170
  51.3 343.4 %all-reduce.2.cloned.1.call-start = ((), (), s32[]{:S(2)}) async-start(), calls=%async_computation.3 | async-start | bytes 1048576 | tf_op jit(solution)/shard_map/psum | solution.py:204
  53.9 11.1 %copy-start.5 = (f32[1,16]{1,0:T(1,128)S(1)}, f32[1,16]{1,0:T(1,128)}, u32[]{:S(2)}) copy-start(f32[1,16]{1,0:T(1,128)} %param.10) | copy-start | bytes 196
  59.4 0.8 copy-start.2
  178.2 4.3 %copy-start.3 = (bf16[128,1,128,16]{2,3,1,0:T(8,128)(2,1)S(1)}, bf16[128,1,128,16]{2,3,1,0:T(8,128)(2,1)}, u32[]{:S(2)}) copy-start(bf16[128,1,128,16]{2,3,1,0:T(8,128)(2,1)} %copy-done.2) | copy-start | bytes 1572868
  182.5 2.4 copy-start.1
Sparse Core Ops, SparseCore 0:
  51.4 76.4 all-gather.1
  349.0 45.6 all-reduce.1

commit v5 on v1

--- a/solution.py
+++ b/solution.py
@@ -7,6 +7,7 @@
 
 BOX = 256
 NS = 16
+SLAB = ("sx", "sz", "sc")
 
 
 wave_length = 0.0197
@@ -73,8 +74,8 @@
 
 
 def on_device(volume, interp, block_index, images, defocus, orient):
-    slab_count = lax.axis_size("slab")
-    slab_index = lax.axis_index("slab")
+    slab_count = lax.axis_size(SLAB)
+    slab_index = lax.axis_index(SLAB)
     orient_count = interp.shape[1]
     ori_dev = orient_count // slab_count
     block_rows = interp.shape[2]
@@ -87,7 +88,7 @@
     owned_idx = lax.dynamic_slice_in_dim(block_index[0], slab_index * ori_dev, ori_dev, 0)
     received = lax.all_to_all(
         partial_value.reshape(slab_count, ori_dev * block_rows, 2 * fourier),
-        "slab",
+        SLAB,
         split_axis=0,
         concat_axis=0,
         tiled=True,
@@ -97,7 +98,7 @@
         "osb,sopx->obpx", place, received, precision=lax.Precision.HIGHEST,
         preferred_element_type=jnp.float32,
     ).reshape(ori_dev, fourier, 2 * fourier)
-    panels = lax.all_gather(summed.astype(jnp.bfloat16), "slab", axis=0, tiled=True)
+    panels = lax.all_gather(summed.astype(jnp.bfloat16), SLAB, axis=0, tiled=True)
     phase_fwd, phase_back = phase_tables(fourier, NS, BOX)
     blk = math.gcd(img_dev, 32)
     blk_total = img_dev // blk
@@ -115,20 +116,23 @@
         ),
     )
     all_slices = backs.reshape(img_dev * picks, 2 * fourier * fourier)
-    member = (
-        orient[0].reshape(-1)[:, None] == jnp.arange(orient_count, dtype=jnp.int32)[None, :]
-    ).astype(jnp.bfloat16)
+    sizes = tuple(lax.axis_size(a) for a in SLAB)
+    perm = jnp.arange(orient_count, dtype=jnp.int32).reshape(sizes + (ori_dev,))
+    perm = perm.transpose(2, 0, 1, 3).reshape(-1)
+    member = (orient[0].reshape(-1)[:, None] == perm[None, :]).astype(jnp.bfloat16)
     contrib = lax.dot_general(
         member, all_slices, (((0,), (0,)), ((), ())), preferred_element_type=jnp.float32
     ).reshape(orient_count, fourier, 2 * fourier)
-    back_own = lax.psum_scatter(contrib, "slab", scatter_dimension=0, tiled=True).astype(jnp.bfloat16)
+    for axis in (SLAB[2], SLAB[0], SLAB[1]):
+        contrib = lax.psum_scatter(contrib, axis, scatter_dimension=0, tiled=True)
+    back_own = contrib.astype(jnp.bfloat16)
     back_own = back_own.reshape(ori_dev, block_count, block_rows, 2 * fourier)
     chosen_back = (owned_idx[:, :, None] == levels).astype(jnp.bfloat16)
     outgoing = jnp.einsum(
         "osb,obpx->sopx", chosen_back, back_own, preferred_element_type=jnp.float32
     )
     outgoing = outgoing.astype(jnp.bfloat16).reshape(slab_count * ori_dev, block_rows, 2 * fourier)
-    incoming = lax.all_to_all(outgoing, "slab", split_axis=0, concat_axis=0, tiled=True)
+    incoming = lax.all_to_all(outgoing, SLAB, split_axis=0, concat_axis=0, tiled=True)
     column = jnp.einsum("jpr,jpx->rx", interp[0], incoming, preferred_element_type=jnp.float32)
     summed_cols = lax.psum(column, "img")
     update = summed_cols / math.sqrt(img_dev * slab_count)
@@ -136,17 +140,22 @@
 
 
 def solution(mesh):
+    devices = mesh.devices
+    cores = 2
+    xs = len({d.coords[0] for d in devices.reshape(-1)}) if hasattr(devices.reshape(-1)[0], "coords") else 4
+    split = devices.reshape((xs, devices.shape[0] // (xs * cores), cores) + devices.shape[1:])
+    fine = jax.sharding.Mesh(split, SLAB + ("img",))
     return jax.shard_map(
         on_device,
-        mesh=mesh,
+        mesh=fine,
         in_specs=(
-            P("slab", None),
-            P("img", None, None, "slab"),
+            P(SLAB, None),
+            P("img", None, None, SLAB),
             P("img", None, None),
-            P("img", "slab", None, None),
-            P("img", "slab"),
-            P("img", "slab", None),
+            P("img", SLAB, None, None),
+            P("img", SLAB),
+            P("img", SLAB, None),
         ),
-        out_specs=(P("slab", None), P("img", "slab", None)),
+        out_specs=(P(SLAB, None), P("img", SLAB, None)),
         check_vma=False,
     )

time: 445 us -> 407 us (0.915)
  waiting for transfers between devices: 277 us -> 240 us
  local copies, waits for them, and re-layouts: 80.9 us -> 75.5 us
    reduce_scatter x1 -> x3, waiting for transfers between devices: 149 us -> 113 us  [on_device(): contrib = lax.psum_scatter(contrib, axis, scatter_dimension=0, tiled=True)]
    dot_general x1 -> x0, local copies, waits for them, and re-layouts: 8.08 us -> none  [on_device(): lax.dot_general(member, all_slices, (((0,), (0,)), ((), ())), preferred_e...]
  transfers between devices with their start and end apart: 4 -> 6, of which waited for: 4 -> 6; matrix products, arithmetic and copies ran while one was open for 5% -> 5% of each run, Pallas kernels for 0% -> 0%
where the time goes in v5:
time: 407 us; the launch traced here: 405 us
  waiting for transfers between devices  240 us (59%)
  local copies, waits for them, and re-layouts  75.5 us (19%)
  blocking collectives  24.7 us (6%)
  other arithmetic  20.7 us (5%)
  matrix products  17.8 us (4%)
  between operations  14 us (3%)
  starting transfers between devices  12.6 us (3%)
    reduce_scatter x3, waiting for transfers between devices, on_device(): contrib = lax.psum_scatter(contrib, axis, scatter_dimension=0, tiled=True)  113 us
    all_gather x1, waiting for transfers between devices, on_device(): lax.all_gather(summed.astype(jnp.bfloat16), SLAB, axis=0, tiled=True)  56.4 us
    psum x1, waiting for transfers between devices, on_device(): summed_cols = lax.psum(column, 'img')  44.9 us
    all_to_all x1, waiting for transfers between devices, on_device(): lax.all_to_all(partial_value.reshape(slab_count, ori_dev * block_rows, 2...  25.9 us
    all_to_all x1, blocking collectives, on_device(): lax.all_to_all(outgoing, SLAB, split_axis=0, concat_axis=0, tiled=True)  24.7 us
    unnamed x16, local copies, waits for them, and re-layouts  14.1 us
    all_to_all x1, starting transfers between devices, on_device(): lax.all_to_all(partial_value.reshape(slab_count, ori_dev * block_rows, 2...  12.2 us
    another operation x3, other arithmetic  11.8 us
  transfers between devices with their start and end apart: 6, of which 6 were waited for; matrix products, arithmetic and copies ran while one was open for 5% of the time, Pallas kernels for 0%

profile of v5, /device:TPU:6, one launch (start us, length us, event | category | flops | bytes accessed | tf_op | source)
XLA Modules:
  0.0 405.4 jit_solution(7230019686168788748)
XLA Ops:
  7.2 1.2 copy-done
  8.4 2.4 fusion.10
  10.8 12.2 %all-to-all-start = ((f32[64,16,256]{2,1,0:T(8,128)}), f32[64,16,256]{2,1,0:T(8,128)S(1)}, u32[]{:S(2)}, u32[]{:S(2)}) async-start(f32[64,16,256]{2,1,0:T(8,128)} %fusion.10), calls=%async_computation | async-start | bytes 2097152 | tf_op jit(solution)/shard_map/all_to_all | solution.py:89
  23.0 0.7 dynamic-slice_bitcast_fusion
  23.7 25.9 %all-to-all-done = f32[64,16,256]{2,1,0:T(8,128)S(1)} async-done(((f32[64,16,256]{2,1,0:T(8,128)}), f32[64,16,256]{2,1,0:T(8,128)S(1)}, u32[]{:S(2)}, u32[]{:S(2)}) %all-to-all-start) | async-done | bytes 1048608 | tf_op jit(solution)/shard_map/all_to_all | solution.py:89
  49.6 1.0 convolution_convert_fusion.1
  50.6 0.6 copy.62
  51.3 0.2 reduce-scatter.4.cloned.1.call-start
  51.8 2.1 reshape.478
  54.0 0.1 copy.68
  54.1 5.4 %fusion.14 = (bf16[128,1,128,16]{2,3,1,0:T(8,128)(2,1)S(1)}, bf16[128,1,128,16]{2,3,1,0:T(8,128)(2,1)}, bf16[128,1,128,16]{2,3,1,0:T(8,128)(2,1)S(1)}) fusion(f32[128,16]{0,1:T(8,128)S(1)} %get-tuple-element.51, f32[128,16]{1,0:T(8,128)S(1)} %copy.68), kind=kLoop, calls=%fused_computation.32 | loop fusion | flops 1572864 | bytes 1589248 | tf_op jit(solution)/shard_map/convert.7
  59.5 0.8 copy-done.2
  60.4 1.9 copy.69
  62.3 2.6 convert_element_type.148
  65.2 3.9 add_negate_fusion
  69.1 1.2 copy_multiply_fusion
  70.3 1.1 slice_bitcast_fusion.1
  71.4 56.4 %all-gather.2.cloned.1.call-done = bf16[64,128,256]{2,1,0:T(8,128)(2,1)} async-done(((bf16[1,128,256]{2,1,0:T(8,128)(2,1)}), bf16[64,128,256]{2,1,0:T(8,128)(2,1)}) %all-gather.2.cloned.1.call-update) | async-done | bytes 4194320 | tf_op jit(solution)/shard_map/all_gather | solution.py:101
  127.9 5.0 %gather_fusion = bf16[64,128,256]{2,1,0:T(8,128)(2,1)} fusion(bf16[64,128,256]{2,1,0:T(8,128)(2,1)} %all-gather.2.cloned.1.call-done, s32[1024]{0:T(1024)S(1)} %pad_clamp_fusion), kind=kCustom, calls=%fused_computation | custom fusion | bytes 8388864 | tf_op jit(solution)/shard_map/while/body/eval_jaxpr/gather | solution.py:53
  132.8 7.0 %copy.64 = f32[64,128,256]{1,2,0:T(8,128)} copy(bf16[64,128,256]{2,1,0:T(8,128)(2,1)} %gather_fusion) | data formatting | bytes 12582912 | tf_op jit(solution)/shard_map/while/body/eval_jaxpr/convert_element_type | solution.py:53
  139.9 7.8 %fusion.37 = (f32[16,4,128,1,128]{2,4,3,1,0:T(8,128)}, f32[16,4,128,1,128]{2,4,3,1,0:T(8,128)}) fusion(f32[16,4,128,2,128]{2,4,3,1,0:T(8,128)} %bitcast.66), kind=kLoop, calls=%fused_computation.75 | loop fusion | bytes 16777216 | tf_op jit(solution)/shard_map/while/body/eval_jaxpr/slice | solution.py:54
  147.7 5.5 %copy.84 = f32[16,4,128,1,128]{4,0,3,2,1:T(8,128)} copy(f32[16,4,128,1,128]{2,4,3,1,0:T(8,128)} %get-tuple-element.41) | data formatting | bytes 8388608
  153.1 5.5 %copy.85 = f32[16,4,128,1,128]{4,0,3,2,1:T(8,128)} copy(f32[16,4,128,1,128]{2,4,3,1,0:T(8,128)} %get-tuple-element.42) | data formatting | bytes 8388608
  158.6 4.9 %add_convert_fusion.1 = (bf16[16,4,128,1,128]{4,0,3,2,1:T(8,128)(2,1)S(1)}, bf16[16,4,128,1,128]{4,0,3,2,1:T(8,128)(2,1)S(1)}) fusion(f32[16,4,128,1,128]{4,0,3,2,1:T(8,128)} %copy.85, f32[16,4,128,1,128]{4,0,3,2,1:T(8,128)} %copy.84, f32[16,128,128]{2,0,1:T(8,128)} %get-tuple-element.44, f32[16,128,128]{2,0,1:T(8,128)S(1)} %get-tuple-element.43), kind=kLoop, calls=%fused_computation.9 | loop fusion | flops 8388608 | bytes 14680064 | tf_op jit(solution)/shard_map/convert.8
  163.5 0.4 pad_maximum_fusion
  163.9 6.6 %copy.67 = bf16[16,4,128,2,128]{4,3,2,1,0:T(2,128)(2,1)} copy(bf16[16,4,128,2,128]{4,0,3,2,1:T(8,128)(2,1)S(1)} %pad_maximum_fusion) | data formatting | bytes 8388608 | tf_op jit(solution)/shard_map/while/body/eval_jaxpr/stack | solution.py:56
  170.5 7.8 %convert_element_type.145 = bf16[64,32768]{1,0:T(8,128)(2,1)} reshape(bf16[16,4,128,2,128]{4,3,2,1,0:T(2,128)(2,1)} %copy.67) | data formatting | bytes 8388608 | tf_op jit(solution)/shard_map/while/body/eval_jaxpr/convert_element_type | solution.py:59
  178.3 3.7 fusion.38
  182.1 0.1 reduce_sum.19
  182.5 2.4 fusion.6
  184.9 1.5 subtract_convert_fusion
  186.4 0.4 pad_maximum_fusion.1
  186.8 6.6 %copy.72 = bf16[16,4,128,2,128]{4,3,2,1,0:T(2,128)(2,1)} copy(bf16[16,4,128,2,128]{4,0,3,2,1:T(8,128)(2,1)S(1)} %pad_maximum_fusion.1) | data formatting | bytes 8388608 | tf_op jit(solution)/shard_map/while/body/eval_jaxpr/stack | solution.py:69
  193.4 7.8 %convert_element_type.150 = bf16[64,32768]{1,0:T(8,128)(2,1)} reshape(bf16[16,4,128,2,128]{4,3,2,1,0:T(2,128)(2,1)} %copy.72) | data formatting | bytes 8388608 | tf_op jit(solution)/shard_map/while/body/eval_jaxpr/convert_element_type | solution.py:72
  201.2 6.7 %fusion = f32[64,128,256]{2,0,1:T(8,128)} fusion(bf16[8,128,8,256]{3,2,1,0:T(8,128)(2,1)} %bitcast.67, s32[64]{0:T(128)S(1)} %eq.67, s32[64]{0:T(128)S(1)} %eq.69), kind=kOutput, calls=%fused_computation.1 | convolution fusion | flops 268439552 | bytes 12583424 | tf_op jit(solution)/shard_map/dot_general | solution.py:123
  208.0 21.0 %reduce-scatter.4.cloned.1.call-done = f32[32,128,256]{2,0,1:T(8,128)} async-done(((f32[64,128,256]{2,0,1:T(8,128)}), f32[32,128,256]{2,0,1:T(8,128)}) %reduce-scatter.4.cloned.1.call-update) | async-done | bytes 4194320 | tf_op jit(solution)/shard_map/reduce_scatter | solution.py:127
  229.1 51.5 %reduce-scatter.6.cloned.1.call-done = f32[8,128,256]{2,0,1:T(8,128)} async-done(((f32[32,128,256]{2,0,1:T(8,128)}), f32[8,128,256]{2,0,1:T(8,128)}) %reduce-scatter.6.cloned.1.call-update) | async-done | bytes 1048592 | tf_op jit(solution)/shard_map/reduce_scatter | solution.py:127
  280.6 2.6 copy.74
  283.2 40.3 %reduce-scatter.8.cloned.1.call-done = f32[1,128,256]{2,1,0:T(8,128)} async-done(((f32[8,128,256]{2,1,0:T(8,128)}), f32[1,128,256]{2,1,0:T(8,128)}) %reduce-scatter.8.cloned.1.call-update) | async-done | bytes 131088 | tf_op jit(solution)/shard_map/reduce_scatter | solution.py:127
  323.5 0.9 convert_element_type.151
  324.4 0.3 fusion.3
  324.8 0.3 copy.76
  325.1 24.7 %all_to_all.10 = bf16[64,16,256]{2,1,0:T(8,128)(2,1)S(1)} all-to-all(bf16[64,16,256]{2,1,0:T(8,128)(2,1)S(1)} %copy.76), channel_id=1, replica_groups=mesh['sx'=4,'sz'=8,'sc'=2,'img'=4] {'sx','sz','sc'}, dimensions={0} | all-to-all | bytes 1048576 | tf_op jit(solution)/shard_map/all_to_all | solution.py:135
  349.8 1.3 convolution_bitcast_fusion
  351.3 0.7 broadcast_divide_fusion
  352.0 44.9 %all-reduce.2.cloned.1.call-done = f32[512,256]{0,1:T(8,128)} async-done(((f32[512,256]{0,1:T(8,128)}), f32[512,256]{0,1:T(8,128)}) %all-reduce.2.cloned.1.call-update) | async-done | bytes 524304 | tf_op jit(solution)/shard_map/psum | solution.py:137
  396.8 1.1 broadcast_multiply_fusion
  397.9 1.0 copy.78
  (42 shorter events, 1.5 us)
Async XLA Ops:
  7.2 1.2 copy-start
  7.2 44.3 %copy-start.4 = (s32[1,16,4]{1,2,0:T(4,128)S(1)}, s32[1,16,4]{1,2,0:T(4,128)}, u32[]{:S(2)}) copy-start(s32[1,16,4]{1,2,0:T(4,128)} %param.11) | copy-start | bytes 772
  10.8 38.8 %all-to-all-start = ((f32[64,16,256]{2,1,0:T(8,128)}), f32[64,16,256]{2,1,0:T(8,128)S(1)}, u32[]{:S(2)}, u32[]{:S(2)}) async-start(f32[64,16,256]{2,1,0:T(8,128)} %fusion.10), calls=%async_computation | async-start | bytes 2097152 | tf_op jit(solution)/shard_map/all_to_all | solution.py:89
  22.9 104.9 %all-gather.2.cloned.1.call-start = ((), (), s32[]{:S(2)}) async-start(), calls=%async_computation.5 | async-start | bytes 4259840 | tf_op jit(solution)/shard_map/all_gather | solution.py:101
  51.3 177.7 %reduce-scatter.4.cloned.1.call-start = ((), (), s32[]{:S(2)}) async-start(), calls=%async_computation.6 | async-start | bytes 12582912 | tf_op jit(solution)/shard_map/reduce_scatter | solution.py:127
  53.9 11.2 %copy-start.5 = (f32[1,16]{1,0:T(1,128)S(1)}, f32[1,16]{1,0:T(1,128)}, u32[]{:S(2)}) copy-start(f32[1,16]{1,0:T(1,128)} %param.10) | copy-start | bytes 196
  59.5 0.8 copy-start.2
  178.3 4.3 %copy-start.3 = (bf16[128,1,128,16]{2,3,1,0:T(8,128)(2,1)S(1)}, bf16[128,1,128,16]{2,3,1,0:T(8,128)(2,1)}, u32[]{:S(2)}) copy-start(bf16[128,1,128,16]{2,3,1,0:T(8,128)(2,1)} %copy-done.2) | copy-start | bytes 1572868
  182.5 2.4 copy-start.1
  207.9 72.6 %reduce-scatter.6.cloned.1.call-start = ((), (), s32[]{:S(2)}) async-start(), calls=%async_computation.7 | async-start | bytes 5242880 | tf_op jit(solution)/shard_map/reduce_scatter | solution.py:127
  229.0 94.5 %reduce-scatter.8.cloned.1.call-start = ((), (), s32[]{:S(2)}) async-start(), calls=%async_computation.8 | async-start | bytes 1179648 | tf_op jit(solution)/shard_map/reduce_scatter | solution.py:127
  283.1 113.7 %all-reduce.2.cloned.1.call-start = ((), (), s32[]{:S(2)}) async-start(), calls=%async_computation.9 | async-start | bytes 1048576 | tf_op jit(solution)/shard_map/psum | solution.py:137
Sparse Core Ops, SparseCore 0:
  51.4 76.4 all-gather.1
  208.0 20.9 reduce-scatter.3
  231.7 48.7 reduce-scatter.5
  283.3 40.2 reduce-scatter.7
  351.2 45.5 all-reduce.1

commit v6 on v3

--- a/solution.py
+++ b/solution.py
@@ -3,6 +3,8 @@
 import jax
 import jax.numpy as jnp
 from jax import lax
+from jax.experimental import pallas as pl
+from jax.experimental.pallas import tpu as pltpu
 from jax.sharding import PartitionSpec as P
 
 BOX = 256
@@ -70,6 +72,93 @@
     )
     backed = backed.astype(jnp.bfloat16).reshape(count * picks, 2 * fourier * fourier)
     return (weights, backed)
+
+
+def _correlate_kernel(orient_ref, panels_ref, image_ref, ctf_ref, cos_ref, sin_ref, w_ref, acc_ref):
+    i = pl.program_id(0)
+    picks = w_ref.shape[1] // cos_ref.shape[0]
+    shifts = cos_ref.shape[0]
+    half = ctf_ref.shape[2]
+
+    @pl.when(i == 0)
+    def _():
+        acc_ref[...] = jnp.zeros_like(acc_ref)
+
+    ctf = ctf_ref[0]
+    image = image_ref[0].astype(jnp.float32)
+    ur = ctf * image[:, :half]
+    ui = ctf * image[:, half:]
+    rows = []
+    for k in range(picks):
+        panel = panels_ref[orient_ref[i * picks + k]].astype(jnp.float32)
+        pr = panel[:, :half]
+        pi = panel[:, half:]
+        prod_re = (pr * ur + pi * ui).astype(jnp.bfloat16).astype(jnp.float32)
+        prod_im = (pr * ui - pi * ur).astype(jnp.bfloat16).astype(jnp.float32)
+        for t in range(shifts):
+            v = prod_re * cos_ref[t] + prod_im * sin_ref[t]
+            rows.append(jnp.sum(v, axis=0, keepdims=True))
+    scores = jnp.sum(jnp.concatenate(rows, axis=0), axis=1, keepdims=True) / half
+    squared = scores * scores
+    mean = jnp.sum(squared, axis=0, keepdims=True) / squared.shape[0]
+    weights = squared / (mean + 1e-05)
+    w_ref[0] = weights
+    wround = weights.astype(jnp.bfloat16).astype(jnp.float32)
+    for k in range(picks):
+        er = jnp.zeros_like(ur)
+        ei = jnp.zeros_like(ur)
+        for t in range(shifts):
+            wt = wround[k * shifts + t : k * shifts + t + 1, :]
+            er = er + wt * cos_ref[t]
+            ei = ei - wt * sin_ref[t]
+        slice_re = (ur * er - ui * ei).astype(jnp.bfloat16).astype(jnp.float32)
+        slice_im = (ur * ei + ui * er).astype(jnp.bfloat16).astype(jnp.float32)
+        j = orient_ref[i * picks + k]
+        acc_ref[j, :, :half] += slice_re
+        acc_ref[j, :, half:] += slice_im
+
+
+def correlate_all(panels, images, orient, defocus):
+    count, fourier, width = images.shape
+    picks = orient.shape[1]
+    orient_count = panels.shape[0]
+    ctf = contrast(defocus, fourier, BOX)
+    freq = (jnp.arange(fourier, dtype=jnp.int32) - fourier // 2).astype(jnp.float32)
+    shift_steps = jnp.arange(NS, dtype=jnp.int32)
+    shift_x = (2 * (shift_steps // grid_side) - (grid_side - 1)).astype(jnp.float32)
+    shift_y = (2 * (shift_steps % grid_side) - (grid_side - 1)).astype(jnp.float32)
+    angle = 2.0 * math.pi / BOX * (
+        freq[None, :, None] * shift_x[:, None, None] + freq[None, None, :] * shift_y[:, None, None]
+    )
+    cos_t = jnp.cos(angle).astype(jnp.bfloat16).astype(jnp.float32)
+    sin_t = jnp.sin(angle).astype(jnp.bfloat16).astype(jnp.float32)
+    grid_spec = pltpu.PrefetchScalarGridSpec(
+        num_scalar_prefetch=1,
+        grid=(count,),
+        in_specs=[
+            pl.BlockSpec((orient_count, fourier, width), lambda i, o: (0, 0, 0)),
+            pl.BlockSpec((1, fourier, width), lambda i, o: (i, 0, 0)),
+            pl.BlockSpec((1, fourier, fourier), lambda i, o: (i, 0, 0)),
+            pl.BlockSpec((NS, fourier, fourier), lambda i, o: (0, 0, 0)),
+            pl.BlockSpec((NS, fourier, fourier), lambda i, o: (0, 0, 0)),
+        ],
+        out_specs=[
+            pl.BlockSpec((1, picks * NS, 1), lambda i, o: (i, 0, 0)),
+            pl.BlockSpec((orient_count, fourier, width), lambda i, o: (0, 0, 0)),
+        ],
+    )
+    weights, contrib = pl.pallas_call(
+        _correlate_kernel,
+        grid_spec=grid_spec,
+        out_shape=[
+            jax.ShapeDtypeStruct((count, picks * NS, 1), jnp.float32),
+            jax.ShapeDtypeStruct((orient_count, fourier, width), jnp.float32),
+        ],
+        compiler_params=pltpu.CompilerParams(
+            dimension_semantics=("arbitrary",), vmem_limit_bytes=56 * 1024 * 1024
+        ),
+    )(orient.reshape(-1), panels, images, ctf, cos_t, sin_t)
+    return weights.reshape(count, picks * NS), contrib
 
 
 def on_device(volume, interp, block_index, images, defocus, orient):
@@ -98,29 +187,7 @@
         preferred_element_type=jnp.float32,
     ).reshape(ori_dev, fourier, 2 * fourier)
     panels = lax.all_gather(summed.astype(jnp.bfloat16), "slab", axis=0, tiled=True)
-    phase_fwd, phase_back = phase_tables(fourier, NS, BOX)
-    blk = math.gcd(img_dev, 32)
-    blk_total = img_dev // blk
-
-    def per_block(pieces):
-        image_blk, list_blk, defocus_blk = pieces
-        return correlate(panels, image_blk, list_blk, defocus_blk, phase_fwd, phase_back, BOX)
-
-    weights, backs = lax.map(
-        per_block,
-        (
-            images[0].reshape(blk_total, blk, fourier, 2 * fourier),
-            orient[0].reshape(blk_total, blk, picks),
-            defocus[0].reshape(blk_total, blk),
-        ),
-    )
-    all_slices = backs.reshape(img_dev * picks, 2 * fourier * fourier)
-    member = (
-        orient[0].reshape(-1)[:, None] == jnp.arange(orient_count, dtype=jnp.int32)[None, :]
-    ).astype(jnp.bfloat16)
-    contrib = lax.dot_general(
-        member, all_slices, (((0,), (0,)), ((), ())), preferred_element_type=jnp.float32
-    ).reshape(orient_count, fourier, 2 * fourier)
+    weights, contrib = correlate_all(panels, images[0], orient[0], defocus[0])
     gathered = lax.all_to_all(
         contrib.astype(jnp.bfloat16), "slab", split_axis=0, concat_axis=0, tiled=True
     ).reshape(slab_count, ori_dev, fourier, 2 * fourier)
@@ -135,7 +202,7 @@
     column = jnp.einsum("jpr,jpx->rx", interp[0], incoming, preferred_element_type=jnp.float32)
     summed_cols = lax.psum(column, "img")
     update = summed_cols / math.sqrt(img_dev * slab_count)
-    return (update, weights)
+    return (update, weights[None])
 
 
 def solution(mesh):

time: 394 us -> 350 us (0.89)
  local copies, waits for them, and re-layouts: 75.3 us -> 4.54 us
  Pallas kernels: 0 us -> 32 us
  matrix products: 14.5 us -> 4.98 us
  waiting for transfers between devices: 127 us -> 136 us
    pallas_call x0 -> x1, Pallas kernels: none -> 32 us  [correlate_all(): pl.pallas_call(_correlate_kernel, grid_spec=grid_spec, out_shape=[jax.Sha...]
    convert_element_type x7 -> x0, local copies, waits for them, and re-layouts: 29.9 us -> none  [the longest x1 7.85 us: correlate(): backed.astype(jnp.bfloat16).reshape(count * picks, 2 * fourier * fourier)]
    another operation x3 -> x1, local copies, waits for them, and re-layouts: 15.1 us -> 0.6 us  [correlate_all(): orient.reshape(-1)]
    another operation x6 -> x0, other arithmetic: 12.6 us -> none
    unnamed x16 -> x10, local copies, waits for them, and re-layouts: 14.1 us -> 2.29 us
    convert_element_type x2 -> x3, other arithmetic: 0.01 us -> 9.58 us  [the longest x1 5.59 us: correlate_all(): sin_t = jnp.sin(angle).astype(jnp.bfloat16).astype(jnp.float32)]
    dot_general x3 -> x0, matrix products: 9.51 us -> none  [the longest x1 3.74 us: correlate(): jnp.dot(product, phase_fwd, preferred_element_type=jnp.float32) / fourier]
    all_gather x1, waiting for transfers between devices: 56.5 us -> 65.2 us  [on_device(): lax.all_gather(summed.astype(jnp.bfloat16), 'slab', axis=0, tiled=True)]
  transfers between devices with their start and end apart: 3 -> 3, of which waited for: 3 -> 3; matrix products, arithmetic and copies ran while one was open for 5% -> 4% of each run, Pallas kernels for 0% -> 0%
where the time goes in v6:
time: 350 us
  waiting for transfers between devices  136 us (39%)
  blocking collectives  127 us (36%)
  Pallas kernels  32 us (9%)
  other arithmetic  19.3 us (6%)
  between operations  14.1 us (4%)
  starting transfers between devices  12.3 us (4%)
  matrix products  4.98 us (1%)
  local copies, waits for them, and re-layouts  4.54 us (1%)
    all_to_all x1, blocking collectives, on_device(): lax.all_to_all(contrib.astype(jnp.bfloat16), 'slab', split_axis=0, concat...  102 us
    all_gather x1, waiting for transfers between devices, on_device(): lax.all_gather(summed.astype(jnp.bfloat16), 'slab', axis=0, tiled=True)  65.2 us
    psum x1, waiting for transfers between devices, on_device(): summed_cols = lax.psum(column, 'img')  44.9 us
    pallas_call x1, Pallas kernels, correlate_all(): pl.pallas_call(_correlate_kernel, grid_spec=grid_spec, out_shape=[jax.Sha...  32 us
    all_to_all x1, waiting for transfers between devices, on_device(): lax.all_to_all(partial_value.reshape(slab_count, ori_dev * block_rows, 2...  25.9 us
    all_to_all x1, blocking collectives, on_device(): lax.all_to_all(outgoing, 'slab', split_axis=0, concat_axis=0, tiled=True)  24.6 us
    all_to_all x1, starting transfers between devices, on_device(): lax.all_to_all(partial_value.reshape(slab_count, ori_dev * block_rows, 2...  12.2 us
  transfers between devices with their start and end apart: 3, of which 3 were waited for; matrix products, arithmetic and copies ran while one was open for 4% of the time, Pallas kernels for 0%

profile of v6, /device:TPU:6, one launch (start us, length us, event | category | flops | bytes accessed | tf_op | source)
XLA Modules:
  0.0 349.8 jit_solution(10750484283597897052)
XLA Ops:
  7.2 0.0 copy-start
  7.2 0.0 copy-start.2
  7.2 0.0 copy-start.3
  7.2 1.2 copy-done
  8.4 2.3 fusion.2
  10.7 12.2 %all-to-all-start = ((f32[64,16,256]{2,1,0:T(8,128)}), f32[64,16,256]{2,1,0:T(8,128)S(1)}, u32[]{:S(2)}, u32[]{:S(2)}) async-start(f32[64,16,256]{2,1,0:T(8,128)} %fusion.2), calls=%async_computation | async-start | bytes 2097152 | tf_op jit(solution)/shard_map/all_to_all | solution.py:177
  22.9 0.0 all-gather.2.cloned.1.call-start
  23.0 0.7 dynamic-slice_bitcast_fusion
  23.7 25.9 %all-to-all-done = f32[64,16,256]{2,1,0:T(8,128)S(1)} async-done(((f32[64,16,256]{2,1,0:T(8,128)}), f32[64,16,256]{2,1,0:T(8,128)S(1)}, u32[]{:S(2)}, u32[]{:S(2)}) %all-to-all-start) | async-done | bytes 1048608 | tf_op jit(solution)/shard_map/all_to_all | solution.py:177
  49.6 1.0 convolution_convert_fusion.1
  50.6 0.6 copy.30
  51.3 0.0 all-gather.2.cloned.1.call-update
  51.3 0.0 all-reduce.2.cloned.1.call-start
  51.3 0.0 copy-done.2
  51.3 0.1 copy.26
  51.4 0.6 reshape_squeeze.3.orient_ref
  52.0 0.0 copy-done.3
  52.1 0.1 broadcast_multiply_fusion.2
  52.1 0.1 add_multiply_fusion.2
  52.2 4.9 %add_negate_fusion.ctf_ref = f32[16,128,128]{2,1,0:T(8,128)} fusion(f32[128,128]{1,0:T(8,128)S(1)} %get-tuple-element.19, f32[128,128]{1,0:T(8,128)S(1)} %get-tuple-element.18, f32[16]{0:T(128)S(1)} %multiply_bitcast_fusion), kind=kLoop, calls=%fused_computation.11 | loop fusion | flops 1572864 | bytes 1179712 | tf_op jit(solution)/shard_map/neg | solution.py:40
  57.1 5.6 %fusion.6 = (f32[16,128,128]{2,1,0:T(8,128)}, f32[16,128,128]{2,1,0:T(8,128)}) fusion(f32[16,128]{1,0:T(8,128)S(1)} %get-tuple-element.17, f32[16,128]{1,0:T(8,128)S(1)} %get-tuple-element.16), kind=kLoop, calls=%fused_computation.13 | loop fusion | flops 1572864 | bytes 2113536 | tf_op jit(solution)/shard_map/convert_element_type | solution.py:134
  62.7 65.2 %all-gather.2.cloned.1.call-done.panels_ref = bf16[64,128,256]{2,1,0:T(8,128)(2,1)} async-done(((bf16[1,128,256]{2,1,0:T(8,128)(2,1)}), bf16[64,128,256]{2,1,0:T(8,128)(2,1)}) %all-gather.2.cloned.1.call-update) | async-done | bytes 4194320 | tf_op jit(solution)/shard_map/all_gather | solution.py:189
  127.9 32.0 %shard_map.77 = (f32[16,64,1]{2,1,0:T(8,128)}, f32[64,128,256]{2,1,0:T(8,128)}) custom-call(s32[64]{0:T(128)} %reshape_squeeze.3.orient_ref, bf16[64,128,256]{2,1,0:T(8,128)(2,1)} %all-gather.2.cloned.1.call-done.panels_ref, bf16[16,128,256]{2,1,0:T(8,128)(2,1)} %bitcast.35, f32[16,128,128]{2,1,0:T(8,128)} %add_negate_fusion.ctf_ref, ...), custom_call_target="tpu_custom_call" | custom-call | tf_op jit(solution)/shard_map/pallas_call | solution.py:150
  159.9 4.0 %convert_element_type.95 = bf16[64,128,256]{2,1,0:T(8,128)(2,1)S(1)} convert(f32[64,128,256]{2,1,0:T(8,128)} %get-tuple-element.4) | non-fusion elementwise | flops 2097152 | bytes 12582912 | tf_op jit(solution)/shard_map/convert_element_type | solution.py:192
  163.8 101.9 %all_to_all.15 = bf16[64,128,256]{2,1,0:T(8,128)(2,1)} all-to-all(bf16[64,128,256]{2,1,0:T(8,128)(2,1)S(1)} %convert_element_type.95), channel_id=1, replica_groups=mesh['slab'=64,'img'=4] {'slab'}, dimensions={0} | all-to-all | bytes 8388608 | tf_op jit(solution)/shard_map/all_to_all | solution.py:191
  265.8 2.8 reduce_sum.12
  268.6 0.3 fusion
  268.9 0.3 copy.32
  269.2 24.6 %all_to_all.16 = bf16[64,16,256]{2,1,0:T(8,128)(2,1)S(1)} all-to-all(bf16[64,16,256]{2,1,0:T(8,128)(2,1)S(1)} %copy.32), channel_id=1, replica_groups=mesh['slab'=64,'img'=4] {'slab'}, dimensions={0} | all-to-all | bytes 1048576 | tf_op jit(solution)/shard_map/all_to_all | solution.py:201
  293.8 0.0 copy-start.1
  293.8 1.3 convolution_bitcast_fusion
  295.1 0.0 all-reduce.2.cloned.1.call-update
  295.1 0.0 copy-done.1
  295.1 0.8 reduce.3
  295.9 44.9 %all-reduce.2.cloned.1.call-done = f32[512,256]{0,1:T(8,128)} async-done(((f32[512,256]{0,1:T(8,128)}), f32[512,256]{0,1:T(8,128)}) %all-reduce.2.cloned.1.call-update) | async-done | bytes 524304 | tf_op jit(solution)/shard_map/psum | solution.py:203
  340.9 1.1 broadcast_multiply_fusion
  342.0 1.0 copy.33
  (4 shorter events, 0.0 us)
Async XLA Ops:
  7.2 1.2 copy-start
  7.2 44.1 %copy-start.2 = (s32[1,16,4]{1,2,0:T(4,128)S(1)}, s32[1,16,4]{1,2,0:T(4,128)}, u32[]{:S(2)}) copy-start(s32[1,16,4]{1,2,0:T(4,128)} %param.11) | copy-start | bytes 772
  7.2 44.9 %copy-start.3 = (f32[1,16]{1,0:T(1,128)S(1)}, f32[1,16]{1,0:T(1,128)}, u32[]{:S(2)}) copy-start(f32[1,16]{1,0:T(1,128)} %param.10) | copy-start | bytes 196
  10.7 38.8 %all-to-all-start = ((f32[64,16,256]{2,1,0:T(8,128)}), f32[64,16,256]{2,1,0:T(8,128)S(1)}, u32[]{:S(2)}, u32[]{:S(2)}) async-start(f32[64,16,256]{2,1,0:T(8,128)} %fusion.2), calls=%async_computation | async-start | bytes 2097152 | tf_op jit(solution)/shard_map/all_to_all | solution.py:177
  22.9 105.0 %all-gather.2.cloned.1.call-start = ((), (), s32[]{:S(2)}) async-start(), calls=%async_computation.3 | async-start | bytes 4259840 | tf_op jit(solution)/shard_map/all_gather | solution.py:189
  51.3 289.6 %all-reduce.2.cloned.1.call-start = ((), (), s32[]{:S(2)}) async-start(), calls=%async_computation.4 | async-start | bytes 1048576 | tf_op jit(solution)/shard_map/psum | solution.py:203
  293.8 1.3 copy-start.1
Sparse Core Ops, SparseCore 0:
  51.4 76.4 all-gather.1
  295.2 45.5 all-reduce.1

commit v7 on v6

--- a/solution.py
+++ b/solution.py
@@ -9,6 +9,7 @@
 
 BOX = 256
 NS = 16
+SLAB = ("sx", "sz", "sc")
 
 
 wave_length = 0.0197
@@ -74,7 +75,7 @@
     return (weights, backed)
 
 
-def _correlate_kernel(orient_ref, panels_ref, image_ref, ctf_ref, cos_ref, sin_ref, w_ref, acc_ref):
+def _correlate_kernel(orient_ref, row_ref, panels_ref, image_ref, ctf_ref, cos_ref, sin_ref, w_ref, acc_ref):
     i = pl.program_id(0)
     picks = w_ref.shape[1] // cos_ref.shape[0]
     shifts = cos_ref.shape[0]
@@ -113,12 +114,12 @@
             ei = ei - wt * sin_ref[t]
         slice_re = (ur * er - ui * ei).astype(jnp.bfloat16).astype(jnp.float32)
         slice_im = (ur * ei + ui * er).astype(jnp.bfloat16).astype(jnp.float32)
-        j = orient_ref[i * picks + k]
+        j = row_ref[i * picks + k]
         acc_ref[j, :, :half] += slice_re
         acc_ref[j, :, half:] += slice_im
 
 
-def correlate_all(panels, images, orient, defocus):
+def correlate_all(panels, images, orient, rows, defocus):
     count, fourier, width = images.shape
     picks = orient.shape[1]
     orient_count = panels.shape[0]
@@ -133,18 +134,18 @@
     cos_t = jnp.cos(angle).astype(jnp.bfloat16).astype(jnp.float32)
     sin_t = jnp.sin(angle).astype(jnp.bfloat16).astype(jnp.float32)
     grid_spec = pltpu.PrefetchScalarGridSpec(
-        num_scalar_prefetch=1,
+        num_scalar_prefetch=2,
         grid=(count,),
         in_specs=[
-            pl.BlockSpec((orient_count, fourier, width), lambda i, o: (0, 0, 0)),
-            pl.BlockSpec((1, fourier, width), lambda i, o: (i, 0, 0)),
-            pl.BlockSpec((1, fourier, fourier), lambda i, o: (i, 0, 0)),
-            pl.BlockSpec((NS, fourier, fourier), lambda i, o: (0, 0, 0)),
-            pl.BlockSpec((NS, fourier, fourier), lambda i, o: (0, 0, 0)),
+            pl.BlockSpec((orient_count, fourier, width), lambda i, o, w: (0, 0, 0)),
+            pl.BlockSpec((1, fourier, width), lambda i, o, w: (i, 0, 0)),
+            pl.BlockSpec((1, fourier, fourier), lambda i, o, w: (i, 0, 0)),
+            pl.BlockSpec((NS, fourier, fourier), lambda i, o, w: (0, 0, 0)),
+            pl.BlockSpec((NS, fourier, fourier), lambda i, o, w: (0, 0, 0)),
         ],
         out_specs=[
-            pl.BlockSpec((1, picks * NS, 1), lambda i, o: (i, 0, 0)),
-            pl.BlockSpec((orient_count, fourier, width), lambda i, o: (0, 0, 0)),
+            pl.BlockSpec((1, picks * NS, 1), lambda i, o, w: (i, 0, 0)),
+            pl.BlockSpec((orient_count, fourier, width), lambda i, o, w: (0, 0, 0)),
         ],
     )
     weights, contrib = pl.pallas_call(
@@ -157,13 +158,13 @@
         compiler_params=pltpu.CompilerParams(
             dimension_semantics=("arbitrary",), vmem_limit_bytes=56 * 1024 * 1024
         ),
-    )(orient.reshape(-1), panels, images, ctf, cos_t, sin_t)
+    )(orient.reshape(-1), rows.reshape(-1), panels, images, ctf, cos_t, sin_t)
     return weights.reshape(count, picks * NS), contrib
 
 
 def on_device(volume, interp, block_index, images, defocus, orient):
-    slab_count = lax.axis_size("slab")
-    slab_index = lax.axis_index("slab")
+    slab_count = lax.axis_size(SLAB)
+    slab_index = lax.axis_index(SLAB)
     orient_count = interp.shape[1]
     ori_dev = orient_count // slab_count
     block_rows = interp.shape[2]
@@ -176,7 +177,7 @@
     owned_idx = lax.dynamic_slice_in_dim(block_index[0], slab_index * ori_dev, ori_dev, 0)
     received = lax.all_to_all(
         partial_value.reshape(slab_count, ori_dev * block_rows, 2 * fourier),
-        "slab",
+        SLAB,
         split_axis=0,
         concat_axis=0,
         tiled=True,
@@ -186,19 +187,28 @@
         "osb,sopx->obpx", place, received, precision=lax.Precision.HIGHEST,
         preferred_element_type=jnp.float32,
     ).reshape(ori_dev, fourier, 2 * fourier)
-    panels = lax.all_gather(summed.astype(jnp.bfloat16), "slab", axis=0, tiled=True)
-    weights, contrib = correlate_all(panels, images[0], orient[0], defocus[0])
-    gathered = lax.all_to_all(
-        contrib.astype(jnp.bfloat16), "slab", split_axis=0, concat_axis=0, tiled=True
-    ).reshape(slab_count, ori_dev, fourier, 2 * fourier)
-    back_own = jnp.sum(gathered.astype(jnp.float32), axis=0).astype(jnp.bfloat16)
+    panels = lax.all_gather(summed.astype(jnp.bfloat16), SLAB, axis=0, tiled=True)
+    sizes = tuple(lax.axis_size(a) for a in SLAB)
+    inv_perm = jnp.arange(orient_count, dtype=jnp.int32).reshape(
+        (sizes[2], sizes[0], sizes[1], ori_dev)
+    ).transpose(1, 2, 0, 3).reshape(-1)
+    weights, contrib = correlate_all(panels, images[0], orient[0], inv_perm[orient[0]], defocus[0])
+    for axis in (SLAB[2], SLAB[0], SLAB[1]):
+        parts = lax.axis_size(axis)
+        moved = lax.all_to_all(
+            contrib.astype(jnp.bfloat16), axis, split_axis=0, concat_axis=0, tiled=True
+        )
+        contrib = jnp.sum(
+            moved.astype(jnp.float32).reshape((parts, -1) + moved.shape[1:]), axis=0
+        )
+    back_own = contrib.astype(jnp.bfloat16)
     back_own = back_own.reshape(ori_dev, block_count, block_rows, 2 * fourier)
     chosen_back = (owned_idx[:, :, None] == levels).astype(jnp.bfloat16)
     outgoing = jnp.einsum(
         "osb,obpx->sopx", chosen_back, back_own, preferred_element_type=jnp.float32
     )
     outgoing = outgoing.astype(jnp.bfloat16).reshape(slab_count * ori_dev, block_rows, 2 * fourier)
-    incoming = lax.all_to_all(outgoing, "slab", split_axis=0, concat_axis=0, tiled=True)
+    incoming = lax.all_to_all(outgoing, SLAB, split_axis=0, concat_axis=0, tiled=True)
     column = jnp.einsum("jpr,jpx->rx", interp[0], incoming, preferred_element_type=jnp.float32)
     summed_cols = lax.psum(column, "img")
     update = summed_cols / math.sqrt(img_dev * slab_count)
@@ -206,17 +216,22 @@
 
 
 def solution(mesh):
+    devices = mesh.devices
+    cores = 2
+    xs = len({d.coords[0] for d in devices.reshape(-1)}) if hasattr(devices.reshape(-1)[0], "coords") else 4
+    split = devices.reshape((xs, devices.shape[0] // (xs * cores), cores) + devices.shape[1:])
+    fine = jax.sharding.Mesh(split, SLAB + ("img",))
     return jax.shard_map(
         on_device,
-        mesh=mesh,
+        mesh=fine,
         in_specs=(
-            P("slab", None),
-            P("img", None, None, "slab"),
+            P(SLAB, None),
+            P("img", None, None, SLAB),
             P("img", None, None),
-            P("img", "slab", None, None),
-            P("img", "slab"),
-            P("img", "slab", None),
+            P("img", SLAB, None, None),
+            P("img", SLAB),
+            P("img", SLAB, None),
         ),
-        out_specs=(P("slab", None), P("img", "slab", None)),
+        out_specs=(P(SLAB, None), P("img", SLAB, None)),
         check_vma=False,
     )

time: 350 us -> 308 us (0.88)
  blocking collectives: 127 us -> 81.7 us
    all_to_all x2 -> x4, blocking collectives: 127 us -> 81.7 us  [the longest x3 59.3 us: on_device(): lax.all_to_all(contrib.astype(jnp.bfloat16), axis, split_axis=0, concat_a...]
  transfers between devices with their start and end apart: 3 -> 3, of which waited for: 3 -> 3; matrix products, arithmetic and copies ran while one was open for 4% -> 5% of each run, Pallas kernels for 0% -> 0%
where the time goes in v7:
time: 308 us; the launch traced here: 307 us
  waiting for transfers between devices  134 us (44%)
  blocking collectives  81.7 us (27%)
  Pallas kernels  32 us (10%)
  other arithmetic  21.9 us (7%)
  between operations  14.2 us (5%)
  starting transfers between devices  12.3 us (4%)
  local copies, waits for them, and re-layouts  6.12 us (2%)
  matrix products  4.98 us (2%)
    all_gather x1, waiting for transfers between devices, on_device(): lax.all_gather(summed.astype(jnp.bfloat16), SLAB, axis=0, tiled=True)  63.6 us
    all_to_all x3, blocking collectives, on_device(): lax.all_to_all(contrib.astype(jnp.bfloat16), axis, split_axis=0, concat_a...  59.3 us
    psum x1, waiting for transfers between devices, on_device(): summed_cols = lax.psum(column, 'img')  44.9 us
    pallas_call x1, Pallas kernels, correlate_all(): pl.pallas_call(_correlate_kernel, grid_spec=grid_spec, out_shape=[jax.Sha...  32 us
    all_to_all x1, waiting for transfers between devices, on_device(): lax.all_to_all(partial_value.reshape(slab_count, ori_dev * block_rows, 2...  25.9 us
    all_to_all x1, blocking collectives, on_device(): lax.all_to_all(outgoing, SLAB, split_axis=0, concat_axis=0, tiled=True)  22.3 us
    all_to_all x1, starting transfers between devices, on_device(): lax.all_to_all(partial_value.reshape(slab_count, ori_dev * block_rows, 2...  12.2 us
  transfers between devices with their start and end apart: 3, of which 3 were waited for; matrix products, arithmetic and copies ran while one was open for 5% of the time, Pallas kernels for 0%

profile of v7, /device:TPU:6, one launch (start us, length us, event | category | flops | bytes accessed | tf_op | source)
XLA Modules:
  0.0 307.4 jit_solution(4141648026732748950)
XLA Ops:
  7.2 0.0 copy-start
  7.2 0.0 copy-start.2
  7.2 1.2 copy-done
  8.4 2.4 fusion.2
  10.7 12.2 %all-to-all-start = ((f32[64,16,256]{2,1,0:T(8,128)}), f32[64,16,256]{2,1,0:T(8,128)S(1)}, u32[]{:S(2)}, u32[]{:S(2)}) async-start(f32[64,16,256]{2,1,0:T(8,128)} %fusion.2), calls=%async_computation | async-start | bytes 2097152 | tf_op jit(solution)/shard_map/all_to_all | solution.py:178
  22.9 0.0 all-gather.2.cloned.1.call-start
  23.0 0.7 dynamic-slice_bitcast_fusion
  23.7 25.9 %all-to-all-done = f32[64,16,256]{2,1,0:T(8,128)S(1)} async-done(((f32[64,16,256]{2,1,0:T(8,128)}), f32[64,16,256]{2,1,0:T(8,128)S(1)}, u32[]{:S(2)}, u32[]{:S(2)}) %all-to-all-start) | async-done | bytes 1048608 | tf_op jit(solution)/shard_map/all_to_all | solution.py:178
  49.6 1.0 convolution_convert_fusion.1
  50.6 0.6 copy.43
  51.3 0.0 all-gather.2.cloned.1.call-update
  51.3 0.0 all-reduce.2.cloned.1.call-start
  51.3 0.0 copy-done.2
  51.3 0.1 copy.38
  51.4 0.1 copy.39
  51.5 0.1 reshape.396
  51.6 0.6 reshape_squeeze.3.orient_ref
  52.2 0.1 reshape.387
  52.3 0.0 copy-start.3
  52.4 1.3 gather_fusion
  53.7 0.0 copy-done.3
  53.7 0.1 broadcast_multiply_fusion.2
  53.8 0.1 add_multiply_fusion.2
  53.8 4.9 %add_negate_fusion.ctf_ref = f32[16,128,128]{2,1,0:T(8,128)} fusion(f32[128,128]{1,0:T(8,128)S(1)} %get-tuple-element.21, f32[128,128]{1,0:T(8,128)S(1)} %get-tuple-element.20, f32[16]{0:T(128)S(1)} %multiply_bitcast_fusion), kind=kLoop, calls=%fused_computation.12 | loop fusion | flops 1572864 | bytes 1179712 | tf_op jit(solution)/shard_map/neg | solution.py:41
  58.7 5.6 %fusion.6 = (f32[16,128,128]{2,1,0:T(8,128)}, f32[16,128,128]{2,1,0:T(8,128)}) fusion(f32[16,128]{1,0:T(8,128)S(1)} %get-tuple-element.19, f32[16,128]{1,0:T(8,128)S(1)} %get-tuple-element.18), kind=kLoop, calls=%fused_computation.14 | loop fusion | flops 1572864 | bytes 2113536 | tf_op jit(solution)/shard_map/convert_element_type | solution.py:135
  64.3 63.6 %all-gather.2.cloned.1.call-done.panels_ref = bf16[64,128,256]{2,1,0:T(8,128)(2,1)} async-done(((bf16[1,128,256]{2,1,0:T(8,128)(2,1)}), bf16[64,128,256]{2,1,0:T(8,128)(2,1)}) %all-gather.2.cloned.1.call-update) | async-done | bytes 4194320 | tf_op jit(solution)/shard_map/all_gather | solution.py:190
  127.9 32.0 %shard_map.77 = (f32[16,64,1]{2,1,0:T(8,128)}, f32[64,128,256]{2,1,0:T(8,128)}) custom-call(s32[64]{0:T(128)} %reshape_squeeze.3.orient_ref, s32[64]{0:T(128)} %gather_fusion, bf16[64,128,256]{2,1,0:T(8,128)(2,1)} %all-gather.2.cloned.1.call-done.panels_ref, bf16[16,128,256]{2,1,0:T(8,128)(2,1)} %bitcast.49, f32[16,128,128]{2,1,0:T(8,128)} %add_negate_fusion.ctf_ref, ...), custom_call_target="tpu_custom_call" | custom-call | tf_op jit(solution)/shard_map/pallas_call | solution.py:151
  159.9 4.0 %convert_element_type.114 = bf16[64,128,256]{2,1,0:T(8,128)(2,1)S(1)} convert(f32[64,128,256]{2,1,0:T(8,128)} %get-tuple-element.4) | non-fusion elementwise | flops 2097152 | bytes 12582912 | tf_op jit(solution)/shard_map/convert_element_type | solution.py:199
  163.9 8.2 %all_to_all.25 = bf16[64,128,256]{2,1,0:T(8,128)(2,1)} all-to-all(bf16[64,128,256]{2,1,0:T(8,128)(2,1)S(1)} %convert_element_type.114), channel_id=1, replica_groups=mesh['sx'=4,'sz'=8,'sc'=2,'img'=4] {'sc'}, dimensions={0} | all-to-all | bytes 8388608 | tf_op jit(solution)/shard_map/all_to_all | solution.py:198
  172.0 3.3 %reduce.3 = bf16[32,128,256]{2,1,0:T(8,128)(2,1)S(1)} reduce(bf16[2,32,128,256]{3,2,1,0:T(8,128)(2,1)} %bitcast.47, bf16[]{:T(256)} %constant.86.clone.1), dimensions={0}, to_apply=%region_0.1.clone | reduce | flops 1048576 | bytes 6291458 | tf_op jit(solution)/shard_map/reduce_sum | solution.py:201
  175.3 30.0 %all_to_all.26 = bf16[32,128,256]{2,1,0:T(8,128)(2,1)} all-to-all(bf16[32,128,256]{2,1,0:T(8,128)(2,1)S(1)} %reduce.3), channel_id=1, replica_groups=mesh['sx'=4,'sz'=8,'sc'=2,'img'=4] {'sx'}, dimensions={0} | all-to-all | bytes 4194304 | tf_op jit(solution)/shard_map/all_to_all | solution.py:198
  205.3 2.0 reduce.4
  207.3 21.1 %all_to_all.27 = bf16[8,128,256]{2,1,0:T(8,128)(2,1)S(1)} all-to-all(bf16[8,128,256]{2,1,0:T(8,128)(2,1)S(1)} %reduce.4), channel_id=1, replica_groups=mesh['sx'=4,'sz'=8,'sc'=2,'img'=4] {'sz'}, dimensions={0} | all-to-all | bytes 1048576 | tf_op jit(solution)/shard_map/all_to_all | solution.py:198
  228.5 0.1 reduce_sum.32
  228.5 0.3 fusion
  228.9 0.3 copy.45
  229.2 22.3 %all_to_all.28 = bf16[64,16,256]{2,1,0:T(8,128)(2,1)S(1)} all-to-all(bf16[64,16,256]{2,1,0:T(8,128)(2,1)S(1)} %copy.45), channel_id=1, replica_groups=mesh['sx'=4,'sz'=8,'sc'=2,'img'=4] {'sx','sz','sc'}, dimensions={0} | all-to-all | bytes 1048576 | tf_op jit(solution)/shard_map/all_to_all | solution.py:211
  251.5 0.0 copy-start.1
  251.5 1.3 convolution_bitcast_fusion
  252.8 0.0 all-reduce.2.cloned.1.call-update
  252.8 0.0 copy-done.1
  252.8 0.8 reduce.5
  253.6 44.9 %all-reduce.2.cloned.1.call-done = f32[512,256]{0,1:T(8,128)} async-done(((f32[512,256]{0,1:T(8,128)}), f32[512,256]{0,1:T(8,128)}) %all-reduce.2.cloned.1.call-update) | async-done | bytes 524304 | tf_op jit(solution)/shard_map/psum | solution.py:213
  298.5 1.1 broadcast_multiply_fusion
  299.6 1.0 copy.46
  (7 shorter events, 0.0 us)
Async XLA Ops:
  7.2 1.2 copy-start
  7.2 44.2 %copy-start.2 = (s32[1,16,4]{1,2,0:T(4,128)S(1)}, s32[1,16,4]{1,2,0:T(4,128)}, u32[]{:S(2)}) copy-start(s32[1,16,4]{1,2,0:T(4,128)} %param.11) | copy-start | bytes 772
  10.7 38.8 %all-to-all-start = ((f32[64,16,256]{2,1,0:T(8,128)}), f32[64,16,256]{2,1,0:T(8,128)S(1)}, u32[]{:S(2)}, u32[]{:S(2)}) async-start(f32[64,16,256]{2,1,0:T(8,128)} %fusion.2), calls=%async_computation | async-start | bytes 2097152 | tf_op jit(solution)/shard_map/all_to_all | solution.py:178
  22.9 105.0 %all-gather.2.cloned.1.call-start = ((), (), s32[]{:S(2)}) async-start(), calls=%async_computation.5 | async-start | bytes 4259840 | tf_op jit(solution)/shard_map/all_gather | solution.py:190
  51.3 247.2 %all-reduce.2.cloned.1.call-start = ((), (), s32[]{:S(2)}) async-start(), calls=%async_computation.6 | async-start | bytes 1048576 | tf_op jit(solution)/shard_map/psum | solution.py:213
  52.3 1.3 copy-start.3
  251.5 1.3 copy-start.1
Sparse Core Ops, SparseCore 0:
  51.4 76.4 all-gather.1
  252.9 45.5 all-reduce.1

commit v8 on v7

--- a/solution.py
+++ b/solution.py
@@ -160,6 +160,60 @@
         ),
     )(orient.reshape(-1), rows.reshape(-1), panels, images, ctf, cos_t, sin_t)
     return weights.reshape(count, picks * NS), contrib
+
+
+def _img_gather_kernel(x_ref, o_ref, send_sems, recv_sems, local_sem):
+    count = o_ref.shape[0]
+    me = lax.axis_index("img")
+    here = tuple(lax.axis_index(a) for a in SLAB)
+    mesh_ids = pl.DeviceIdType.MESH
+    barrier = pltpu.get_barrier_semaphore()
+    for i in range(count - 1):
+        peer = lax.rem(me + 1 + i, count)
+        pl.semaphore_signal(barrier, inc=1, device_id=here + (peer,), device_id_type=mesh_ids)
+    pl.semaphore_wait(barrier, count - 1)
+    local = pltpu.make_async_copy(x_ref, o_ref.at[me], local_sem)
+    local.start()
+    sends = []
+    for i in range(count - 1):
+        peer = lax.rem(me + 1 + i, count)
+        copy = pltpu.make_async_remote_copy(
+            src_ref=x_ref,
+            dst_ref=o_ref.at[me],
+            send_sem=send_sems.at[i],
+            recv_sem=recv_sems.at[me],
+            device_id=here + (peer,),
+            device_id_type=mesh_ids,
+        )
+        copy.start()
+        sends.append(copy)
+    for i in range(count - 1):
+        src = lax.rem(me + 1 + i, count)
+        sends[i].wait_send()
+        pltpu.make_async_remote_copy(
+            src_ref=x_ref,
+            dst_ref=o_ref.at[src],
+            send_sem=send_sems.at[i],
+            recv_sem=recv_sems.at[src],
+            device_id=here + (src,),
+            device_id_type=mesh_ids,
+        ).wait_recv()
+    local.wait()
+
+
+def img_gather(x, count, cid):
+    return pl.pallas_call(
+        _img_gather_kernel,
+        out_shape=jax.ShapeDtypeStruct((count,) + x.shape, x.dtype),
+        in_specs=[pl.BlockSpec(memory_space=pl.ANY)],
+        out_specs=pl.BlockSpec(memory_space=pl.ANY),
+        scratch_shapes=[
+            pltpu.SemaphoreType.DMA((count,)),
+            pltpu.SemaphoreType.DMA((count,)),
+            pltpu.SemaphoreType.DMA,
+        ],
+        compiler_params=pltpu.CompilerParams(collective_id=cid, has_side_effects=True),
+    )(x)
 
 
 def on_device(volume, interp, block_index, images, defocus, orient):
@@ -210,7 +264,7 @@
     outgoing = outgoing.astype(jnp.bfloat16).reshape(slab_count * ori_dev, block_rows, 2 * fourier)
     incoming = lax.all_to_all(outgoing, SLAB, split_axis=0, concat_axis=0, tiled=True)
     column = jnp.einsum("jpr,jpx->rx", interp[0], incoming, preferred_element_type=jnp.float32)
-    summed_cols = lax.psum(column, "img")
+    summed_cols = jnp.sum(img_gather(column, lax.axis_size("img"), 0), axis=0)
     update = summed_cols / math.sqrt(img_dev * slab_count)
     return (update, weights[None])
 

time: 308 us -> 293 us (0.951)
  waiting for transfers between devices: 134 us -> 105 us
  Pallas kernels: 32 us -> 60.2 us
  blocking collectives: 81.7 us -> 59.3 us
  starting transfers between devices: 12.3 us -> 18.7 us
    psum x1 -> x0, waiting for transfers between devices: 44.9 us -> none  [on_device(): summed_cols = lax.psum(column, 'img')]
    pallas_call x0 -> x1, Pallas kernels: none -> 28.3 us  [img_gather(): pl.pallas_call(_img_gather_kernel, out_shape=jax.ShapeDtypeStruct((count,...]
    all_to_all x1 -> x0, blocking collectives: 22.3 us -> none  [on_device(): lax.all_to_all(outgoing, SLAB, split_axis=0, concat_axis=0, tiled=True)]
    all_to_all x0 -> x1, waiting for transfers between devices: none -> 15.9 us  [on_device(): lax.all_to_all(outgoing, SLAB, split_axis=0, concat_axis=0, tiled=True)]
    all_to_all x0 -> x1, starting transfers between devices: none -> 6.46 us  [on_device(): lax.all_to_all(outgoing, SLAB, split_axis=0, concat_axis=0, tiled=True)]
where the time goes in v8:
time: 293 us; the launch traced here: 292 us
  waiting for transfers between devices  105 us (36%)
  Pallas kernels  60.2 us (21%)
  blocking collectives  59.3 us (20%)
  other arithmetic  23.4 us (8%)
  starting transfers between devices  18.7 us (6%)
  between operations  14.2 us (5%)
  local copies, waits for them, and re-layouts  5.86 us (2%)
  matrix products  5.06 us (2%)
    all_gather x1, waiting for transfers between devices, on_device(): lax.all_gather(summed.astype(jnp.bfloat16), SLAB, axis=0, tiled=True)  63.7 us
    all_to_all x3, blocking collectives, on_device(): lax.all_to_all(contrib.astype(jnp.bfloat16), axis, split_axis=0, concat_a...  59.3 us
    pallas_call x1, Pallas kernels, correlate_all(): pl.pallas_call(_correlate_kernel, grid_spec=grid_spec, out_shape=[jax.Sha...  32 us
    pallas_call x1, Pallas kernels, img_gather(): pl.pallas_call(_img_gather_kernel, out_shape=jax.ShapeDtypeStruct((count,...  28.3 us
    all_to_all x1, waiting for transfers between devices, on_device(): lax.all_to_all(partial_value.reshape(slab_count, ori_dev * block_rows, 2...  25.9 us
    all_to_all x1, waiting for transfers between devices, on_device(): lax.all_to_all(outgoing, SLAB, split_axis=0, concat_axis=0, tiled=True)  15.9 us
    all_to_all x1, starting transfers between devices, on_device(): lax.all_to_all(partial_value.reshape(slab_count, ori_dev * block_rows, 2...  12.2 us
    all_to_all x1, starting transfers between devices, on_device(): lax.all_to_all(outgoing, SLAB, split_axis=0, concat_axis=0, tiled=True)  6.46 us
  transfers between devices with their start and end apart: 3, of which 3 were waited for; matrix products, arithmetic and copies ran while one was open for 5% of the time, Pallas kernels for 0%

profile of v8, /device:TPU:6, one launch (start us, length us, event | category | flops | bytes accessed | tf_op | source)
XLA Modules:
  0.0 292.2 jit_solution(2810653916426096738)
XLA Ops:
  7.2 0.0 copy-start
  7.2 0.0 copy-start.2
  7.2 1.2 copy-done
  8.4 2.4 fusion.2
  10.8 12.2 %all-to-all-start = ((f32[64,16,256]{2,1,0:T(8,128)}), f32[64,16,256]{2,1,0:T(8,128)S(1)}, u32[]{:S(2)}, u32[]{:S(2)}) async-start(f32[64,16,256]{2,1,0:T(8,128)} %fusion.2), calls=%async_computation | async-start | bytes 2097152 | tf_op jit(solution)/shard_map/all_to_all | solution.py:232
  22.9 0.0 all-gather.2.cloned.1.call-start
  23.0 0.7 dynamic-slice_bitcast_fusion
  23.7 25.9 %all-to-all-done = f32[64,16,256]{2,1,0:T(8,128)S(1)} async-done(((f32[64,16,256]{2,1,0:T(8,128)}), f32[64,16,256]{2,1,0:T(8,128)S(1)}, u32[]{:S(2)}, u32[]{:S(2)}) %all-to-all-start) | async-done | bytes 1048608 | tf_op jit(solution)/shard_map/all_to_all | solution.py:232
  49.6 1.0 convolution_convert_fusion.1
  50.6 0.6 copy.43
  51.3 0.0 all-gather.2.cloned.1.call-update
  51.3 0.0 copy-done.2
  51.3 0.1 copy.38
  51.4 0.1 copy.39
  51.5 0.1 reshape.396
  51.6 0.6 reshape_squeeze.3.orient_ref
  52.2 0.1 reshape.387
  52.3 0.0 copy-start.3
  52.3 1.3 gather_fusion
  53.6 0.0 copy-done.3
  53.6 0.1 broadcast_multiply_fusion.2
  53.7 0.1 add_multiply_fusion.2
  53.8 4.9 %add_negate_fusion.ctf_ref = f32[16,128,128]{2,1,0:T(8,128)} fusion(f32[128,128]{1,0:T(8,128)S(1)} %get-tuple-element.11, f32[128,128]{1,0:T(8,128)S(1)} %get-tuple-element.10, f32[16]{0:T(128)S(1)} %multiply_bitcast_fusion), kind=kLoop, calls=%fused_computation.12 | loop fusion | flops 1572864 | bytes 1179712 | tf_op jit(solution)/shard_map/neg | solution.py:41
  58.6 5.6 %fusion.6 = (f32[16,128,128]{2,1,0:T(8,128)}, f32[16,128,128]{2,1,0:T(8,128)}) fusion(f32[16,128]{1,0:T(8,128)S(1)} %get-tuple-element.9, f32[16,128]{1,0:T(8,128)S(1)} %get-tuple-element.8), kind=kLoop, calls=%fused_computation.14 | loop fusion | flops 1572864 | bytes 2113536 | tf_op jit(solution)/shard_map/convert_element_type | solution.py:135
  64.2 63.7 %all-gather.2.cloned.1.call-done.panels_ref = bf16[64,128,256]{2,1,0:T(8,128)(2,1)} async-done(((bf16[1,128,256]{2,1,0:T(8,128)(2,1)}), bf16[64,128,256]{2,1,0:T(8,128)(2,1)}) %all-gather.2.cloned.1.call-update) | async-done | bytes 4194320 | tf_op jit(solution)/shard_map/all_gather | solution.py:244
  127.9 32.0 %shard_map.77 = (f32[16,64,1]{2,1,0:T(8,128)}, f32[64,128,256]{2,1,0:T(8,128)}) custom-call(s32[64]{0:T(128)} %reshape_squeeze.3.orient_ref, s32[64]{0:T(128)} %gather_fusion, bf16[64,128,256]{2,1,0:T(8,128)(2,1)} %all-gather.2.cloned.1.call-done.panels_ref, bf16[16,128,256]{2,1,0:T(8,128)(2,1)} %bitcast.49, f32[16,128,128]{2,1,0:T(8,128)} %add_negate_fusion.ctf_ref, ...), custom_call_target="tpu_custom_call" | custom-call | tf_op jit(solution)/shard_map/pallas_call | solution.py:151
  159.9 4.0 %convert_element_type.114 = bf16[64,128,256]{2,1,0:T(8,128)(2,1)S(1)} convert(f32[64,128,256]{2,1,0:T(8,128)} %get-tuple-element.4) | non-fusion elementwise | flops 2097152 | bytes 12582912 | tf_op jit(solution)/shard_map/convert_element_type | solution.py:253
  163.9 8.2 %all_to_all.25 = bf16[64,128,256]{2,1,0:T(8,128)(2,1)} all-to-all(bf16[64,128,256]{2,1,0:T(8,128)(2,1)S(1)} %convert_element_type.114), channel_id=1, replica_groups=mesh['sx'=4,'sz'=8,'sc'=2,'img'=4] {'sc'}, dimensions={0} | all-to-all | bytes 8388608 | tf_op jit(solution)/shard_map/all_to_all | solution.py:252
  172.0 3.3 %reduce.3 = bf16[32,128,256]{2,1,0:T(8,128)(2,1)S(1)} reduce(bf16[2,32,128,256]{3,2,1,0:T(8,128)(2,1)} %bitcast.47, bf16[]{:T(256)} %constant.86.clone.1), dimensions={0}, to_apply=%region_0.1.clone | reduce | flops 1048576 | bytes 6291458 | tf_op jit(solution)/shard_map/reduce_sum | solution.py:255
  175.3 30.0 %all_to_all.26 = bf16[32,128,256]{2,1,0:T(8,128)(2,1)} all-to-all(bf16[32,128,256]{2,1,0:T(8,128)(2,1)S(1)} %reduce.3), channel_id=1, replica_groups=mesh['sx'=4,'sz'=8,'sc'=2,'img'=4] {'sx'}, dimensions={0} | all-to-all | bytes 4194304 | tf_op jit(solution)/shard_map/all_to_all | solution.py:252
  205.3 0.0 copy-start.1
  205.3 2.0 reduce.4
  207.4 21.1 %all_to_all.27 = bf16[8,128,256]{2,1,0:T(8,128)(2,1)S(1)} all-to-all(bf16[8,128,256]{2,1,0:T(8,128)(2,1)S(1)} %reduce.4), channel_id=1, replica_groups=mesh['sx'=4,'sz'=8,'sc'=2,'img'=4] {'sz'}, dimensions={0} | all-to-all | bytes 1048576 | tf_op jit(solution)/shard_map/all_to_all | solution.py:252
  228.5 0.1 reduce_sum.41
  228.6 0.3 fusion
  228.9 1.1 copy.45
  230.0 6.5 %all-to-all-start.4 = ((bf16[64,16,256]{2,1,0:T(8,128)(2,1)}), bf16[64,16,256]{2,1,0:T(8,128)(2,1)S(1)}, u32[]{:S(2)}, u32[]{:S(2)}) async-start(bf16[64,16,256]{2,1,0:T(8,128)(2,1)} %copy.45), calls=%async_computation.4 | async-start | bytes 1048576 | tf_op jit(solution)/shard_map/all_to_all | solution.py:265
  236.5 0.0 copy-done.1
  236.5 0.8 reduce.5
  237.3 15.9 %all-to-all-done.4 = bf16[64,16,256]{2,1,0:T(8,128)(2,1)S(1)} async-done(((bf16[64,16,256]{2,1,0:T(8,128)(2,1)}), bf16[64,16,256]{2,1,0:T(8,128)(2,1)S(1)}, u32[]{:S(2)}, u32[]{:S(2)}) %all-to-all-start.4) | async-done | bytes 524320 | tf_op jit(solution)/shard_map/all_to_all | solution.py:265
  253.2 1.3 convolution_bitcast_fusion.x_ref
  254.5 28.3 %shard_map.78 = f32[4,512,256]{2,1,0:T(8,128)} custom-call(f32[512,256]{1,0:T(8,128)} %convolution_bitcast_fusion.x_ref), custom_call_target="tpu_custom_call" | custom-call | tf_op jit(solution)/shard_map/pallas_call | solution.py:205
  282.8 1.8 reduce_sum.42
  284.6 0.8 broadcast_multiply_fusion
  (7 shorter events, 0.0 us)
Async XLA Ops:
  7.2 1.2 copy-start
  7.2 44.1 %copy-start.2 = (s32[1,16,4]{1,2,0:T(4,128)S(1)}, s32[1,16,4]{1,2,0:T(4,128)}, u32[]{:S(2)}) copy-start(s32[1,16,4]{1,2,0:T(4,128)} %param.11) | copy-start | bytes 772
  10.8 38.8 %all-to-all-start = ((f32[64,16,256]{2,1,0:T(8,128)}), f32[64,16,256]{2,1,0:T(8,128)S(1)}, u32[]{:S(2)}, u32[]{:S(2)}) async-start(f32[64,16,256]{2,1,0:T(8,128)} %fusion.2), calls=%async_computation | async-start | bytes 2097152 | tf_op jit(solution)/shard_map/all_to_all | solution.py:232
  22.9 105.0 %all-gather.2.cloned.1.call-start = ((), (), s32[]{:S(2)}) async-start(), calls=%async_computation.5 | async-start | bytes 4259840 | tf_op jit(solution)/shard_map/all_gather | solution.py:244
  52.3 1.3 copy-start.3
  205.3 31.2 %copy-start.1 = (f32[16,64,1]{2,1,0:T(8,128)S(1)}, f32[16,64,1]{2,1,0:T(8,128)}, u32[]{:S(2)}) copy-start(f32[16,64,1]{2,1,0:T(8,128)} %get-tuple-element.5) | copy-start | bytes 12292
  230.0 23.2 %all-to-all-start.4 = ((bf16[64,16,256]{2,1,0:T(8,128)(2,1)}), bf16[64,16,256]{2,1,0:T(8,128)(2,1)S(1)}, u32[]{:S(2)}, u32[]{:S(2)}) async-start(bf16[64,16,256]{2,1,0:T(8,128)(2,1)} %copy.45), calls=%async_computation.4 | async-start | bytes 1048576 | tf_op jit(solution)/shard_map/all_to_all | solution.py:265
Sparse Core Ops, SparseCore 0:
  51.4 76.4 all-gather.1

commit v9 on v8

--- a/solution.py
+++ b/solution.py
@@ -91,7 +91,7 @@
     ui = ctf * image[:, half:]
     rows = []
     for k in range(picks):
-        panel = panels_ref[orient_ref[i * picks + k]].astype(jnp.float32)
+        panel = panels_ref[row_ref[i * picks + k]].astype(jnp.float32)
         pr = panel[:, :half]
         pi = panel[:, half:]
         prod_re = (pr * ur + pi * ui).astype(jnp.bfloat16).astype(jnp.float32)
@@ -241,7 +241,13 @@
         "osb,sopx->obpx", place, received, precision=lax.Precision.HIGHEST,
         preferred_element_type=jnp.float32,
     ).reshape(ori_dev, fourier, 2 * fourier)
-    panels = lax.all_gather(summed.astype(jnp.bfloat16), SLAB, axis=0, tiled=True)
+    panels = summed.astype(jnp.bfloat16)
+    for axis in (SLAB[1], SLAB[0], SLAB[2]):
+        parts = lax.axis_size(axis)
+        panels = lax.all_to_all(
+            jnp.broadcast_to(panels[None], (parts,) + panels.shape),
+            axis, split_axis=0, concat_axis=0, tiled=True,
+        ).reshape((-1,) + panels.shape[1:])
     sizes = tuple(lax.axis_size(a) for a in SLAB)
     inv_perm = jnp.arange(orient_count, dtype=jnp.int32).reshape(
         (sizes[2], sizes[0], sizes[1], ori_dev)

time: 293 us -> 265 us (0.904)
  waiting for transfers between devices: 105 us -> 72.3 us
  between operations: 14.2 us -> 0.8 us
  starting transfers between devices: 18.7 us -> 27.8 us
  blocking collectives: 59.3 us -> 66.1 us
    all_gather x1 -> x0, waiting for transfers between devices: 63.7 us -> none  [on_device(): lax.all_gather(summed.astype(jnp.bfloat16), SLAB, axis=0, tiled=True)]
    all_to_all x0 -> x2, waiting for transfers between devices: none -> 30.4 us  [on_device(): lax.all_to_all(jnp.broadcast_to(panels[None], (parts,) + panels.shape), a...]
    all_to_all x0 -> x2, starting transfers between devices: none -> 9.13 us  [on_device(): lax.all_to_all(jnp.broadcast_to(panels[None], (parts,) + panels.shape), a...]
    all_to_all x0 -> x1, blocking collectives: none -> 8.19 us  [on_device(): lax.all_to_all(jnp.broadcast_to(panels[None], (parts,) + panels.shape), a...]
    broadcast_in_dim x0 -> x3, local copies, waits for them, and re-layouts: none -> 3.08 us  [on_device(): jnp.broadcast_to(panels[None], (parts,) + panels.shape)]
  transfers between devices with their start and end apart: 3 -> 4, of which waited for: 3 -> 4; matrix products, arithmetic and copies ran while one was open for 5% -> 5% of each run, Pallas kernels for 0% -> 0%
where the time goes in v9:
time: 265 us; the launch traced here: 264 us
  waiting for transfers between devices  72.3 us (27%)
  blocking collectives  66.1 us (25%)
  Pallas kernels  60.5 us (23%)
  starting transfers between devices  27.8 us (10%)
  other arithmetic  23.5 us (9%)
  local copies, waits for them, and re-layouts  8.36 us (3%)
  matrix products  5.05 us (2%)
    all_to_all x3, blocking collectives, on_device(): lax.all_to_all(contrib.astype(jnp.bfloat16), axis, split_axis=0, concat_a...  58 us
    pallas_call x1, Pallas kernels, correlate_all(): pl.pallas_call(_correlate_kernel, grid_spec=grid_spec, out_shape=[jax.Sha...  32 us
    all_to_all x2, waiting for transfers between devices, on_device(): lax.all_to_all(jnp.broadcast_to(panels[None], (parts,) + panels.shape), a...  30.4 us
    pallas_call x1, Pallas kernels, img_gather(): pl.pallas_call(_img_gather_kernel, out_shape=jax.ShapeDtypeStruct((count,...  28.5 us
    all_to_all x1, waiting for transfers between devices, on_device(): lax.all_to_all(partial_value.reshape(slab_count, ori_dev * block_rows, 2...  25.9 us
    all_to_all x1, waiting for transfers between devices, on_device(): lax.all_to_all(outgoing, SLAB, split_axis=0, concat_axis=0, tiled=True)  15.9 us
    all_to_all x1, starting transfers between devices, on_device(): lax.all_to_all(partial_value.reshape(slab_count, ori_dev * block_rows, 2...  12.2 us
    all_to_all x2, starting transfers between devices, on_device(): lax.all_to_all(jnp.broadcast_to(panels[None], (parts,) + panels.shape), a...  9.13 us
  transfers between devices with their start and end apart: 4, of which 4 were waited for; matrix products, arithmetic and copies ran while one was open for 5% of the time, Pallas kernels for 0%

profile of v9, /device:TPU:6, one launch (start us, length us, event | category | flops | bytes accessed | tf_op | source)
XLA Modules:
  0.0 264.4 jit_solution(11036096426015737527)
XLA Ops:
  0.6 0.0 copy-start
  0.6 0.0 copy-start.2
  0.7 1.2 copy-done
  1.9 2.4 fusion.2
  4.2 12.2 %all-to-all-start = ((f32[64,16,256]{2,1,0:T(8,128)}), f32[64,16,256]{2,1,0:T(8,128)S(1)}, u32[]{:S(2)}, u32[]{:S(2)}) async-start(f32[64,16,256]{2,1,0:T(8,128)} %fusion.2), calls=%async_computation | async-start | bytes 2097152 | tf_op jit(solution)/shard_map/all_to_all | solution.py:232
  16.4 0.7 dynamic-slice_bitcast_fusion
  17.1 25.9 %all-to-all-done = f32[64,16,256]{2,1,0:T(8,128)S(1)} async-done(((f32[64,16,256]{2,1,0:T(8,128)}), f32[64,16,256]{2,1,0:T(8,128)S(1)}, u32[]{:S(2)}, u32[]{:S(2)}) %all-to-all-start) | async-done | bytes 1048608 | tf_op jit(solution)/shard_map/all_to_all | solution.py:232
  43.0 1.0 convolution_convert_fusion.1
  44.1 0.8 broadcast_in_dim.10
  44.9 3.9 %all-to-all-start.1 = ((bf16[8,1,128,256]{3,2,1,0:T(8,128)(2,1)}), bf16[8,1,128,256]{3,2,1,0:T(8,128)(2,1)S(1)}, u32[]{:S(2)}, u32[]{:S(2)}) async-start(bf16[8,1,128,256]{3,2,1,0:T(8,128)(2,1)} %broadcast_in_dim.10), calls=%async_computation.1 | async-start | bytes 1048576 | tf_op jit(solution)/shard_map/all_to_all | solution.py:247
  48.8 0.0 copy-done.2
  48.8 0.1 copy.30
  48.9 0.1 reshape.400
  49.0 18.7 %all-to-all-done.1 = bf16[8,1,128,256]{3,2,1,0:T(8,128)(2,1)S(1)} async-done(((bf16[8,1,128,256]{3,2,1,0:T(8,128)(2,1)}), bf16[8,1,128,256]{3,2,1,0:T(8,128)(2,1)S(1)}, u32[]{:S(2)}, u32[]{:S(2)}) %all-to-all-start.1) | async-done | bytes 524320 | tf_op jit(solution)/shard_map/all_to_all | solution.py:247
  67.7 1.6 broadcast_in_dim.12
  69.2 5.2 %all-to-all-start.2 = ((bf16[4,8,128,256]{3,2,1,0:T(8,128)(2,1)}), bf16[4,8,128,256]{3,2,1,0:T(8,128)(2,1)S(1)}, u32[]{:S(2)}, u32[]{:S(2)}) async-start(bf16[4,8,128,256]{3,2,1,0:T(8,128)(2,1)} %broadcast_in_dim.12), calls=%async_computation.2 | async-start | bytes 4194304 | tf_op jit(solution)/shard_map/all_to_all | solution.py:247
  74.5 0.1 copy.29
  74.6 0.6 reshape_squeeze.3.orient_ref
  75.2 0.1 reshape.390
  75.3 0.0 copy-start.3
  75.3 1.3 gather_fusion
  76.6 0.0 copy-done.3
  76.6 0.1 broadcast_multiply_fusion.2
  76.7 0.1 add_multiply_fusion.2
  76.8 4.9 %add_negate_fusion.ctf_ref = f32[16,128,128]{2,1,0:T(8,128)} fusion(f32[128,128]{1,0:T(8,128)S(1)} %get-tuple-element.11, f32[128,128]{1,0:T(8,128)S(1)} %get-tuple-element.10, f32[16]{0:T(128)S(1)} %multiply_bitcast_fusion), kind=kLoop, calls=%fused_computation.12 | loop fusion | flops 1572864 | bytes 1179712 | tf_op jit(solution)/shard_map/neg | solution.py:41
  81.7 5.6 %fusion.6 = (f32[16,128,128]{2,1,0:T(8,128)}, f32[16,128,128]{2,1,0:T(8,128)}) fusion(f32[16,128]{1,0:T(8,128)S(1)} %get-tuple-element.9, f32[16,128]{1,0:T(8,128)S(1)} %get-tuple-element.8), kind=kLoop, calls=%fused_computation.14 | loop fusion | flops 1572864 | bytes 2113536 | tf_op jit(solution)/shard_map/convert_element_type | solution.py:135
  87.3 11.8 %all-to-all-done.2 = bf16[4,8,128,256]{3,2,1,0:T(8,128)(2,1)S(1)} async-done(((bf16[4,8,128,256]{3,2,1,0:T(8,128)(2,1)}), bf16[4,8,128,256]{3,2,1,0:T(8,128)(2,1)S(1)}, u32[]{:S(2)}, u32[]{:S(2)}) %all-to-all-start.2) | async-done | bytes 2097184 | tf_op jit(solution)/shard_map/all_to_all | solution.py:247
  99.0 0.7 broadcast_in_dim.14
  99.7 8.2 %all_to_all.40 = bf16[2,32,128,256]{3,2,1,0:T(8,128)(2,1)} all-to-all(bf16[2,32,128,256]{3,2,1,0:T(8,128)(2,1)S(1)} %broadcast_in_dim.14), channel_id=1, replica_groups=mesh['sx'=4,'sz'=8,'sc'=2,'img'=4] {'sc'}, dimensions={0} | all-to-all | bytes 8388608 | tf_op jit(solution)/shard_map/all_to_all | solution.py:247
  107.9 32.0 %shard_map.77 = (f32[16,64,1]{2,1,0:T(8,128)}, f32[64,128,256]{2,1,0:T(8,128)}) custom-call(s32[64]{0:T(128)} %reshape_squeeze.3.orient_ref, s32[64]{0:T(128)} %gather_fusion, bf16[64,128,256]{2,1,0:T(8,128)(2,1)} %bitcast.50, bf16[16,128,256]{2,1,0:T(8,128)(2,1)} %bitcast.55, f32[16,128,128]{2,1,0:T(8,128)} %add_negate_fusion.ctf_ref, ...), custom_call_target="tpu_custom_call" | custom-call | tf_op jit(solution)/shard_map/pallas_call | solution.py:151
  139.9 4.0 %convert_element_type.112 = bf16[64,128,256]{2,1,0:T(8,128)(2,1)S(1)} convert(f32[64,128,256]{2,1,0:T(8,128)} %get-tuple-element.4) | non-fusion elementwise | flops 2097152 | bytes 12582912 | tf_op jit(solution)/shard_map/convert_element_type | solution.py:259
  143.9 8.2 %all_to_all.41 = bf16[64,128,256]{2,1,0:T(8,128)(2,1)} all-to-all(bf16[64,128,256]{2,1,0:T(8,128)(2,1)S(1)} %convert_element_type.112), channel_id=1, replica_groups=mesh['sx'=4,'sz'=8,'sc'=2,'img'=4] {'sc'}, dimensions={0} | all-to-all | bytes 8388608 | tf_op jit(solution)/shard_map/all_to_all | solution.py:258
  152.1 3.3 %reduce.3 = bf16[32,128,256]{2,1,0:T(8,128)(2,1)S(1)} reduce(bf16[2,32,128,256]{3,2,1,0:T(8,128)(2,1)} %bitcast.51, bf16[]{:T(256)} %constant.86.clone.1), dimensions={0}, to_apply=%region_0.1.clone | reduce | flops 1048576 | bytes 6291458 | tf_op jit(solution)/shard_map/reduce_sum | solution.py:261
  155.4 30.1 %all_to_all.42 = bf16[32,128,256]{2,1,0:T(8,128)(2,1)} all-to-all(bf16[32,128,256]{2,1,0:T(8,128)(2,1)S(1)} %reduce.3), channel_id=1, replica_groups=mesh['sx'=4,'sz'=8,'sc'=2,'img'=4] {'sx'}, dimensions={0} | all-to-all | bytes 4194304 | tf_op jit(solution)/shard_map/all_to_all | solution.py:258
  185.5 0.0 copy-start.1
  185.5 2.0 reduce.4
  187.5 19.7 %all_to_all.43 = bf16[8,128,256]{2,1,0:T(8,128)(2,1)S(1)} all-to-all(bf16[8,128,256]{2,1,0:T(8,128)(2,1)S(1)} %reduce.4), channel_id=1, replica_groups=mesh['sx'=4,'sz'=8,'sc'=2,'img'=4] {'sz'}, dimensions={0} | all-to-all | bytes 1048576 | tf_op jit(solution)/shard_map/all_to_all | solution.py:258
  207.2 0.1 reduce_sum.41
  207.3 0.3 fusion
  207.6 1.1 copy.36
  208.7 6.5 %all-to-all-start.7 = ((bf16[64,16,256]{2,1,0:T(8,128)(2,1)}), bf16[64,16,256]{2,1,0:T(8,128)(2,1)S(1)}, u32[]{:S(2)}, u32[]{:S(2)}) async-start(bf16[64,16,256]{2,1,0:T(8,128)(2,1)} %copy.36), calls=%async_computation.7 | async-start | bytes 1048576 | tf_op jit(solution)/shard_map/all_to_all | solution.py:271
  215.2 0.0 copy-done.1
  215.2 0.8 reduce.5
  216.0 15.9 %all-to-all-done.7 = bf16[64,16,256]{2,1,0:T(8,128)(2,1)S(1)} async-done(((bf16[64,16,256]{2,1,0:T(8,128)(2,1)}), bf16[64,16,256]{2,1,0:T(8,128)(2,1)S(1)}, u32[]{:S(2)}, u32[]{:S(2)}) %all-to-all-start.7) | async-done | bytes 524320 | tf_op jit(solution)/shard_map/all_to_all | solution.py:271
  231.9 1.3 convolution_bitcast_fusion.x_ref
  233.2 28.5 %shard_map.78 = f32[4,512,256]{2,1,0:T(8,128)} custom-call(f32[512,256]{1,0:T(8,128)} %convolution_bitcast_fusion.x_ref), custom_call_target="tpu_custom_call" | custom-call | tf_op jit(solution)/shard_map/pallas_call | solution.py:205
  261.7 1.8 reduce_sum.42
  263.5 0.8 broadcast_multiply_fusion
  (8 shorter events, 0.1 us)
Async XLA Ops:
  0.6 1.2 copy-start
  0.6 48.2 %copy-start.2 = (s32[1,16,4]{1,2,0:T(4,128)S(1)}, s32[1,16,4]{1,2,0:T(4,128)}, u32[]{:S(2)}) copy-start(s32[1,16,4]{1,2,0:T(4,128)} %param.11) | copy-start | bytes 772
  4.2 38.8 %all-to-all-start = ((f32[64,16,256]{2,1,0:T(8,128)}), f32[64,16,256]{2,1,0:T(8,128)S(1)}, u32[]{:S(2)}, u32[]{:S(2)}) async-start(f32[64,16,256]{2,1,0:T(8,128)} %fusion.2), calls=%async_computation | async-start | bytes 2097152 | tf_op jit(solution)/shard_map/all_to_all | solution.py:232
  44.9 22.7 %all-to-all-start.1 = ((bf16[8,1,128,256]{3,2,1,0:T(8,128)(2,1)}), bf16[8,1,128,256]{3,2,1,0:T(8,128)(2,1)S(1)}, u32[]{:S(2)}, u32[]{:S(2)}) async-start(bf16[8,1,128,256]{3,2,1,0:T(8,128)(2,1)} %broadcast_in_dim.10), calls=%async_computation.1 | async-start | bytes 1048576 | tf_op jit(solution)/shard_map/all_to_all | solution.py:247
  69.2 29.8 %all-to-all-start.2 = ((bf16[4,8,128,256]{3,2,1,0:T(8,128)(2,1)}), bf16[4,8,128,256]{3,2,1,0:T(8,128)(2,1)S(1)}, u32[]{:S(2)}, u32[]{:S(2)}) async-start(bf16[4,8,128,256]{3,2,1,0:T(8,128)(2,1)} %broadcast_in_dim.12), calls=%async_computation.2 | async-start | bytes 4194304 | tf_op jit(solution)/shard_map/all_to_all | solution.py:247
  75.3 1.3 copy-start.3
  185.5 29.7 %copy-start.1 = (f32[16,64,1]{2,1,0:T(8,128)S(1)}, f32[16,64,1]{2,1,0:T(8,128)}, u32[]{:S(2)}) copy-start(f32[16,64,1]{2,1,0:T(8,128)} %get-tuple-element.5) | copy-start | bytes 12292
  208.7 23.2 %all-to-all-start.7 = ((bf16[64,16,256]{2,1,0:T(8,128)(2,1)}), bf16[64,16,256]{2,1,0:T(8,128)(2,1)S(1)}, u32[]{:S(2)}, u32[]{:S(2)}) async-start(bf16[64,16,256]{2,1,0:T(8,128)(2,1)} %copy.36), calls=%async_computation.7 | async-start | bytes 1048576 | tf_op jit(solution)/shard_map/all_to_all | solution.py:271

commit v10 on v9

--- a/solution.py
+++ b/solution.py
@@ -216,6 +216,79 @@
     )(x)
 
 
+def _a2a_kernel(x_ref, o_ref, send_sems, recv_sems, local_sem):
+    count = x_ref.shape[0]
+    sizes = tuple(lax.axis_size(a) for a in SLAB)
+    me = lax.axis_index(SLAB)
+    grp = lax.axis_index("img")
+    mesh_ids = pl.DeviceIdType.MESH
+    barrier = pltpu.get_barrier_semaphore()
+
+    def where(peer):
+        return (peer // (sizes[1] * sizes[2]), (peer // sizes[2]) % sizes[1], peer % sizes[2], grp)
+
+    def greet(i, carry):
+        pl.semaphore_signal(
+            barrier, inc=1, device_id=where(lax.rem(me + 1 + i, count)), device_id_type=mesh_ids
+        )
+        return carry
+
+    lax.fori_loop(0, count - 1, greet, 0)
+    pl.semaphore_wait(barrier, count - 1)
+    local = pltpu.make_async_copy(x_ref.at[me], o_ref.at[me], local_sem)
+    local.start()
+
+    def outgoing(peer):
+        return pltpu.make_async_remote_copy(
+            src_ref=x_ref.at[peer],
+            dst_ref=o_ref.at[me],
+            send_sem=send_sems.at[peer],
+            recv_sem=recv_sems.at[me],
+            device_id=where(peer),
+            device_id_type=mesh_ids,
+        )
+
+    def incoming(src):
+        return pltpu.make_async_remote_copy(
+            src_ref=x_ref.at[src],
+            dst_ref=o_ref.at[src],
+            send_sem=send_sems.at[src],
+            recv_sem=recv_sems.at[src],
+            device_id=where(src),
+            device_id_type=mesh_ids,
+        )
+
+    def send(i, carry):
+        outgoing(lax.rem(me + 1 + i, count)).start()
+        return carry
+
+    lax.fori_loop(0, count - 1, send, 0)
+
+    def finish(i, carry):
+        outgoing(lax.rem(me + 1 + i, count)).wait_send()
+        incoming(lax.rem(me + count - 1 - i, count)).wait_recv()
+        return carry
+
+    lax.fori_loop(0, count - 1, finish, 0)
+    local.wait()
+
+
+def slab_all_to_all(x, cid):
+    count = x.shape[0]
+    return pl.pallas_call(
+        _a2a_kernel,
+        out_shape=jax.ShapeDtypeStruct(x.shape, x.dtype),
+        in_specs=[pl.BlockSpec(memory_space=pl.ANY)],
+        out_specs=pl.BlockSpec(memory_space=pl.ANY),
+        scratch_shapes=[
+            pltpu.SemaphoreType.DMA((count,)),
+            pltpu.SemaphoreType.DMA((count,)),
+            pltpu.SemaphoreType.DMA,
+        ],
+        compiler_params=pltpu.CompilerParams(collective_id=cid, has_side_effects=True),
+    )(x)
+
+
 def on_device(volume, interp, block_index, images, defocus, orient):
     slab_count = lax.axis_size(SLAB)
     slab_index = lax.axis_index(SLAB)
@@ -229,12 +302,8 @@
     levels = jnp.arange(block_count, dtype=jnp.int32)
     partial_value = jnp.einsum("jpr,rx->jpx", interp[0], volume, preferred_element_type=jnp.float32)
     owned_idx = lax.dynamic_slice_in_dim(block_index[0], slab_index * ori_dev, ori_dev, 0)
-    received = lax.all_to_all(
-        partial_value.reshape(slab_count, ori_dev * block_rows, 2 * fourier),
-        SLAB,
-        split_axis=0,
-        concat_axis=0,
-        tiled=True,
+    received = slab_all_to_all(
+        partial_value.reshape(slab_count, ori_dev * block_rows, 2 * fourier), 1
     ).reshape(slab_count, ori_dev, block_rows, 2 * fourier)
     place = (owned_idx[:, :, None] == levels).astype(jnp.float32)
     summed = jnp.einsum(

time: 265 us -> 263 us (level)
  Pallas kernels: 60.5 us -> 94.6 us
  waiting for transfers between devices: 72.3 us -> 45.1 us
  starting transfers between devices: 27.8 us -> 17.8 us
    pallas_call x0 -> x1, Pallas kernels: none -> 34.1 us  [slab_all_to_all(): pl.pallas_call(_a2a_kernel, out_shape=jax.ShapeDtypeStruct(x.shape, x.dty...]
    all_to_all x1 -> x0, waiting for transfers between devices: 25.9 us -> none  [on_device(): lax.all_to_all(partial_value.reshape(slab_count, ori_dev * block_rows, 2...]
    all_to_all x1 -> x0, starting transfers between devices: 12.2 us -> none  [on_device(): lax.all_to_all(partial_value.reshape(slab_count, ori_dev * block_rows, 2...]
  transfers between devices with their start and end apart: 4 -> 3, of which waited for: 4 -> 3; matrix products, arithmetic and copies ran while one was open for 5% -> 5% of each run, Pallas kernels for 0% -> 0%
where the time goes in v10:
time: 263 us
  Pallas kernels  94.6 us (36%)
  blocking collectives  66.2 us (25%)
  waiting for transfers between devices  45.1 us (17%)
  other arithmetic  23.5 us (9%)
  starting transfers between devices  17.8 us (7%)
  local copies, waits for them, and re-layouts  8.41 us (3%)
  matrix products  6.24 us (2%)
    all_to_all x3, blocking collectives, on_device(): lax.all_to_all(contrib.astype(jnp.bfloat16), axis, split_axis=0, concat_a...  58 us
    pallas_call x1, Pallas kernels, slab_all_to_all(): pl.pallas_call(_a2a_kernel, out_shape=jax.ShapeDtypeStruct(x.shape, x.dty...  34.1 us
    pallas_call x1, Pallas kernels, correlate_all(): pl.pallas_call(_correlate_kernel, grid_spec=grid_spec, out_shape=[jax.Sha...  32 us
    all_to_all x2, waiting for transfers between devices, on_device(): lax.all_to_all(jnp.broadcast_to(panels[None], (parts,) + panels.shape), a...  29.2 us
    pallas_call x1, Pallas kernels, img_gather(): pl.pallas_call(_img_gather_kernel, out_shape=jax.ShapeDtypeStruct((count,...  28.5 us
    all_to_all x1, waiting for transfers between devices, on_device(): lax.all_to_all(outgoing, SLAB, split_axis=0, concat_axis=0, tiled=True)  15.9 us
    all_to_all x2, starting transfers between devices, on_device(): lax.all_to_all(jnp.broadcast_to(panels[None], (parts,) + panels.shape), a...  11.4 us
    all_to_all x1, blocking collectives, on_device(): lax.all_to_all(jnp.broadcast_to(panels[None], (parts,) + panels.shape), a...  8.21 us
  transfers between devices with their start and end apart: 3, of which 3 were waited for; matrix products, arithmetic and copies ran while one was open for 5% of the time, Pallas kernels for 0%

profile of v10, /device:TPU:6, one launch (start us, length us, event | category | flops | bytes accessed | tf_op | source)
XLA Modules:
  0.0 262.6 jit_solution(11953887033940500209)
XLA Ops:
  0.6 0.0 copy-start
  0.6 0.0 copy-start.2
  0.7 1.2 copy-done
  1.9 2.4 fusion.2.x_ref
  4.2 34.1 %shard_map.77 = f32[64,16,256]{2,1,0:T(8,128)} custom-call(f32[64,16,256]{2,1,0:T(8,128)} %fusion.2.x_ref), custom_call_target="tpu_custom_call" | custom-call | tf_op jit(solution)/shard_map/pallas_call | solution.py:278
  38.4 0.7 dynamic-slice_bitcast_fusion
  39.1 2.2 convolution_convert_fusion.1
  41.3 0.8 broadcast_in_dim.10
  42.1 6.9 %all-to-all-start = ((bf16[8,1,128,256]{3,2,1,0:T(8,128)(2,1)}), bf16[8,1,128,256]{3,2,1,0:T(8,128)(2,1)S(1)}, u32[]{:S(2)}, u32[]{:S(2)}) async-start(bf16[8,1,128,256]{3,2,1,0:T(8,128)(2,1)} %broadcast_in_dim.10), calls=%async_computation | async-start | bytes 1048576 | tf_op jit(solution)/shard_map/all_to_all | solution.py:316
  49.0 0.0 copy-done.2
  49.0 0.1 copy.30
  49.1 0.1 reshape.400
  49.2 17.6 %all-to-all-done = bf16[8,1,128,256]{3,2,1,0:T(8,128)(2,1)S(1)} async-done(((bf16[8,1,128,256]{3,2,1,0:T(8,128)(2,1)}), bf16[8,1,128,256]{3,2,1,0:T(8,128)(2,1)S(1)}, u32[]{:S(2)}, u32[]{:S(2)}) %all-to-all-start) | async-done | bytes 524320 | tf_op jit(solution)/shard_map/all_to_all | solution.py:316
  66.8 1.6 broadcast_in_dim.12
  68.3 4.5 %all-to-all-start.1 = ((bf16[4,8,128,256]{3,2,1,0:T(8,128)(2,1)}), bf16[4,8,128,256]{3,2,1,0:T(8,128)(2,1)S(1)}, u32[]{:S(2)}, u32[]{:S(2)}) async-start(bf16[4,8,128,256]{3,2,1,0:T(8,128)(2,1)} %broadcast_in_dim.12), calls=%async_computation.1 | async-start | bytes 4194304 | tf_op jit(solution)/shard_map/all_to_all | solution.py:316
  72.9 0.1 copy.29
  72.9 0.6 reshape_squeeze.3.orient_ref
  73.5 0.1 reshape.390
  73.6 0.0 copy-start.3
  73.7 1.4 gather_fusion
  75.0 0.0 copy-done.3
  75.0 0.1 broadcast_multiply_fusion.2
  75.1 0.1 add_multiply_fusion.2
  75.2 4.9 %add_negate_fusion.ctf_ref = f32[16,128,128]{2,1,0:T(8,128)} fusion(f32[128,128]{1,0:T(8,128)S(1)} %get-tuple-element.11, f32[128,128]{1,0:T(8,128)S(1)} %get-tuple-element.10, f32[16]{0:T(128)S(1)} %multiply_bitcast_fusion), kind=kLoop, calls=%fused_computation.12 | loop fusion | flops 1572864 | bytes 1179712 | tf_op jit(solution)/shard_map/neg | solution.py:41
  80.1 5.6 %fusion.6 = (f32[16,128,128]{2,1,0:T(8,128)}, f32[16,128,128]{2,1,0:T(8,128)}) fusion(f32[16,128]{1,0:T(8,128)S(1)} %get-tuple-element.9, f32[16,128]{1,0:T(8,128)S(1)} %get-tuple-element.8), kind=kLoop, calls=%fused_computation.14 | loop fusion | flops 1572864 | bytes 2113536 | tf_op jit(solution)/shard_map/convert_element_type | solution.py:135
  85.7 11.6 %all-to-all-done.1 = bf16[4,8,128,256]{3,2,1,0:T(8,128)(2,1)S(1)} async-done(((bf16[4,8,128,256]{3,2,1,0:T(8,128)(2,1)}), bf16[4,8,128,256]{3,2,1,0:T(8,128)(2,1)S(1)}, u32[]{:S(2)}, u32[]{:S(2)}) %all-to-all-start.1) | async-done | bytes 2097184 | tf_op jit(solution)/shard_map/all_to_all | solution.py:316
  97.3 0.7 broadcast_in_dim.14
  98.0 8.2 %all_to_all.35 = bf16[2,32,128,256]{3,2,1,0:T(8,128)(2,1)} all-to-all(bf16[2,32,128,256]{3,2,1,0:T(8,128)(2,1)S(1)} %broadcast_in_dim.14), channel_id=1, replica_groups=mesh['sx'=4,'sz'=8,'sc'=2,'img'=4] {'sc'}, dimensions={0} | all-to-all | bytes 8388608 | tf_op jit(solution)/shard_map/all_to_all | solution.py:316
  106.2 32.0 %shard_map.78 = (f32[16,64,1]{2,1,0:T(8,128)}, f32[64,128,256]{2,1,0:T(8,128)}) custom-call(s32[64]{0:T(128)} %reshape_squeeze.3.orient_ref, s32[64]{0:T(128)} %gather_fusion, bf16[64,128,256]{2,1,0:T(8,128)(2,1)} %bitcast.50, bf16[16,128,256]{2,1,0:T(8,128)(2,1)} %bitcast.55, f32[16,128,128]{2,1,0:T(8,128)} %add_negate_fusion.ctf_ref, ...), custom_call_target="tpu_custom_call" | custom-call | tf_op jit(solution)/shard_map/pallas_call | solution.py:151
  138.2 4.0 %convert_element_type.112 = bf16[64,128,256]{2,1,0:T(8,128)(2,1)S(1)} convert(f32[64,128,256]{2,1,0:T(8,128)} %get-tuple-element.4) | non-fusion elementwise | flops 2097152 | bytes 12582912 | tf_op jit(solution)/shard_map/convert_element_type | solution.py:328
  142.2 8.2 %all_to_all.36 = bf16[64,128,256]{2,1,0:T(8,128)(2,1)} all-to-all(bf16[64,128,256]{2,1,0:T(8,128)(2,1)S(1)} %convert_element_type.112), channel_id=1, replica_groups=mesh['sx'=4,'sz'=8,'sc'=2,'img'=4] {'sc'}, dimensions={0} | all-to-all | bytes 8388608 | tf_op jit(solution)/shard_map/all_to_all | solution.py:327
  150.3 3.3 %reduce.3 = bf16[32,128,256]{2,1,0:T(8,128)(2,1)S(1)} reduce(bf16[2,32,128,256]{3,2,1,0:T(8,128)(2,1)} %bitcast.51, bf16[]{:T(256)} %constant.86.clone.1), dimensions={0}, to_apply=%region_0.1.clone | reduce | flops 1048576 | bytes 6291458 | tf_op jit(solution)/shard_map/reduce_sum | solution.py:330
  153.6 30.1 %all_to_all.37 = bf16[32,128,256]{2,1,0:T(8,128)(2,1)} all-to-all(bf16[32,128,256]{2,1,0:T(8,128)(2,1)S(1)} %reduce.3), channel_id=1, replica_groups=mesh['sx'=4,'sz'=8,'sc'=2,'img'=4] {'sx'}, dimensions={0} | all-to-all | bytes 4194304 | tf_op jit(solution)/shard_map/all_to_all | solution.py:327
  183.8 0.0 copy-start.1
  183.8 2.0 reduce.4
  185.8 19.7 %all_to_all.38 = bf16[8,128,256]{2,1,0:T(8,128)(2,1)S(1)} all-to-all(bf16[8,128,256]{2,1,0:T(8,128)(2,1)S(1)} %reduce.4), channel_id=1, replica_groups=mesh['sx'=4,'sz'=8,'sc'=2,'img'=4] {'sz'}, dimensions={0} | all-to-all | bytes 1048576 | tf_op jit(solution)/shard_map/all_to_all | solution.py:327
  205.5 0.1 reduce_sum.41
  205.5 0.3 fusion
  205.9 1.1 copy.34
  207.0 6.5 %all-to-all-start.6 = ((bf16[64,16,256]{2,1,0:T(8,128)(2,1)}), bf16[64,16,256]{2,1,0:T(8,128)(2,1)S(1)}, u32[]{:S(2)}, u32[]{:S(2)}) async-start(bf16[64,16,256]{2,1,0:T(8,128)(2,1)} %copy.34), calls=%async_computation.6 | async-start | bytes 1048576 | tf_op jit(solution)/shard_map/all_to_all | solution.py:340
  213.4 0.0 copy-done.1
  213.4 0.8 reduce.5
  214.3 15.9 %all-to-all-done.6 = bf16[64,16,256]{2,1,0:T(8,128)(2,1)S(1)} async-done(((bf16[64,16,256]{2,1,0:T(8,128)(2,1)}), bf16[64,16,256]{2,1,0:T(8,128)(2,1)S(1)}, u32[]{:S(2)}, u32[]{:S(2)}) %all-to-all-start.6) | async-done | bytes 524320 | tf_op jit(solution)/shard_map/all_to_all | solution.py:340
  230.2 1.3 convolution_bitcast_fusion.x_ref
  231.5 28.5 %shard_map.79 = f32[4,512,256]{2,1,0:T(8,128)} custom-call(f32[512,256]{1,0:T(8,128)} %convolution_bitcast_fusion.x_ref), custom_call_target="tpu_custom_call" | custom-call | tf_op jit(solution)/shard_map/pallas_call | solution.py:205
  260.0 1.8 reduce_sum.42
  261.8 0.8 broadcast_multiply_fusion
  (8 shorter events, 0.1 us)
Async XLA Ops:
  0.6 1.2 copy-start
  0.6 48.4 %copy-start.2 = (s32[1,16,4]{1,2,0:T(4,128)S(1)}, s32[1,16,4]{1,2,0:T(4,128)}, u32[]{:S(2)}) copy-start(s32[1,16,4]{1,2,0:T(4,128)} %param.11) | copy-start | bytes 772
  42.1 24.6 %all-to-all-start = ((bf16[8,1,128,256]{3,2,1,0:T(8,128)(2,1)}), bf16[8,1,128,256]{3,2,1,0:T(8,128)(2,1)S(1)}, u32[]{:S(2)}, u32[]{:S(2)}) async-start(bf16[8,1,128,256]{3,2,1,0:T(8,128)(2,1)} %broadcast_in_dim.10), calls=%async_computation | async-start | bytes 1048576 | tf_op jit(solution)/shard_map/all_to_all | solution.py:316
  68.3 28.9 %all-to-all-start.1 = ((bf16[4,8,128,256]{3,2,1,0:T(8,128)(2,1)}), bf16[4,8,128,256]{3,2,1,0:T(8,128)(2,1)S(1)}, u32[]{:S(2)}, u32[]{:S(2)}) async-start(bf16[4,8,128,256]{3,2,1,0:T(8,128)(2,1)} %broadcast_in_dim.12), calls=%async_computation.1 | async-start | bytes 4194304 | tf_op jit(solution)/shard_map/all_to_all | solution.py:316
  73.6 1.4 copy-start.3
  183.8 29.7 %copy-start.1 = (f32[16,64,1]{2,1,0:T(8,128)S(1)}, f32[16,64,1]{2,1,0:T(8,128)}, u32[]{:S(2)}) copy-start(f32[16,64,1]{2,1,0:T(8,128)} %get-tuple-element.5) | copy-start | bytes 12292
  207.0 23.2 %all-to-all-start.6 = ((bf16[64,16,256]{2,1,0:T(8,128)(2,1)}), bf16[64,16,256]{2,1,0:T(8,128)(2,1)S(1)}, u32[]{:S(2)}, u32[]{:S(2)}) async-start(bf16[64,16,256]{2,1,0:T(8,128)(2,1)} %copy.34), calls=%async_computation.6 | async-start | bytes 1048576 | tf_op jit(solution)/shard_map/all_to_all | solution.py:340

commit v11 on v10

--- a/solution.py
+++ b/solution.py
@@ -75,7 +75,7 @@
     return (weights, backed)
 
 
-def _correlate_kernel(orient_ref, row_ref, panels_ref, image_ref, ctf_ref, cos_ref, sin_ref, w_ref, acc_ref):
+def _correlate_kernel(orient_ref, row_ref, panels_ref, image_ref, ctf_ref, cos_ref, sin_ref, w_ref, out_ref, acc_ref):
     i = pl.program_id(0)
     picks = w_ref.shape[1] // cos_ref.shape[0]
     shifts = cos_ref.shape[0]
@@ -118,6 +118,10 @@
         acc_ref[j, :, :half] += slice_re
         acc_ref[j, :, half:] += slice_im
 
+    @pl.when(i == pl.num_programs(0) - 1)
+    def _():
+        out_ref[...] = acc_ref[...].astype(out_ref.dtype)
+
 
 def correlate_all(panels, images, orient, rows, defocus):
     count, fourier, width = images.shape
@@ -147,13 +151,14 @@
             pl.BlockSpec((1, picks * NS, 1), lambda i, o, w: (i, 0, 0)),
             pl.BlockSpec((orient_count, fourier, width), lambda i, o, w: (0, 0, 0)),
         ],
+        scratch_shapes=[pltpu.VMEM((orient_count, fourier, width), jnp.float32)],
     )
     weights, contrib = pl.pallas_call(
         _correlate_kernel,
         grid_spec=grid_spec,
         out_shape=[
             jax.ShapeDtypeStruct((count, picks * NS, 1), jnp.float32),
-            jax.ShapeDtypeStruct((orient_count, fourier, width), jnp.float32),
+            jax.ShapeDtypeStruct((orient_count, fourier, width), jnp.bfloat16),
         ],
         compiler_params=pltpu.CompilerParams(
             dimension_semantics=("arbitrary",), vmem_limit_bytes=56 * 1024 * 1024
@@ -162,58 +167,77 @@
     return weights.reshape(count, picks * NS), contrib
 
 
-def _img_gather_kernel(x_ref, o_ref, send_sems, recv_sems, local_sem):
-    count = o_ref.shape[0]
+def _img_sum_kernel(x_ref, o_ref, gat, qbuf, s1, r1, s2, r2, l1, l2):
+    count, rows = gat.shape[0], gat.shape[1]
     me = lax.axis_index("img")
     here = tuple(lax.axis_index(a) for a in SLAB)
     mesh_ids = pl.DeviceIdType.MESH
     barrier = pltpu.get_barrier_semaphore()
-    for i in range(count - 1):
-        peer = lax.rem(me + 1 + i, count)
+    peers = [lax.rem(me + 1 + i, count) for i in range(count - 1)]
+    for peer in peers:
         pl.semaphore_signal(barrier, inc=1, device_id=here + (peer,), device_id_type=mesh_ids)
     pl.semaphore_wait(barrier, count - 1)
-    local = pltpu.make_async_copy(x_ref, o_ref.at[me], local_sem)
+
+    def part(p):
+        return x_ref.at[pl.ds(pl.multiple_of(p * rows, rows), rows)]
+
+    local = pltpu.make_async_copy(part(me), gat.at[me], l1)
     local.start()
     sends = []
-    for i in range(count - 1):
-        peer = lax.rem(me + 1 + i, count)
+    for i, peer in enumerate(peers):
         copy = pltpu.make_async_remote_copy(
-            src_ref=x_ref,
-            dst_ref=o_ref.at[me],
-            send_sem=send_sems.at[i],
-            recv_sem=recv_sems.at[me],
-            device_id=here + (peer,),
-            device_id_type=mesh_ids,
+            src_ref=part(peer), dst_ref=gat.at[me], send_sem=s1.at[i], recv_sem=r1.at[me],
+            device_id=here + (peer,), device_id_type=mesh_ids,
         )
         copy.start()
         sends.append(copy)
-    for i in range(count - 1):
-        src = lax.rem(me + 1 + i, count)
+    for i, peer in enumerate(peers):
         sends[i].wait_send()
         pltpu.make_async_remote_copy(
-            src_ref=x_ref,
-            dst_ref=o_ref.at[src],
-            send_sem=send_sems.at[i],
-            recv_sem=recv_sems.at[src],
-            device_id=here + (src,),
-            device_id_type=mesh_ids,
+            src_ref=part(peer), dst_ref=gat.at[peer], send_sem=s1.at[i], recv_sem=r1.at[peer],
+            device_id=here + (peer,), device_id_type=mesh_ids,
         ).wait_recv()
     local.wait()
-
-
-def img_gather(x, count, cid):
-    return pl.pallas_call(
-        _img_gather_kernel,
-        out_shape=jax.ShapeDtypeStruct((count,) + x.shape, x.dtype),
-        in_specs=[pl.BlockSpec(memory_space=pl.ANY)],
+    qbuf[...] = jnp.sum(gat[...], axis=0)
+    local = pltpu.make_async_copy(qbuf, o_ref.at[me], l2)
+    local.start()
+    sends = []
+    for i, peer in enumerate(peers):
+        copy = pltpu.make_async_remote_copy(
+            src_ref=qbuf, dst_ref=o_ref.at[me], send_sem=s2.at[i], recv_sem=r2.at[me],
+            device_id=here + (peer,), device_id_type=mesh_ids,
+        )
+        copy.start()
+        sends.append(copy)
+    for i, peer in enumerate(peers):
+        sends[i].wait_send()
+        pltpu.make_async_remote_copy(
+            src_ref=qbuf, dst_ref=o_ref.at[peer], send_sem=s2.at[i], recv_sem=r2.at[peer],
+            device_id=here + (peer,), device_id_type=mesh_ids,
+        ).wait_recv()
+    local.wait()
+
+
+def img_sum(x, count, cid):
+    rows = x.shape[0] // count
+    out = pl.pallas_call(
+        _img_sum_kernel,
+        out_shape=jax.ShapeDtypeStruct((count, rows) + x.shape[1:], x.dtype),
+        in_specs=[pl.BlockSpec(memory_space=pltpu.VMEM)],
         out_specs=pl.BlockSpec(memory_space=pl.ANY),
         scratch_shapes=[
-            pltpu.SemaphoreType.DMA((count,)),
-            pltpu.SemaphoreType.DMA((count,)),
+            pltpu.VMEM((count, rows) + x.shape[1:], x.dtype),
+            pltpu.VMEM((rows,) + x.shape[1:], x.dtype),
+            pltpu.SemaphoreType.DMA((count,)),
+            pltpu.SemaphoreType.DMA((count,)),
+            pltpu.SemaphoreType.DMA((count,)),
+            pltpu.SemaphoreType.DMA((count,)),
+            pltpu.SemaphoreType.DMA,
             pltpu.SemaphoreType.DMA,
         ],
         compiler_params=pltpu.CompilerParams(collective_id=cid, has_side_effects=True),
     )(x)
+    return out.reshape(x.shape)
 
 
 def _a2a_kernel(x_ref, o_ref, send_sems, recv_sems, local_sem):
@@ -339,7 +363,7 @@
     outgoing = outgoing.astype(jnp.bfloat16).reshape(slab_count * ori_dev, block_rows, 2 * fourier)
     incoming = lax.all_to_all(outgoing, SLAB, split_axis=0, concat_axis=0, tiled=True)
     column = jnp.einsum("jpr,jpx->rx", interp[0], incoming, preferred_element_type=jnp.float32)
-    summed_cols = jnp.sum(img_gather(column, lax.axis_size("img"), 0), axis=0)
+    summed_cols = img_sum(column, lax.axis_size("img"), 0)
     update = summed_cols / math.sqrt(img_dev * slab_count)
     return (update, weights[None])
 

time: 263 us -> 254 us (0.966)
  Pallas kernels: 94.6 us -> 86.5 us
  other arithmetic: 23.5 us -> 18.7 us
  blocking collectives: 66.2 us -> 69.8 us
    pallas_call x1, Pallas kernels: 28.5 us -> 21.3 us  [img_sum(): pl.pallas_call(_img_sum_kernel, out_shape=jax.ShapeDtypeStruct((count, ro...]
    convert_element_type x1 -> x0, other arithmetic: 3.98 us -> none  [on_device(): contrib.astype(jnp.bfloat16)]
    all_to_all x3, blocking collectives: 58 us -> 61.6 us  [on_device(): lax.all_to_all(contrib.astype(jnp.bfloat16), axis, split_axis=0, concat_a...]
where the time goes in v11:
time: 254 us; the launch traced here: 253 us
  Pallas kernels  86.5 us (34%)
  blocking collectives  69.8 us (27%)
  waiting for transfers between devices  45.2 us (18%)
  other arithmetic  18.7 us (7%)
  starting transfers between devices  17.8 us (7%)
  local copies, waits for them, and re-layouts  8.34 us (3%)
  matrix products  6.22 us (2%)
    all_to_all x3, blocking collectives, on_device(): lax.all_to_all(contrib.astype(jnp.bfloat16), axis, split_axis=0, concat_a...  61.6 us
    pallas_call x1, Pallas kernels, slab_all_to_all(): pl.pallas_call(_a2a_kernel, out_shape=jax.ShapeDtypeStruct(x.shape, x.dty...  34.1 us
    pallas_call x1, Pallas kernels, correlate_all(): pl.pallas_call(_correlate_kernel, grid_spec=grid_spec, out_shape=[jax.Sha...  31.1 us
    all_to_all x2, waiting for transfers between devices, on_device(): lax.all_to_all(jnp.broadcast_to(panels[None], (parts,) + panels.shape), a...  29.3 us
    pallas_call x1, Pallas kernels, img_sum(): pl.pallas_call(_img_sum_kernel, out_shape=jax.ShapeDtypeStruct((count, ro...  21.3 us
    all_to_all x1, waiting for transfers between devices, on_device(): lax.all_to_all(outgoing, SLAB, split_axis=0, concat_axis=0, tiled=True)  15.9 us
    all_to_all x2, starting transfers between devices, on_device(): lax.all_to_all(jnp.broadcast_to(panels[None], (parts,) + panels.shape), a...  11.4 us
    all_to_all x1, blocking collectives, on_device(): lax.all_to_all(jnp.broadcast_to(panels[None], (parts,) + panels.shape), a...  8.13 us
  transfers between devices with their start and end apart: 3, of which 3 were waited for; matrix products, arithmetic and copies ran while one was open for 5% of the time, Pallas kernels for 0%

profile of v11, /device:TPU:6, one launch (start us, length us, event | category | flops | bytes accessed | tf_op | source)
XLA Modules:
  0.0 253.4 jit_solution(15551110955403758565)
XLA Ops:
  0.6 0.0 copy-start
  0.6 0.0 copy-start.2
  0.7 1.2 copy-done
  1.9 2.3 fusion.2.x_ref
  4.2 34.1 %shard_map.77 = f32[64,16,256]{2,1,0:T(8,128)} custom-call(f32[64,16,256]{2,1,0:T(8,128)} %fusion.2.x_ref), custom_call_target="tpu_custom_call" | custom-call | tf_op jit(solution)/shard_map/pallas_call | solution.py:302
  38.3 0.7 dynamic-slice_bitcast_fusion
  39.0 2.2 convolution_convert_fusion.1
  41.3 0.8 broadcast_in_dim.10
  42.1 6.9 %all-to-all-start = ((bf16[8,1,128,256]{3,2,1,0:T(8,128)(2,1)}), bf16[8,1,128,256]{3,2,1,0:T(8,128)(2,1)S(1)}, u32[]{:S(2)}, u32[]{:S(2)}) async-start(bf16[8,1,128,256]{3,2,1,0:T(8,128)(2,1)} %broadcast_in_dim.10), calls=%async_computation | async-start | bytes 1048576 | tf_op jit(solution)/shard_map/all_to_all | solution.py:340
  49.0 0.0 copy-done.2
  49.0 0.1 copy.30
  49.1 0.1 reshape.403
  49.2 17.6 %all-to-all-done = bf16[8,1,128,256]{3,2,1,0:T(8,128)(2,1)S(1)} async-done(((bf16[8,1,128,256]{3,2,1,0:T(8,128)(2,1)}), bf16[8,1,128,256]{3,2,1,0:T(8,128)(2,1)S(1)}, u32[]{:S(2)}, u32[]{:S(2)}) %all-to-all-start) | async-done | bytes 524320 | tf_op jit(solution)/shard_map/all_to_all | solution.py:340
  66.7 1.6 broadcast_in_dim.12
  68.3 4.5 %all-to-all-start.1 = ((bf16[4,8,128,256]{3,2,1,0:T(8,128)(2,1)}), bf16[4,8,128,256]{3,2,1,0:T(8,128)(2,1)S(1)}, u32[]{:S(2)}, u32[]{:S(2)}) async-start(bf16[4,8,128,256]{3,2,1,0:T(8,128)(2,1)} %broadcast_in_dim.12), calls=%async_computation.1 | async-start | bytes 4194304 | tf_op jit(solution)/shard_map/all_to_all | solution.py:340
  72.8 0.1 copy.29
  72.9 0.6 reshape_squeeze.3.orient_ref
  73.5 0.1 reshape.393
  73.6 0.0 copy-start.3
  73.6 1.3 gather_fusion
  74.9 0.0 copy-done.3
  74.9 0.1 broadcast_multiply_fusion.2
  75.0 0.1 add_multiply_fusion.2
  75.1 4.9 %add_negate_fusion.ctf_ref = f32[16,128,128]{2,1,0:T(8,128)} fusion(f32[128,128]{1,0:T(8,128)S(1)} %get-tuple-element.11, f32[128,128]{1,0:T(8,128)S(1)} %get-tuple-element.10, f32[16]{0:T(128)S(1)} %multiply_bitcast_fusion), kind=kLoop, calls=%fused_computation.12 | loop fusion | flops 1572864 | bytes 1179712 | tf_op jit(solution)/shard_map/neg | solution.py:41
  80.0 5.5 %fusion.6 = (f32[16,128,128]{2,1,0:T(8,128)}, f32[16,128,128]{2,1,0:T(8,128)}) fusion(f32[16,128]{1,0:T(8,128)S(1)} %get-tuple-element.9, f32[16,128]{1,0:T(8,128)S(1)} %get-tuple-element.8), kind=kLoop, calls=%fused_computation.14 | loop fusion | flops 1572864 | bytes 2113536 | tf_op jit(solution)/shard_map/convert_element_type | solution.py:139
  85.6 11.7 %all-to-all-done.1 = bf16[4,8,128,256]{3,2,1,0:T(8,128)(2,1)S(1)} async-done(((bf16[4,8,128,256]{3,2,1,0:T(8,128)(2,1)}), bf16[4,8,128,256]{3,2,1,0:T(8,128)(2,1)S(1)}, u32[]{:S(2)}, u32[]{:S(2)}) %all-to-all-start.1) | async-done | bytes 2097184 | tf_op jit(solution)/shard_map/all_to_all | solution.py:340
  97.3 0.7 broadcast_in_dim.14
  97.9 8.1 %all_to_all.35 = bf16[2,32,128,256]{3,2,1,0:T(8,128)(2,1)} all-to-all(bf16[2,32,128,256]{3,2,1,0:T(8,128)(2,1)S(1)} %broadcast_in_dim.14), channel_id=1, replica_groups=mesh['sx'=4,'sz'=8,'sc'=2,'img'=4] {'sc'}, dimensions={0} | all-to-all | bytes 8388608 | tf_op jit(solution)/shard_map/all_to_all | solution.py:340
  106.1 31.1 %shard_map.78 = (f32[16,64,1]{2,1,0:T(8,128)}, bf16[64,128,256]{2,1,0:T(8,128)(2,1)}) custom-call(s32[64]{0:T(128)} %reshape_squeeze.3.orient_ref, s32[64]{0:T(128)} %gather_fusion, bf16[64,128,256]{2,1,0:T(8,128)(2,1)} %bitcast.51, bf16[16,128,256]{2,1,0:T(8,128)(2,1)} %bitcast.56, f32[16,128,128]{2,1,0:T(8,128)} %add_negate_fusion.ctf_ref, ...), custom_call_target="tpu_custom_call" | custom-call | tf_op jit(solution)/shard_map/pallas_call | solution.py:156
  137.2 11.9 %all_to_all.36 = bf16[64,128,256]{2,1,0:T(8,128)(2,1)} all-to-all(bf16[64,128,256]{2,1,0:T(8,128)(2,1)} %get-tuple-element.4), channel_id=1, replica_groups=mesh['sx'=4,'sz'=8,'sc'=2,'img'=4] {'sc'}, dimensions={0} | all-to-all | bytes 8388608 | tf_op jit(solution)/shard_map/all_to_all | solution.py:351
  149.1 3.3 %reduce.3 = bf16[32,128,256]{2,1,0:T(8,128)(2,1)S(1)} reduce(bf16[2,32,128,256]{3,2,1,0:T(8,128)(2,1)} %bitcast.52, bf16[]{:T(256)} %constant.86.clone.1), dimensions={0}, to_apply=%region_0.1.clone | reduce | flops 1048576 | bytes 6291458 | tf_op jit(solution)/shard_map/reduce_sum | solution.py:354
  152.4 30.1 %all_to_all.37 = bf16[32,128,256]{2,1,0:T(8,128)(2,1)} all-to-all(bf16[32,128,256]{2,1,0:T(8,128)(2,1)S(1)} %reduce.3), channel_id=1, replica_groups=mesh['sx'=4,'sz'=8,'sc'=2,'img'=4] {'sx'}, dimensions={0} | all-to-all | bytes 4194304 | tf_op jit(solution)/shard_map/all_to_all | solution.py:351
  182.5 0.0 copy-start.1
  182.5 2.0 reduce.4
  184.6 19.7 %all_to_all.38 = bf16[8,128,256]{2,1,0:T(8,128)(2,1)S(1)} all-to-all(bf16[8,128,256]{2,1,0:T(8,128)(2,1)S(1)} %reduce.4), channel_id=1, replica_groups=mesh['sx'=4,'sz'=8,'sc'=2,'img'=4] {'sz'}, dimensions={0} | all-to-all | bytes 1048576 | tf_op jit(solution)/shard_map/all_to_all | solution.py:351
  204.2 0.1 reduce_sum.32
  204.3 0.3 fusion
  204.6 1.1 copy.34
  205.7 6.5 %all-to-all-start.6 = ((bf16[64,16,256]{2,1,0:T(8,128)(2,1)}), bf16[64,16,256]{2,1,0:T(8,128)(2,1)S(1)}, u32[]{:S(2)}, u32[]{:S(2)}) async-start(bf16[64,16,256]{2,1,0:T(8,128)(2,1)} %copy.34), calls=%async_computation.6 | async-start | bytes 1048576 | tf_op jit(solution)/shard_map/all_to_all | solution.py:364
  212.2 0.0 copy-done.1
  212.2 0.8 reduce.5
  213.0 15.9 %all-to-all-done.6 = bf16[64,16,256]{2,1,0:T(8,128)(2,1)S(1)} async-done(((bf16[64,16,256]{2,1,0:T(8,128)(2,1)}), bf16[64,16,256]{2,1,0:T(8,128)(2,1)S(1)}, u32[]{:S(2)}, u32[]{:S(2)}) %all-to-all-start.6) | async-done | bytes 524320 | tf_op jit(solution)/shard_map/all_to_all | solution.py:364
  228.9 1.3 convolution_bitcast_fusion.x_ref
  230.2 21.3 %shard_map.79 = f32[4,128,256]{2,1,0:T(8,128)} custom-call(f32[512,256]{1,0:T(8,128)} %convolution_bitcast_fusion.x_ref), custom_call_target="tpu_custom_call" | custom-call | tf_op jit(solution)/shard_map/pallas_call | solution.py:223
  251.5 1.9 broadcast_multiply_fusion
  (8 shorter events, 0.1 us)
Async XLA Ops:
  0.6 1.2 copy-start
  0.6 48.3 %copy-start.2 = (s32[1,16,4]{1,2,0:T(4,128)S(1)}, s32[1,16,4]{1,2,0:T(4,128)}, u32[]{:S(2)}) copy-start(s32[1,16,4]{1,2,0:T(4,128)} %param.11) | copy-start | bytes 772
  42.1 24.6 %all-to-all-start = ((bf16[8,1,128,256]{3,2,1,0:T(8,128)(2,1)}), bf16[8,1,128,256]{3,2,1,0:T(8,128)(2,1)S(1)}, u32[]{:S(2)}, u32[]{:S(2)}) async-start(bf16[8,1,128,256]{3,2,1,0:T(8,128)(2,1)} %broadcast_in_dim.10), calls=%async_computation | async-start | bytes 1048576 | tf_op jit(solution)/shard_map/all_to_all | solution.py:340
  68.3 28.9 %all-to-all-start.1 = ((bf16[4,8,128,256]{3,2,1,0:T(8,128)(2,1)}), bf16[4,8,128,256]{3,2,1,0:T(8,128)(2,1)S(1)}, u32[]{:S(2)}, u32[]{:S(2)}) async-start(bf16[4,8,128,256]{3,2,1,0:T(8,128)(2,1)} %broadcast_in_dim.12), calls=%async_computation.1 | async-start | bytes 4194304 | tf_op jit(solution)/shard_map/all_to_all | solution.py:340
  73.6 1.3 copy-start.3
  182.5 29.7 %copy-start.1 = (f32[16,64,1]{2,1,0:T(8,128)S(1)}, f32[16,64,1]{2,1,0:T(8,128)}, u32[]{:S(2)}) copy-start(f32[16,64,1]{2,1,0:T(8,128)} %get-tuple-element.5) | copy-start | bytes 12292
  205.7 23.2 %all-to-all-start.6 = ((bf16[64,16,256]{2,1,0:T(8,128)(2,1)}), bf16[64,16,256]{2,1,0:T(8,128)(2,1)S(1)}, u32[]{:S(2)}, u32[]{:S(2)}) async-start(bf16[64,16,256]{2,1,0:T(8,128)(2,1)} %copy.34), calls=%async_computation.6 | async-start | bytes 1048576 | tf_op jit(solution)/shard_map/all_to_all | solution.py:364

commit v12 on v11

--- a/solution.py
+++ b/solution.py
@@ -77,8 +77,9 @@
 
 def _correlate_kernel(orient_ref, row_ref, panels_ref, image_ref, ctf_ref, cos_ref, sin_ref, w_ref, out_ref, acc_ref):
     i = pl.program_id(0)
-    picks = w_ref.shape[1] // cos_ref.shape[0]
-    shifts = cos_ref.shape[0]
+    mirror = cos_ref.shape[0]
+    shifts = 2 * mirror
+    picks = w_ref.shape[1] // shifts
     half = ctf_ref.shape[2]
 
     @pl.when(i == 0)
@@ -96,9 +97,13 @@
         pi = panel[:, half:]
         prod_re = (pr * ur + pi * ui).astype(jnp.bfloat16).astype(jnp.float32)
         prod_im = (pr * ui - pi * ur).astype(jnp.bfloat16).astype(jnp.float32)
-        for t in range(shifts):
-            v = prod_re * cos_ref[t] + prod_im * sin_ref[t]
-            rows.append(jnp.sum(v, axis=0, keepdims=True))
+        even = []
+        odd = []
+        for t in range(mirror):
+            even.append(jnp.sum(prod_re * cos_ref[t], axis=0, keepdims=True))
+            odd.append(jnp.sum(prod_im * sin_ref[t], axis=0, keepdims=True))
+        rows.extend(even[t] + odd[t] for t in range(mirror))
+        rows.extend(even[shifts - 1 - t] - odd[shifts - 1 - t] for t in range(mirror, shifts))
     scores = jnp.sum(jnp.concatenate(rows, axis=0), axis=1, keepdims=True) / half
     squared = scores * scores
     mean = jnp.sum(squared, axis=0, keepdims=True) / squared.shape[0]
@@ -108,10 +113,11 @@
     for k in range(picks):
         er = jnp.zeros_like(ur)
         ei = jnp.zeros_like(ur)
-        for t in range(shifts):
+        for t in range(mirror):
             wt = wround[k * shifts + t : k * shifts + t + 1, :]
-            er = er + wt * cos_ref[t]
-            ei = ei - wt * sin_ref[t]
+            wm = wround[k * shifts + shifts - 1 - t : k * shifts + shifts - t, :]
+            er = er + (wt + wm) * cos_ref[t]
+            ei = ei - (wt - wm) * sin_ref[t]
         slice_re = (ur * er - ui * ei).astype(jnp.bfloat16).astype(jnp.float32)
         slice_im = (ur * ei + ui * er).astype(jnp.bfloat16).astype(jnp.float32)
         j = row_ref[i * picks + k]
@@ -129,7 +135,7 @@
     orient_count = panels.shape[0]
     ctf = contrast(defocus, fourier, BOX)
     freq = (jnp.arange(fourier, dtype=jnp.int32) - fourier // 2).astype(jnp.float32)
-    shift_steps = jnp.arange(NS, dtype=jnp.int32)
+    shift_steps = jnp.arange(NS // 2, dtype=jnp.int32)
     shift_x = (2 * (shift_steps // grid_side) - (grid_side - 1)).astype(jnp.float32)
     shift_y = (2 * (shift_steps % grid_side) - (grid_side - 1)).astype(jnp.float32)
     angle = 2.0 * math.pi / BOX * (
@@ -144,8 +150,8 @@
             pl.BlockSpec((orient_count, fourier, width), lambda i, o, w: (0, 0, 0)),
             pl.BlockSpec((1, fourier, width), lambda i, o, w: (i, 0, 0)),
             pl.BlockSpec((1, fourier, fourier), lambda i, o, w: (i, 0, 0)),
-            pl.BlockSpec((NS, fourier, fourier), lambda i, o, w: (0, 0, 0)),
-            pl.BlockSpec((NS, fourier, fourier), lambda i, o, w: (0, 0, 0)),
+            pl.BlockSpec((NS // 2, fourier, fourier), lambda i, o, w: (0, 0, 0)),
+            pl.BlockSpec((NS // 2, fourier, fourier), lambda i, o, w: (0, 0, 0)),
         ],
         out_specs=[
             pl.BlockSpec((1, picks * NS, 1), lambda i, o, w: (i, 0, 0)),

time: 254 us -> 246 us (0.969)
  Pallas kernels: 86.5 us -> 78.1 us
    pallas_call x1, Pallas kernels: 31.1 us -> 22.7 us  [correlate_all(): pl.pallas_call(_correlate_kernel, grid_spec=grid_spec, out_shape=[jax.Sha...]
where the time goes in v12:
time: 246 us; the launch traced here: 245 us
  Pallas kernels  78.1 us (32%)
  blocking collectives  69.8 us (28%)
  waiting for transfers between devices  47.6 us (19%)
  starting transfers between devices  17.8 us (7%)
  other arithmetic  16.2 us (7%)
  local copies, waits for them, and re-layouts  8.36 us (3%)
  matrix products  6.22 us (3%)
    all_to_all x3, blocking collectives, on_device(): lax.all_to_all(contrib.astype(jnp.bfloat16), axis, split_axis=0, concat_a...  61.6 us
    pallas_call x1, Pallas kernels, slab_all_to_all(): pl.pallas_call(_a2a_kernel, out_shape=jax.ShapeDtypeStruct(x.shape, x.dty...  34.1 us
    all_to_all x2, waiting for transfers between devices, on_device(): lax.all_to_all(jnp.broadcast_to(panels[None], (parts,) + panels.shape), a...  31.8 us
    pallas_call x1, Pallas kernels, correlate_all(): pl.pallas_call(_correlate_kernel, grid_spec=grid_spec, out_shape=[jax.Sha...  22.7 us
    pallas_call x1, Pallas kernels, img_sum(): pl.pallas_call(_img_sum_kernel, out_shape=jax.ShapeDtypeStruct((count, ro...  21.3 us
    all_to_all x1, waiting for transfers between devices, on_device(): lax.all_to_all(outgoing, SLAB, split_axis=0, concat_axis=0, tiled=True)  15.9 us
    all_to_all x2, starting transfers between devices, on_device(): lax.all_to_all(jnp.broadcast_to(panels[None], (parts,) + panels.shape), a...  11.4 us
    all_to_all x1, blocking collectives, on_device(): lax.all_to_all(jnp.broadcast_to(panels[None], (parts,) + panels.shape), a...  8.13 us
  transfers between devices with their start and end apart: 3, of which 3 were waited for; matrix products, arithmetic and copies ran while one was open for 5% of the time, Pallas kernels for 0%

profile of v12, /device:TPU:6, one launch (start us, length us, event | category | flops | bytes accessed | tf_op | source)
XLA Modules:
  0.0 245.0 jit_solution(17266637363632013153)
XLA Ops:
  0.6 0.0 copy-start
  0.6 0.0 copy-start.2
  0.7 1.2 copy-done
  1.9 2.3 fusion.2.x_ref
  4.2 34.1 %shard_map.77 = f32[64,16,256]{2,1,0:T(8,128)} custom-call(f32[64,16,256]{2,1,0:T(8,128)} %fusion.2.x_ref), custom_call_target="tpu_custom_call" | custom-call | tf_op jit(solution)/shard_map/pallas_call | solution.py:308
  38.3 0.7 dynamic-slice_bitcast_fusion
  39.0 2.2 convolution_convert_fusion.1
  41.3 0.8 broadcast_in_dim.10
  42.1 6.9 %all-to-all-start = ((bf16[8,1,128,256]{3,2,1,0:T(8,128)(2,1)}), bf16[8,1,128,256]{3,2,1,0:T(8,128)(2,1)S(1)}, u32[]{:S(2)}, u32[]{:S(2)}) async-start(bf16[8,1,128,256]{3,2,1,0:T(8,128)(2,1)} %broadcast_in_dim.10), calls=%async_computation | async-start | bytes 1048576 | tf_op jit(solution)/shard_map/all_to_all | solution.py:346
  49.0 0.0 copy-done.2
  49.0 0.1 copy.30
  49.1 0.1 reshape.403
  49.2 17.6 %all-to-all-done = bf16[8,1,128,256]{3,2,1,0:T(8,128)(2,1)S(1)} async-done(((bf16[8,1,128,256]{3,2,1,0:T(8,128)(2,1)}), bf16[8,1,128,256]{3,2,1,0:T(8,128)(2,1)S(1)}, u32[]{:S(2)}, u32[]{:S(2)}) %all-to-all-start) | async-done | bytes 524320 | tf_op jit(solution)/shard_map/all_to_all | solution.py:346
  66.7 1.6 broadcast_in_dim.12
  68.3 4.5 %all-to-all-start.1 = ((bf16[4,8,128,256]{3,2,1,0:T(8,128)(2,1)}), bf16[4,8,128,256]{3,2,1,0:T(8,128)(2,1)S(1)}, u32[]{:S(2)}, u32[]{:S(2)}) async-start(bf16[4,8,128,256]{3,2,1,0:T(8,128)(2,1)} %broadcast_in_dim.12), calls=%async_computation.1 | async-start | bytes 4194304 | tf_op jit(solution)/shard_map/all_to_all | solution.py:346
  72.8 0.1 copy.29
  72.9 0.6 reshape_squeeze.3.orient_ref
  73.5 0.1 reshape.393
  73.6 0.0 copy-start.3
  73.6 1.3 gather_fusion
  74.9 0.0 copy-done.3
  75.0 0.1 broadcast_multiply_fusion.2
  75.0 0.1 add_multiply_fusion.2
  75.1 3.1 %fusion.6 = (f32[8,128,128]{2,1,0:T(8,128)}, f32[8,128,128]{2,1,0:T(8,128)}) fusion(f32[8,128]{1,0:T(8,128)S(1)} %get-tuple-element.9, f32[8,128]{1,0:T(8,128)S(1)} %get-tuple-element.8), kind=kLoop, calls=%fused_computation.14 | loop fusion | flops 786432 | bytes 1056768 | tf_op jit(solution)/shard_map/convert_element_type | solution.py:145
  78.2 4.9 %add_negate_fusion.ctf_ref = f32[16,128,128]{2,1,0:T(8,128)} fusion(f32[128,128]{1,0:T(8,128)S(1)} %get-tuple-element.11, f32[128,128]{1,0:T(8,128)S(1)} %get-tuple-element.10, f32[16]{0:T(128)S(1)} %multiply_bitcast_fusion), kind=kLoop, calls=%fused_computation.9 | loop fusion | flops 1572864 | bytes 1179712 | tf_op jit(solution)/shard_map/neg | solution.py:41
  83.1 14.2 %all-to-all-done.1 = bf16[4,8,128,256]{3,2,1,0:T(8,128)(2,1)S(1)} async-done(((bf16[4,8,128,256]{3,2,1,0:T(8,128)(2,1)}), bf16[4,8,128,256]{3,2,1,0:T(8,128)(2,1)S(1)}, u32[]{:S(2)}, u32[]{:S(2)}) %all-to-all-start.1) | async-done | bytes 2097184 | tf_op jit(solution)/shard_map/all_to_all | solution.py:346
  97.3 0.7 broadcast_in_dim.14
  97.9 8.1 %all_to_all.35 = bf16[2,32,128,256]{3,2,1,0:T(8,128)(2,1)} all-to-all(bf16[2,32,128,256]{3,2,1,0:T(8,128)(2,1)S(1)} %broadcast_in_dim.14), channel_id=1, replica_groups=mesh['sx'=4,'sz'=8,'sc'=2,'img'=4] {'sc'}, dimensions={0} | all-to-all | bytes 8388608 | tf_op jit(solution)/shard_map/all_to_all | solution.py:346
  106.1 22.7 %shard_map.78 = (f32[16,64,1]{2,1,0:T(8,128)}, bf16[64,128,256]{2,1,0:T(8,128)(2,1)}) custom-call(s32[64]{0:T(128)} %reshape_squeeze.3.orient_ref, s32[64]{0:T(128)} %gather_fusion, bf16[64,128,256]{2,1,0:T(8,128)(2,1)} %bitcast.51, bf16[16,128,256]{2,1,0:T(8,128)(2,1)} %bitcast.56, f32[16,128,128]{2,1,0:T(8,128)} %add_negate_fusion.ctf_ref, ...), custom_call_target="tpu_custom_call" | custom-call | tf_op jit(solution)/shard_map/pallas_call | solution.py:162
  128.8 11.9 %all_to_all.36 = bf16[64,128,256]{2,1,0:T(8,128)(2,1)} all-to-all(bf16[64,128,256]{2,1,0:T(8,128)(2,1)} %get-tuple-element.4), channel_id=1, replica_groups=mesh['sx'=4,'sz'=8,'sc'=2,'img'=4] {'sc'}, dimensions={0} | all-to-all | bytes 8388608 | tf_op jit(solution)/shard_map/all_to_all | solution.py:357
  140.6 3.3 %reduce.3 = bf16[32,128,256]{2,1,0:T(8,128)(2,1)S(1)} reduce(bf16[2,32,128,256]{3,2,1,0:T(8,128)(2,1)} %bitcast.52, bf16[]{:T(256)} %constant.86.clone.1), dimensions={0}, to_apply=%region_0.1.clone | reduce | flops 1048576 | bytes 6291458 | tf_op jit(solution)/shard_map/reduce_sum | solution.py:360
  143.9 30.1 %all_to_all.37 = bf16[32,128,256]{2,1,0:T(8,128)(2,1)} all-to-all(bf16[32,128,256]{2,1,0:T(8,128)(2,1)S(1)} %reduce.3), channel_id=1, replica_groups=mesh['sx'=4,'sz'=8,'sc'=2,'img'=4] {'sx'}, dimensions={0} | all-to-all | bytes 4194304 | tf_op jit(solution)/shard_map/all_to_all | solution.py:357
  174.1 0.0 copy-start.1
  174.1 2.0 reduce.4
  176.1 19.7 %all_to_all.38 = bf16[8,128,256]{2,1,0:T(8,128)(2,1)S(1)} all-to-all(bf16[8,128,256]{2,1,0:T(8,128)(2,1)S(1)} %reduce.4), channel_id=1, replica_groups=mesh['sx'=4,'sz'=8,'sc'=2,'img'=4] {'sz'}, dimensions={0} | all-to-all | bytes 1048576 | tf_op jit(solution)/shard_map/all_to_all | solution.py:357
  195.8 0.1 reduce_sum.32
  195.9 0.3 fusion
  196.2 1.1 copy.34
  197.3 6.5 %all-to-all-start.6 = ((bf16[64,16,256]{2,1,0:T(8,128)(2,1)}), bf16[64,16,256]{2,1,0:T(8,128)(2,1)S(1)}, u32[]{:S(2)}, u32[]{:S(2)}) async-start(bf16[64,16,256]{2,1,0:T(8,128)(2,1)} %copy.34), calls=%async_computation.6 | async-start | bytes 1048576 | tf_op jit(solution)/shard_map/all_to_all | solution.py:370
  203.8 0.0 copy-done.1
  203.8 0.8 reduce.5
  204.6 15.9 %all-to-all-done.6 = bf16[64,16,256]{2,1,0:T(8,128)(2,1)S(1)} async-done(((bf16[64,16,256]{2,1,0:T(8,128)(2,1)}), bf16[64,16,256]{2,1,0:T(8,128)(2,1)S(1)}, u32[]{:S(2)}, u32[]{:S(2)}) %all-to-all-start.6) | async-done | bytes 524320 | tf_op jit(solution)/shard_map/all_to_all | solution.py:370
  220.5 1.3 convolution_bitcast_fusion.x_ref
  221.8 21.3 %shard_map.79 = f32[4,128,256]{2,1,0:T(8,128)} custom-call(f32[512,256]{1,0:T(8,128)} %convolution_bitcast_fusion.x_ref), custom_call_target="tpu_custom_call" | custom-call | tf_op jit(solution)/shard_map/pallas_call | solution.py:229
  243.1 1.9 broadcast_multiply_fusion
  (8 shorter events, 0.1 us)
Async XLA Ops:
  0.6 1.2 copy-start
  0.6 48.3 %copy-start.2 = (s32[1,16,4]{1,2,0:T(4,128)S(1)}, s32[1,16,4]{1,2,0:T(4,128)}, u32[]{:S(2)}) copy-start(s32[1,16,4]{1,2,0:T(4,128)} %param.11) | copy-start | bytes 772
  42.1 24.6 %all-to-all-start = ((bf16[8,1,128,256]{3,2,1,0:T(8,128)(2,1)}), bf16[8,1,128,256]{3,2,1,0:T(8,128)(2,1)S(1)}, u32[]{:S(2)}, u32[]{:S(2)}) async-start(bf16[8,1,128,256]{3,2,1,0:T(8,128)(2,1)} %broadcast_in_dim.10), calls=%async_computation | async-start | bytes 1048576 | tf_op jit(solution)/shard_map/all_to_all | solution.py:346
  68.3 28.9 %all-to-all-start.1 = ((bf16[4,8,128,256]{3,2,1,0:T(8,128)(2,1)}), bf16[4,8,128,256]{3,2,1,0:T(8,128)(2,1)S(1)}, u32[]{:S(2)}, u32[]{:S(2)}) async-start(bf16[4,8,128,256]{3,2,1,0:T(8,128)(2,1)} %broadcast_in_dim.12), calls=%async_computation.1 | async-start | bytes 4194304 | tf_op jit(solution)/shard_map/all_to_all | solution.py:346
  73.6 1.3 copy-start.3
  174.1 29.7 %copy-start.1 = (f32[16,64,1]{2,1,0:T(8,128)S(1)}, f32[16,64,1]{2,1,0:T(8,128)}, u32[]{:S(2)}) copy-start(f32[16,64,1]{2,1,0:T(8,128)} %get-tuple-element.5) | copy-start | bytes 12292
  197.3 23.2 %all-to-all-start.6 = ((bf16[64,16,256]{2,1,0:T(8,128)(2,1)}), bf16[64,16,256]{2,1,0:T(8,128)(2,1)S(1)}, u32[]{:S(2)}, u32[]{:S(2)}) async-start(bf16[64,16,256]{2,1,0:T(8,128)(2,1)} %copy.34), calls=%async_computation.6 | async-start | bytes 1048576 | tf_op jit(solution)/shard_map/all_to_all | solution.py:370

commit v13 on v12

--- a/solution.py
+++ b/solution.py
@@ -173,6 +173,52 @@
     return weights.reshape(count, picks * NS), contrib
 
 
+def _pair_sum_kernel(x_ref, o_ref, own, recv, send_sem, recv_sem, local_sem):
+    half = own.shape[0]
+    me = lax.axis_index(SLAB[2])
+    mate = 1 - me
+    where = (lax.axis_index(SLAB[0]), lax.axis_index(SLAB[1]), mate, lax.axis_index("img"))
+    mesh_ids = pl.DeviceIdType.MESH
+    barrier = pltpu.get_barrier_semaphore()
+    pl.semaphore_signal(barrier, inc=1, device_id=where, device_id_type=mesh_ids)
+    pl.semaphore_wait(barrier, 1)
+    local = pltpu.make_async_copy(x_ref.at[pl.ds(me * half, half)], own, local_sem)
+    local.start()
+    copy = pltpu.make_async_remote_copy(
+        src_ref=x_ref.at[pl.ds(mate * half, half)], dst_ref=recv, send_sem=send_sem,
+        recv_sem=recv_sem, device_id=where, device_id_type=mesh_ids,
+    )
+    copy.start()
+    local.wait()
+    copy.wait()
+
+    def add(b, carry):
+        o_ref[b] = (own[b].astype(jnp.float32) + recv[b].astype(jnp.float32)).astype(o_ref.dtype)
+        return carry
+
+    lax.fori_loop(0, half, add, 0)
+
+
+def pair_sum(x, cid):
+    half = x.shape[0] // 2
+    return pl.pallas_call(
+        _pair_sum_kernel,
+        out_shape=jax.ShapeDtypeStruct((half,) + x.shape[1:], x.dtype),
+        in_specs=[pl.BlockSpec(memory_space=pl.ANY)],
+        out_specs=pl.BlockSpec(memory_space=pltpu.VMEM),
+        scratch_shapes=[
+            pltpu.VMEM((half,) + x.shape[1:], x.dtype),
+            pltpu.VMEM((half,) + x.shape[1:], x.dtype),
+            pltpu.SemaphoreType.DMA,
+            pltpu.SemaphoreType.DMA,
+            pltpu.SemaphoreType.DMA,
+        ],
+        compiler_params=pltpu.CompilerParams(
+            collective_id=cid, has_side_effects=True, vmem_limit_bytes=48 * 1024 * 1024
+        ),
+    )(x)
+
+
 def _img_sum_kernel(x_ref, o_ref, gat, qbuf, s1, r1, s2, r2, l1, l2):
     count, rows = gat.shape[0], gat.shape[1]
     me = lax.axis_index("img")
@@ -352,7 +398,8 @@
         (sizes[2], sizes[0], sizes[1], ori_dev)
     ).transpose(1, 2, 0, 3).reshape(-1)
     weights, contrib = correlate_all(panels, images[0], orient[0], inv_perm[orient[0]], defocus[0])
-    for axis in (SLAB[2], SLAB[0], SLAB[1]):
+    contrib = pair_sum(contrib, 2)
+    for axis in (SLAB[0], SLAB[1]):
         parts = lax.axis_size(axis)
         moved = lax.all_to_all(
             contrib.astype(jnp.bfloat16), axis, split_axis=0, concat_axis=0, tiled=True

time: 246 us -> 235 us (0.955)
  blocking collectives: 69.8 us -> 58.3 us
  Pallas kernels: 78.1 us -> 83.3 us
  other arithmetic: 16.2 us -> 12.2 us
    all_to_all x3 -> x2, blocking collectives: 61.6 us -> 50.1 us  [on_device(): lax.all_to_all(contrib.astype(jnp.bfloat16), axis, split_axis=0, concat_a...]
    pallas_call x0 -> x1, Pallas kernels: none -> 5 us  [pair_sum(): pl.pallas_call(_pair_sum_kernel, out_shape=jax.ShapeDtypeStruct((half,) +...]
    reduce_sum x3 -> x2, other arithmetic: 5.41 us -> 1.34 us  [on_device(): jnp.sum(moved.astype(jnp.float32).reshape((parts, -1) + moved.shape[1:]),...]
where the time goes in v13:
time: 235 us
  Pallas kernels  83.3 us (35%)
  blocking collectives  58.3 us (25%)
  waiting for transfers between devices  47.7 us (20%)
  starting transfers between devices  17.8 us (8%)
  other arithmetic  12.2 us (5%)
  local copies, waits for them, and re-layouts  8.36 us (4%)
  matrix products  6.22 us (3%)
    all_to_all x2, blocking collectives, on_device(): lax.all_to_all(contrib.astype(jnp.bfloat16), axis, split_axis=0, concat_a...  50.1 us
    pallas_call x1, Pallas kernels, slab_all_to_all(): pl.pallas_call(_a2a_kernel, out_shape=jax.ShapeDtypeStruct(x.shape, x.dty...  34.2 us
    all_to_all x2, waiting for transfers between devices, on_device(): lax.all_to_all(jnp.broadcast_to(panels[None], (parts,) + panels.shape), a...  31.8 us
    pallas_call x1, Pallas kernels, correlate_all(): pl.pallas_call(_correlate_kernel, grid_spec=grid_spec, out_shape=[jax.Sha...  22.7 us
    pallas_call x1, Pallas kernels, img_sum(): pl.pallas_call(_img_sum_kernel, out_shape=jax.ShapeDtypeStruct((count, ro...  21.3 us
    all_to_all x1, waiting for transfers between devices, on_device(): lax.all_to_all(outgoing, SLAB, split_axis=0, concat_axis=0, tiled=True)  15.9 us
    all_to_all x2, starting transfers between devices, on_device(): lax.all_to_all(jnp.broadcast_to(panels[None], (parts,) + panels.shape), a...  11.4 us
    all_to_all x1, blocking collectives, on_device(): lax.all_to_all(jnp.broadcast_to(panels[None], (parts,) + panels.shape), a...  8.18 us
  transfers between devices with their start and end apart: 3, of which 3 were waited for; matrix products, arithmetic and copies ran while one was open for 5% of the time, Pallas kernels for 0%

profile of v13, /device:TPU:6, one launch (start us, length us, event | category | flops | bytes accessed | tf_op | source)
XLA Modules:
  0.0 234.6 jit_solution(4407358222815076302)
XLA Ops:
  0.6 0.0 copy-start
  0.7 1.2 copy-done
  1.9 2.3 %fusion.2.x_ref = f32[64,16,256]{2,1,0:T(8,128)} fusion(bf16[1,64,16,512]{3,2,1,0:T(8,128)(2,1)S(1)} %copy-done, bf16[512,256]{1,0:T(8,128)(2,1)} %param.6), kind=kOutput, calls=%fused_computation.6 | convolution fusion | flops 268435456 | bytes 2359296 | tf_op jit(solution)/shard_map/jpr,rx->jpx/dot_general | solution.py:379
  4.2 0.0 copy-start.2
  4.2 34.2 %shard_map.77 = f32[64,16,256]{2,1,0:T(8,128)} custom-call(f32[64,16,256]{2,1,0:T(8,128)} %fusion.2.x_ref), custom_call_target="tpu_custom_call" | custom-call | tf_op jit(solution)/shard_map/pallas_call | solution.py:354
  38.5 0.7 dynamic-slice_bitcast_fusion
  39.2 2.2 convolution_convert_fusion.1
  41.4 0.8 broadcast_in_dim.10
  42.2 6.9 %all-to-all-start = ((bf16[8,1,128,256]{3,2,1,0:T(8,128)(2,1)}), bf16[8,1,128,256]{3,2,1,0:T(8,128)(2,1)S(1)}, u32[]{:S(2)}, u32[]{:S(2)}) async-start(bf16[8,1,128,256]{3,2,1,0:T(8,128)(2,1)} %broadcast_in_dim.10), calls=%async_computation | async-start | bytes 1048576 | tf_op jit(solution)/shard_map/all_to_all | solution.py:392
  49.1 0.0 copy-done.2
  49.1 0.1 copy.30
  49.2 0.1 reshape.395
  49.3 17.6 %all-to-all-done = bf16[8,1,128,256]{3,2,1,0:T(8,128)(2,1)S(1)} async-done(((bf16[8,1,128,256]{3,2,1,0:T(8,128)(2,1)}), bf16[8,1,128,256]{3,2,1,0:T(8,128)(2,1)S(1)}, u32[]{:S(2)}, u32[]{:S(2)}) %all-to-all-start) | async-done | bytes 524320 | tf_op jit(solution)/shard_map/all_to_all | solution.py:392
  66.9 1.6 broadcast_in_dim.12
  68.5 4.5 %all-to-all-start.1 = ((bf16[4,8,128,256]{3,2,1,0:T(8,128)(2,1)}), bf16[4,8,128,256]{3,2,1,0:T(8,128)(2,1)S(1)}, u32[]{:S(2)}, u32[]{:S(2)}) async-start(bf16[4,8,128,256]{3,2,1,0:T(8,128)(2,1)} %broadcast_in_dim.12), calls=%async_computation.1 | async-start | bytes 4194304 | tf_op jit(solution)/shard_map/all_to_all | solution.py:392
  73.0 0.1 copy.29
  73.0 0.6 reshape_squeeze.3.orient_ref
  73.6 0.1 reshape.387
  73.8 0.0 copy-start.3
  73.8 1.3 gather_fusion
  75.1 0.0 copy-done.3
  75.1 0.1 broadcast_multiply_fusion.2
  75.2 0.1 add_multiply_fusion.2
  75.2 3.1 %fusion.6 = (f32[8,128,128]{2,1,0:T(8,128)}, f32[8,128,128]{2,1,0:T(8,128)}) fusion(f32[8,128]{1,0:T(8,128)S(1)} %get-tuple-element.9, f32[8,128]{1,0:T(8,128)S(1)} %get-tuple-element.8), kind=kLoop, calls=%fused_computation.14 | loop fusion | flops 786432 | bytes 1056768 | tf_op jit(solution)/shard_map/convert_element_type | solution.py:145
  78.3 4.9 %add_negate_fusion.ctf_ref = f32[16,128,128]{2,1,0:T(8,128)} fusion(f32[128,128]{1,0:T(8,128)S(1)} %get-tuple-element.11, f32[128,128]{1,0:T(8,128)S(1)} %get-tuple-element.10, f32[16]{0:T(128)S(1)} %multiply_bitcast_fusion), kind=kLoop, calls=%fused_computation.9 | loop fusion | flops 1572864 | bytes 1179712 | tf_op jit(solution)/shard_map/neg | solution.py:41
  83.2 14.2 %all-to-all-done.1 = bf16[4,8,128,256]{3,2,1,0:T(8,128)(2,1)S(1)} async-done(((bf16[4,8,128,256]{3,2,1,0:T(8,128)(2,1)}), bf16[4,8,128,256]{3,2,1,0:T(8,128)(2,1)S(1)}, u32[]{:S(2)}, u32[]{:S(2)}) %all-to-all-start.1) | async-done | bytes 2097184 | tf_op jit(solution)/shard_map/all_to_all | solution.py:392
  97.4 0.7 broadcast_in_dim.14
  98.1 8.2 %all_to_all.30 = bf16[2,32,128,256]{3,2,1,0:T(8,128)(2,1)} all-to-all(bf16[2,32,128,256]{3,2,1,0:T(8,128)(2,1)S(1)} %broadcast_in_dim.14), channel_id=1, replica_groups=mesh['sx'=4,'sz'=8,'sc'=2,'img'=4] {'sc'}, dimensions={0} | all-to-all | bytes 8388608 | tf_op jit(solution)/shard_map/all_to_all | solution.py:392
  106.3 22.7 %shard_map.78 = (f32[16,64,1]{2,1,0:T(8,128)}, bf16[64,128,256]{2,1,0:T(8,128)(2,1)}) custom-call(s32[64]{0:T(128)} %reshape_squeeze.3.orient_ref, s32[64]{0:T(128)} %gather_fusion, bf16[64,128,256]{2,1,0:T(8,128)(2,1)} %bitcast.50, bf16[16,128,256]{2,1,0:T(8,128)(2,1)} %bitcast.54, f32[16,128,128]{2,1,0:T(8,128)} %add_negate_fusion.ctf_ref, ...), custom_call_target="tpu_custom_call" | custom-call | tf_op jit(solution)/shard_map/pallas_call | solution.py:162
  129.0 5.0 %shard_map.79 = bf16[32,128,256]{2,1,0:T(8,128)(2,1)S(1)} custom-call(bf16[64,128,256]{2,1,0:T(8,128)(2,1)} %get-tuple-element.4.x_ref), custom_call_target="tpu_custom_call" | custom-call | tf_op jit(solution)/shard_map/pallas_call | solution.py:204
  134.0 29.4 %all_to_all.31 = bf16[32,128,256]{2,1,0:T(8,128)(2,1)S(1)} all-to-all(bf16[32,128,256]{2,1,0:T(8,128)(2,1)S(1)} %shard_map.79), channel_id=1, replica_groups=mesh['sx'=4,'sz'=8,'sc'=2,'img'=4] {'sx'}, dimensions={0} | all-to-all | bytes 4194304 | tf_op jit(solution)/shard_map/all_to_all | solution.py:404
  163.4 1.3 reduce.3
  164.6 0.0 copy-start.1
  164.6 20.8 %all_to_all.32 = bf16[8,128,256]{2,1,0:T(8,128)(2,1)S(1)} all-to-all(bf16[8,128,256]{2,1,0:T(8,128)(2,1)} %reduce.3), channel_id=1, replica_groups=mesh['sx'=4,'sz'=8,'sc'=2,'img'=4] {'sz'}, dimensions={0} | all-to-all | bytes 1048576 | tf_op jit(solution)/shard_map/all_to_all | solution.py:404
  185.4 0.1 reduce_sum.22
  185.5 0.3 fusion
  185.8 1.1 copy.34
  186.9 6.5 %all-to-all-start.5 = ((bf16[64,16,256]{2,1,0:T(8,128)(2,1)}), bf16[64,16,256]{2,1,0:T(8,128)(2,1)S(1)}, u32[]{:S(2)}, u32[]{:S(2)}) async-start(bf16[64,16,256]{2,1,0:T(8,128)(2,1)} %copy.34), calls=%async_computation.5 | async-start | bytes 1048576 | tf_op jit(solution)/shard_map/all_to_all | solution.py:417
  193.4 0.0 copy-done.1
  193.4 0.8 reduce.4
  194.2 15.9 %all-to-all-done.5 = bf16[64,16,256]{2,1,0:T(8,128)(2,1)S(1)} async-done(((bf16[64,16,256]{2,1,0:T(8,128)(2,1)}), bf16[64,16,256]{2,1,0:T(8,128)(2,1)S(1)}, u32[]{:S(2)}, u32[]{:S(2)}) %all-to-all-start.5) | async-done | bytes 524320 | tf_op jit(solution)/shard_map/all_to_all | solution.py:417
  210.1 1.3 convolution_bitcast_fusion.x_ref
  211.4 21.3 %shard_map.80 = f32[4,128,256]{2,1,0:T(8,128)} custom-call(f32[512,256]{1,0:T(8,128)} %convolution_bitcast_fusion.x_ref), custom_call_target="tpu_custom_call" | custom-call | tf_op jit(solution)/shard_map/pallas_call | solution.py:275
  232.7 1.9 broadcast_multiply_fusion
  (8 shorter events, 0.1 us)
Async XLA Ops:
  0.6 1.2 copy-start
  4.2 44.9 %copy-start.2 = (s32[1,16,4]{1,2,0:T(4,128)S(1)}, s32[1,16,4]{1,2,0:T(4,128)}, u32[]{:S(2)}) copy-start(s32[1,16,4]{1,2,0:T(4,128)} %param.11) | copy-start | bytes 772
  42.2 24.6 %all-to-all-start = ((bf16[8,1,128,256]{3,2,1,0:T(8,128)(2,1)}), bf16[8,1,128,256]{3,2,1,0:T(8,128)(2,1)S(1)}, u32[]{:S(2)}, u32[]{:S(2)}) async-start(bf16[8,1,128,256]{3,2,1,0:T(8,128)(2,1)} %broadcast_in_dim.10), calls=%async_computation | async-start | bytes 1048576 | tf_op jit(solution)/shard_map/all_to_all | solution.py:392
  68.5 28.9 %all-to-all-start.1 = ((bf16[4,8,128,256]{3,2,1,0:T(8,128)(2,1)}), bf16[4,8,128,256]{3,2,1,0:T(8,128)(2,1)S(1)}, u32[]{:S(2)}, u32[]{:S(2)}) async-start(bf16[4,8,128,256]{3,2,1,0:T(8,128)(2,1)} %broadcast_in_dim.12), calls=%async_computation.1 | async-start | bytes 4194304 | tf_op jit(solution)/shard_map/all_to_all | solution.py:392
  73.8 1.3 copy-start.3
  164.6 28.8 %copy-start.1 = (f32[16,64,1]{2,1,0:T(8,128)S(1)}, f32[16,64,1]{2,1,0:T(8,128)}, u32[]{:S(2)}) copy-start(f32[16,64,1]{2,1,0:T(8,128)} %get-tuple-element.5) | copy-start | bytes 12292
  186.9 23.2 %all-to-all-start.5 = ((bf16[64,16,256]{2,1,0:T(8,128)(2,1)}), bf16[64,16,256]{2,1,0:T(8,128)(2,1)S(1)}, u32[]{:S(2)}, u32[]{:S(2)}) async-start(bf16[64,16,256]{2,1,0:T(8,128)(2,1)} %copy.34), calls=%async_computation.5 | async-start | bytes 1048576 | tf_op jit(solution)/shard_map/all_to_all | solution.py:417

commit v14 on v13

--- a/solution.py
+++ b/solution.py
@@ -1,3 +1,4 @@
+import functools
 import math
 
 import jax
@@ -219,6 +220,74 @@
     )(x)
 
 
+def _axis_sum_kernel(axis, x_ref, o_ref, got, send_sems, recv_sems, local_sem):
+    count, chunk = got.shape[0], got.shape[1]
+    me = lax.axis_index(axis)
+    names = SLAB + ("img",)
+    coords = [lax.axis_index(a) for a in names]
+    at = names.index(axis)
+    mesh_ids = pl.DeviceIdType.MESH
+    peers = [lax.rem(me + 1 + i, count) for i in range(count - 1)]
+
+    def where(peer):
+        return tuple(coords[:at]) + (peer,) + tuple(coords[at + 1:])
+
+    barrier = pltpu.get_barrier_semaphore()
+    for peer in peers:
+        pl.semaphore_signal(barrier, inc=1, device_id=where(peer), device_id_type=mesh_ids)
+    pl.semaphore_wait(barrier, count - 1)
+
+    def part(p):
+        return x_ref.at[pl.ds(p * chunk, chunk)]
+
+    local = pltpu.make_async_copy(part(me), got.at[me], local_sem)
+    local.start()
+    sends = []
+    for i, peer in enumerate(peers):
+        copy = pltpu.make_async_remote_copy(
+            src_ref=part(peer), dst_ref=got.at[me], send_sem=send_sems.at[i], recv_sem=recv_sems.at[me],
+            device_id=where(peer), device_id_type=mesh_ids,
+        )
+        copy.start()
+        sends.append(copy)
+    for i, peer in enumerate(peers):
+        sends[i].wait_send()
+        pltpu.make_async_remote_copy(
+            src_ref=part(peer), dst_ref=got.at[peer], send_sem=send_sems.at[i], recv_sem=recv_sems.at[peer],
+            device_id=where(peer), device_id_type=mesh_ids,
+        ).wait_recv()
+    local.wait()
+
+    def add(b, carry):
+        total = got[0, b].astype(jnp.float32)
+        for p in range(1, count):
+            total = total + got[p, b].astype(jnp.float32)
+        o_ref[b] = total.astype(o_ref.dtype)
+        return carry
+
+    lax.fori_loop(0, chunk, add, 0)
+
+
+def axis_sum(x, axis, cid):
+    count = lax.axis_size(axis)
+    chunk = x.shape[0] // count
+    return pl.pallas_call(
+        functools.partial(_axis_sum_kernel, axis),
+        out_shape=jax.ShapeDtypeStruct((chunk,) + x.shape[1:], x.dtype),
+        in_specs=[pl.BlockSpec(memory_space=pl.ANY)],
+        out_specs=pl.BlockSpec(memory_space=pltpu.VMEM),
+        scratch_shapes=[
+            pltpu.VMEM((count, chunk) + x.shape[1:], x.dtype),
+            pltpu.SemaphoreType.DMA((count,)),
+            pltpu.SemaphoreType.DMA((count,)),
+            pltpu.SemaphoreType.DMA,
+        ],
+        compiler_params=pltpu.CompilerParams(
+            collective_id=cid, has_side_effects=True, vmem_limit_bytes=48 * 1024 * 1024
+        ),
+    )(x)
+
+
 def _img_sum_kernel(x_ref, o_ref, gat, qbuf, s1, r1, s2, r2, l1, l2):
     count, rows = gat.shape[0], gat.shape[1]
     me = lax.axis_index("img")
@@ -399,15 +468,8 @@
     ).transpose(1, 2, 0, 3).reshape(-1)
     weights, contrib = correlate_all(panels, images[0], orient[0], inv_perm[orient[0]], defocus[0])
     contrib = pair_sum(contrib, 2)
-    for axis in (SLAB[0], SLAB[1]):
-        parts = lax.axis_size(axis)
-        moved = lax.all_to_all(
-            contrib.astype(jnp.bfloat16), axis, split_axis=0, concat_axis=0, tiled=True
-        )
-        contrib = jnp.sum(
-            moved.astype(jnp.float32).reshape((parts, -1) + moved.shape[1:]), axis=0
-        )
-    back_own = contrib.astype(jnp.bfloat16)
+    contrib = axis_sum(contrib, SLAB[0], 3)
+    back_own = axis_sum(contrib, SLAB[1], 4)
     back_own = back_own.reshape(ori_dev, block_count, block_rows, 2 * fourier)
     chosen_back = (owned_idx[:, :, None] == levels).astype(jnp.bfloat16)
     outgoing = jnp.einsum(

time: 235 us -> 228 us (0.970)
  blocking collectives: 58.3 us -> 8.15 us
  Pallas kernels: 83.3 us -> 128 us
    all_to_all x2 -> x0, blocking collectives: 50.1 us -> none  [on_device(): lax.all_to_all(contrib.astype(jnp.bfloat16), axis, split_axis=0, concat_a...]
    pallas_call x0 -> x2, Pallas kernels: none -> 45 us  [axis_sum(): pl.pallas_call(functools.partial(_axis_sum_kernel, axis), out_shape=jax.S...]
where the time goes in v14:
time: 228 us
  Pallas kernels  128 us (56%)
  waiting for transfers between devices  47.6 us (21%)
  starting transfers between devices  17.7 us (8%)
  other arithmetic  10.8 us (5%)
  local copies, waits for them, and re-layouts  8.36 us (4%)
  blocking collectives  8.15 us (4%)
  matrix products  6.23 us (3%)
    pallas_call x2, Pallas kernels, axis_sum(): pl.pallas_call(functools.partial(_axis_sum_kernel, axis), out_shape=jax.S...  45 us
    pallas_call x1, Pallas kernels, slab_all_to_all(): pl.pallas_call(_a2a_kernel, out_shape=jax.ShapeDtypeStruct(x.shape, x.dty...  34.1 us
    all_to_all x2, waiting for transfers between devices, on_device(): lax.all_to_all(jnp.broadcast_to(panels[None], (parts,) + panels.shape), a...  31.8 us
    pallas_call x1, Pallas kernels, correlate_all(): pl.pallas_call(_correlate_kernel, grid_spec=grid_spec, out_shape=[jax.Sha...  22.7 us
    pallas_call x1, Pallas kernels, img_sum(): pl.pallas_call(_img_sum_kernel, out_shape=jax.ShapeDtypeStruct((count, ro...  21.3 us
    all_to_all x1, waiting for transfers between devices, on_device(): lax.all_to_all(outgoing, SLAB, split_axis=0, concat_axis=0, tiled=True)  15.9 us
    all_to_all x2, starting transfers between devices, on_device(): lax.all_to_all(jnp.broadcast_to(panels[None], (parts,) + panels.shape), a...  11.4 us
    all_to_all x1, blocking collectives, on_device(): lax.all_to_all(jnp.broadcast_to(panels[None], (parts,) + panels.shape), a...  8.15 us
  transfers between devices with their start and end apart: 3, of which 3 were waited for; matrix products, arithmetic and copies ran while one was open for 5% of the time, Pallas kernels for 0%

profile of v14, /device:TPU:6, one launch (start us, length us, event | category | flops | bytes accessed | tf_op | source)
XLA Modules:
  0.0 227.8 jit_solution(11147848211784398762)
XLA Ops:
  0.6 0.0 copy-start
  0.6 0.0 copy-start.2
  0.7 1.2 copy-done
  1.9 2.4 %fusion.2.x_ref = f32[64,16,256]{2,1,0:T(8,128)} fusion(bf16[1,64,16,512]{3,2,1,0:T(8,128)(2,1)S(1)} %copy-done, bf16[512,256]{1,0:T(8,128)(2,1)} %param.6), kind=kOutput, calls=%fused_computation.6 | convolution fusion | flops 268435456 | bytes 2359296 | tf_op jit(solution)/shard_map/jpr,rx->jpx/dot_general | solution.py:448
  4.2 34.1 %shard_map.77 = f32[64,16,256]{2,1,0:T(8,128)} custom-call(f32[64,16,256]{2,1,0:T(8,128)} %fusion.2.x_ref), custom_call_target="tpu_custom_call" | custom-call | tf_op jit(solution)/shard_map/pallas_call | solution.py:423
  38.3 0.7 dynamic-slice_bitcast_fusion
  39.0 2.2 convolution_convert_fusion.1
  41.3 0.8 broadcast_in_dim.10
  42.1 6.9 %all-to-all-start = ((bf16[8,1,128,256]{3,2,1,0:T(8,128)(2,1)}), bf16[8,1,128,256]{3,2,1,0:T(8,128)(2,1)S(1)}, u32[]{:S(2)}, u32[]{:S(2)}) async-start(bf16[8,1,128,256]{3,2,1,0:T(8,128)(2,1)} %broadcast_in_dim.10), calls=%async_computation | async-start | bytes 1048576 | tf_op jit(solution)/shard_map/all_to_all | solution.py:461
  49.0 0.0 copy-done.2
  49.0 0.1 copy.22
  49.1 0.1 reshape.380
  49.2 17.6 %all-to-all-done = bf16[8,1,128,256]{3,2,1,0:T(8,128)(2,1)S(1)} async-done(((bf16[8,1,128,256]{3,2,1,0:T(8,128)(2,1)}), bf16[8,1,128,256]{3,2,1,0:T(8,128)(2,1)S(1)}, u32[]{:S(2)}, u32[]{:S(2)}) %all-to-all-start) | async-done | bytes 524320 | tf_op jit(solution)/shard_map/all_to_all | solution.py:461
  66.7 1.6 broadcast_in_dim.12
  68.3 4.5 %all-to-all-start.1 = ((bf16[4,8,128,256]{3,2,1,0:T(8,128)(2,1)}), bf16[4,8,128,256]{3,2,1,0:T(8,128)(2,1)S(1)}, u32[]{:S(2)}, u32[]{:S(2)}) async-start(bf16[4,8,128,256]{3,2,1,0:T(8,128)(2,1)} %broadcast_in_dim.12), calls=%async_computation.1 | async-start | bytes 4194304 | tf_op jit(solution)/shard_map/all_to_all | solution.py:461
  72.8 0.1 copy.21
  72.9 0.6 reshape_squeeze.3.orient_ref
  73.5 0.1 reshape.373
  73.6 0.0 copy-start.3
  73.6 1.3 gather_fusion
  75.0 0.0 copy-done.3
  75.0 0.1 broadcast_multiply_fusion.2
  75.0 0.1 add_multiply_fusion.2
  75.1 3.1 %fusion.6 = (f32[8,128,128]{2,1,0:T(8,128)}, f32[8,128,128]{2,1,0:T(8,128)}) fusion(f32[8,128]{1,0:T(8,128)S(1)} %get-tuple-element.9, f32[8,128]{1,0:T(8,128)S(1)} %get-tuple-element.8), kind=kLoop, calls=%fused_computation.14 | loop fusion | flops 786432 | bytes 1056768 | tf_op jit(solution)/shard_map/convert_element_type | solution.py:146
  78.2 4.9 %add_negate_fusion.ctf_ref = f32[16,128,128]{2,1,0:T(8,128)} fusion(f32[128,128]{1,0:T(8,128)S(1)} %get-tuple-element.11, f32[128,128]{1,0:T(8,128)S(1)} %get-tuple-element.10, f32[16]{0:T(128)S(1)} %multiply_bitcast_fusion), kind=kLoop, calls=%fused_computation.9 | loop fusion | flops 1572864 | bytes 1179712 | tf_op jit(solution)/shard_map/neg | solution.py:42
  83.1 14.2 %all-to-all-done.1 = bf16[4,8,128,256]{3,2,1,0:T(8,128)(2,1)S(1)} async-done(((bf16[4,8,128,256]{3,2,1,0:T(8,128)(2,1)}), bf16[4,8,128,256]{3,2,1,0:T(8,128)(2,1)S(1)}, u32[]{:S(2)}, u32[]{:S(2)}) %all-to-all-start.1) | async-done | bytes 2097184 | tf_op jit(solution)/shard_map/all_to_all | solution.py:461
  97.3 0.7 broadcast_in_dim.14
  98.0 8.2 %all_to_all.20 = bf16[2,32,128,256]{3,2,1,0:T(8,128)(2,1)} all-to-all(bf16[2,32,128,256]{3,2,1,0:T(8,128)(2,1)S(1)} %broadcast_in_dim.14), channel_id=1, replica_groups=mesh['sx'=4,'sz'=8,'sc'=2,'img'=4] {'sc'}, dimensions={0} | all-to-all | bytes 8388608 | tf_op jit(solution)/shard_map/all_to_all | solution.py:461
  106.1 22.7 %shard_map.78 = (f32[16,64,1]{2,1,0:T(8,128)}, bf16[64,128,256]{2,1,0:T(8,128)(2,1)}) custom-call(s32[64]{0:T(128)} %reshape_squeeze.3.orient_ref, s32[64]{0:T(128)} %gather_fusion, bf16[64,128,256]{2,1,0:T(8,128)(2,1)} %bitcast.50, bf16[16,128,256]{2,1,0:T(8,128)(2,1)} %bitcast.53, f32[16,128,128]{2,1,0:T(8,128)} %add_negate_fusion.ctf_ref, ...), custom_call_target="tpu_custom_call" | custom-call | tf_op jit(solution)/shard_map/pallas_call | solution.py:163
  128.8 5.0 %shard_map.79.x_ref = bf16[32,128,256]{2,1,0:T(8,128)(2,1)S(1)} custom-call(bf16[64,128,256]{2,1,0:T(8,128)(2,1)} %get-tuple-element.4.x_ref), custom_call_target="tpu_custom_call" | custom-call | tf_op jit(solution)/shard_map/pallas_call | solution.py:205
  133.8 0.0 copy-start.1
  133.8 27.0 %shard_map.80.x_ref = bf16[8,128,256]{2,1,0:T(8,128)(2,1)S(1)} custom-call(bf16[32,128,256]{2,1,0:T(8,128)(2,1)S(1)} %shard_map.79.x_ref), custom_call_target="tpu_custom_call" | custom-call | tf_op jit(solution)/shard_map/pallas_call | solution.py:274
  160.8 18.0 %shard_map.81 = bf16[1,128,256]{2,1,0:T(8,128)(2,1)S(1)} custom-call(bf16[8,128,256]{2,1,0:T(8,128)(2,1)S(1)} %shard_map.80.x_ref), custom_call_target="tpu_custom_call" | custom-call | tf_op jit(solution)/shard_map/pallas_call | solution.py:274
  178.8 0.3 fusion
  179.2 1.1 copy.26
  180.2 6.3 %all-to-all-start.3 = ((bf16[64,16,256]{2,1,0:T(8,128)(2,1)}), bf16[64,16,256]{2,1,0:T(8,128)(2,1)S(1)}, u32[]{:S(2)}, u32[]{:S(2)}) async-start(bf16[64,16,256]{2,1,0:T(8,128)(2,1)} %copy.26), calls=%async_computation.3 | async-start | bytes 1048576 | tf_op jit(solution)/shard_map/all_to_all | solution.py:479
  186.6 0.0 copy-done.1
  186.6 0.8 reduce
  187.4 15.9 %all-to-all-done.3 = bf16[64,16,256]{2,1,0:T(8,128)(2,1)S(1)} async-done(((bf16[64,16,256]{2,1,0:T(8,128)(2,1)}), bf16[64,16,256]{2,1,0:T(8,128)(2,1)S(1)}, u32[]{:S(2)}, u32[]{:S(2)}) %all-to-all-start.3) | async-done | bytes 524320 | tf_op jit(solution)/shard_map/all_to_all | solution.py:479
  203.3 1.3 convolution_bitcast_fusion.x_ref
  204.6 21.3 %shard_map.82 = f32[4,128,256]{2,1,0:T(8,128)} custom-call(f32[512,256]{1,0:T(8,128)} %convolution_bitcast_fusion.x_ref), custom_call_target="tpu_custom_call" | custom-call | tf_op jit(solution)/shard_map/pallas_call | solution.py:344
  225.9 1.9 broadcast_multiply_fusion
  (8 shorter events, 0.1 us)
Async XLA Ops:
  0.6 1.2 copy-start
  0.6 48.3 %copy-start.2 = (s32[1,16,4]{1,2,0:T(4,128)S(1)}, s32[1,16,4]{1,2,0:T(4,128)}, u32[]{:S(2)}) copy-start(s32[1,16,4]{1,2,0:T(4,128)} %param.11) | copy-start | bytes 772
  42.1 24.6 %all-to-all-start = ((bf16[8,1,128,256]{3,2,1,0:T(8,128)(2,1)}), bf16[8,1,128,256]{3,2,1,0:T(8,128)(2,1)S(1)}, u32[]{:S(2)}, u32[]{:S(2)}) async-start(bf16[8,1,128,256]{3,2,1,0:T(8,128)(2,1)} %broadcast_in_dim.10), calls=%async_computation | async-start | bytes 1048576 | tf_op jit(solution)/shard_map/all_to_all | solution.py:461
  68.3 28.9 %all-to-all-start.1 = ((bf16[4,8,128,256]{3,2,1,0:T(8,128)(2,1)}), bf16[4,8,128,256]{3,2,1,0:T(8,128)(2,1)S(1)}, u32[]{:S(2)}, u32[]{:S(2)}) async-start(bf16[4,8,128,256]{3,2,1,0:T(8,128)(2,1)} %broadcast_in_dim.12), calls=%async_computation.1 | async-start | bytes 4194304 | tf_op jit(solution)/shard_map/all_to_all | solution.py:461
  73.6 1.3 copy-start.3
  133.8 52.7 %copy-start.1 = (f32[16,64,1]{2,1,0:T(8,128)S(1)}, f32[16,64,1]{2,1,0:T(8,128)}, u32[]{:S(2)}) copy-start(f32[16,64,1]{2,1,0:T(8,128)} %get-tuple-element.5) | copy-start | bytes 12292
  180.2 23.0 %all-to-all-start.3 = ((bf16[64,16,256]{2,1,0:T(8,128)(2,1)}), bf16[64,16,256]{2,1,0:T(8,128)(2,1)S(1)}, u32[]{:S(2)}, u32[]{:S(2)}) async-start(bf16[64,16,256]{2,1,0:T(8,128)(2,1)} %copy.26), calls=%async_computation.3 | async-start | bytes 1048576 | tf_op jit(solution)/shard_map/all_to_all | solution.py:479

commit v15 on v14

--- a/solution.py
+++ b/solution.py
@@ -288,6 +288,58 @@
     )(x)
 
 
+def _axis_gather_kernel(axis, x_ref, o_ref, send_sems, recv_sems, local_sem):
+    count = o_ref.shape[0]
+    me = lax.axis_index(axis)
+    names = SLAB + ("img",)
+    coords = [lax.axis_index(a) for a in names]
+    at = names.index(axis)
+    mesh_ids = pl.DeviceIdType.MESH
+    peers = [lax.rem(me + 1 + i, count) for i in range(count - 1)]
+
+    def where(peer):
+        return tuple(coords[:at]) + (peer,) + tuple(coords[at + 1:])
+
+    barrier = pltpu.get_barrier_semaphore()
+    for peer in peers:
+        pl.semaphore_signal(barrier, inc=1, device_id=where(peer), device_id_type=mesh_ids)
+    pl.semaphore_wait(barrier, count - 1)
+    local = pltpu.make_async_copy(x_ref, o_ref.at[me], local_sem)
+    local.start()
+    sends = []
+    for i, peer in enumerate(peers):
+        copy = pltpu.make_async_remote_copy(
+            src_ref=x_ref, dst_ref=o_ref.at[me], send_sem=send_sems.at[i], recv_sem=recv_sems.at[me],
+            device_id=where(peer), device_id_type=mesh_ids,
+        )
+        copy.start()
+        sends.append(copy)
+    for i, peer in enumerate(peers):
+        sends[i].wait_send()
+        pltpu.make_async_remote_copy(
+            src_ref=x_ref, dst_ref=o_ref.at[peer], send_sem=send_sems.at[i], recv_sem=recv_sems.at[peer],
+            device_id=where(peer), device_id_type=mesh_ids,
+        ).wait_recv()
+    local.wait()
+
+
+def axis_gather(x, axis, cid):
+    count = lax.axis_size(axis)
+    out = pl.pallas_call(
+        functools.partial(_axis_gather_kernel, axis),
+        out_shape=jax.ShapeDtypeStruct((count,) + x.shape, x.dtype),
+        in_specs=[pl.BlockSpec(memory_space=pl.ANY)],
+        out_specs=pl.BlockSpec(memory_space=pl.ANY),
+        scratch_shapes=[
+            pltpu.SemaphoreType.DMA((count,)),
+            pltpu.SemaphoreType.DMA((count,)),
+            pltpu.SemaphoreType.DMA,
+        ],
+        compiler_params=pltpu.CompilerParams(collective_id=cid, has_side_effects=True),
+    )(x)
+    return out.reshape((-1,) + x.shape[1:])
+
+
 def _img_sum_kernel(x_ref, o_ref, gat, qbuf, s1, r1, s2, r2, l1, l2):
     count, rows = gat.shape[0], gat.shape[1]
     me = lax.axis_index("img")
@@ -456,12 +508,8 @@
         preferred_element_type=jnp.float32,
     ).reshape(ori_dev, fourier, 2 * fourier)
     panels = summed.astype(jnp.bfloat16)
-    for axis in (SLAB[1], SLAB[0], SLAB[2]):
-        parts = lax.axis_size(axis)
-        panels = lax.all_to_all(
-            jnp.broadcast_to(panels[None], (parts,) + panels.shape),
-            axis, split_axis=0, concat_axis=0, tiled=True,
-        ).reshape((-1,) + panels.shape[1:])
+    for cid, axis in ((5, SLAB[1]), (6, SLAB[0]), (7, SLAB[2])):
+        panels = axis_gather(panels, axis, cid)
     sizes = tuple(lax.axis_size(a) for a in SLAB)
     inv_perm = jnp.arange(orient_count, dtype=jnp.int32).reshape(
         (sizes[2], sizes[0], sizes[1], ori_dev)

time: 228 us -> 289 us (1.27)
  Pallas kernels: 128 us -> 239 us
  waiting for transfers between devices: 47.6 us -> 15.9 us
  starting transfers between devices: 17.7 us -> 8.19 us
  blocking collectives: 8.15 us -> 0 us
  local copies, waits for them, and re-layouts: 8.36 us -> 5.35 us
    pallas_call x0 -> x3, Pallas kernels: none -> 111 us  [axis_gather(): pl.pallas_call(functools.partial(_axis_gather_kernel, axis), out_shape=ja...]
    all_to_all x2 -> x0, waiting for transfers between devices: 31.8 us -> none  [on_device(): lax.all_to_all(jnp.broadcast_to(panels[None], (parts,) + panels.shape), a...]
    all_to_all x2 -> x0, starting transfers between devices: 11.4 us -> none  [on_device(): lax.all_to_all(jnp.broadcast_to(panels[None], (parts,) + panels.shape), a...]
    all_to_all x1 -> x0, blocking collectives: 8.15 us -> none  [on_device(): lax.all_to_all(jnp.broadcast_to(panels[None], (parts,) + panels.shape), a...]
    broadcast_in_dim x3 -> x0, local copies, waits for them, and re-layouts: 3.08 us -> none  [on_device(): jnp.broadcast_to(panels[None], (parts,) + panels.shape)]
  transfers between devices with their start and end apart: 3 -> 1, of which waited for: 3 -> 1; matrix products, arithmetic and copies ran while one was open for 5% -> 0% of each run, Pallas kernels for 0% -> 0%
where the time goes in v15:
time: 289 us; the launch traced here: 288 us
  Pallas kernels  239 us (83%)
  waiting for transfers between devices  15.9 us (6%)
  other arithmetic  12.2 us (4%)
  starting transfers between devices  8.19 us (3%)
  matrix products  6.23 us (2%)
  local copies, waits for them, and re-layouts  5.35 us (2%)
    pallas_call x3, Pallas kernels, axis_gather(): pl.pallas_call(functools.partial(_axis_gather_kernel, axis), out_shape=ja...  111 us
    pallas_call x2, Pallas kernels, axis_sum(): pl.pallas_call(functools.partial(_axis_sum_kernel, axis), out_shape=jax.S...  45.6 us
    pallas_call x1, Pallas kernels, slab_all_to_all(): pl.pallas_call(_a2a_kernel, out_shape=jax.ShapeDtypeStruct(x.shape, x.dty...  34.2 us
    pallas_call x1, Pallas kernels, correlate_all(): pl.pallas_call(_correlate_kernel, grid_spec=grid_spec, out_shape=[jax.Sha...  22.7 us
    pallas_call x1, Pallas kernels, img_sum(): pl.pallas_call(_img_sum_kernel, out_shape=jax.ShapeDtypeStruct((count, ro...  21.3 us
    all_to_all x1, waiting for transfers between devices, on_device(): lax.all_to_all(outgoing, SLAB, split_axis=0, concat_axis=0, tiled=True)  15.9 us
    all_to_all x1, starting transfers between devices, on_device(): lax.all_to_all(outgoing, SLAB, split_axis=0, concat_axis=0, tiled=True)  8.19 us
  transfers between devices with their start and end apart: 1, of which 1 were waited for; matrix products, arithmetic and copies ran while one was open for 0% of the time, Pallas kernels for 0%

profile of v15, /device:TPU:6, one launch (start us, length us, event | category | flops | bytes accessed | tf_op | source)
XLA Modules:
  0.0 288.1 jit_solution(7621807645273997712)
XLA Ops:
  0.6 0.0 copy-start
  0.7 0.8 compare_select_fusion
  1.4 0.8 copy.22
  2.2 0.7 multiply_bitcast_fusion
  2.9 0.1 copy.23
  3.0 0.1 reshape.388
  3.1 0.6 reshape_squeeze.3.orient_ref
  3.7 0.1 reshape.379
  3.8 0.1 add_multiply_fusion.2
  3.9 0.0 copy-done
  3.9 2.4 fusion.2.x_ref
  6.2 34.2 %shard_map.77 = f32[64,16,256]{2,1,0:T(8,128)} custom-call(f32[64,16,256]{2,1,0:T(8,128)} %fusion.2.x_ref), custom_call_target="tpu_custom_call" | custom-call | tf_op jit(solution)/shard_map/pallas_call | solution.py:475
  40.4 0.7 dynamic-slice_bitcast_fusion
  41.1 2.2 convolution_convert_fusion.1
  43.3 0.6 copy.25
  44.0 19.5 %shard_map.78 = bf16[8,1,128,256]{3,2,1,0:T(8,128)(2,1)} custom-call(bf16[1,128,256]{2,1,0:T(8,128)(2,1)} %bitcast.55), custom_call_target="tpu_custom_call" | custom-call | tf_op jit(solution)/shard_map/pallas_call | solution.py:328
  63.5 26.2 %shard_map.79 = bf16[4,8,128,256]{3,2,1,0:T(8,128)(2,1)} custom-call(bf16[8,128,256]{2,1,0:T(8,128)(2,1)} %bitcast.52), custom_call_target="tpu_custom_call" | custom-call | tf_op jit(solution)/shard_map/pallas_call | solution.py:328
  89.7 64.8 %shard_map.80 = bf16[2,32,128,256]{3,2,1,0:T(8,128)(2,1)} custom-call(bf16[32,128,256]{2,1,0:T(8,128)(2,1)} %bitcast.51), custom_call_target="tpu_custom_call" | custom-call | tf_op jit(solution)/shard_map/pallas_call | solution.py:328
  154.5 1.3 gather_fusion
  155.8 0.1 broadcast_multiply_fusion.2
  155.9 3.0 %fusion.6 = (f32[8,128,128]{2,1,0:T(8,128)}, f32[8,128,128]{2,1,0:T(8,128)}) fusion(f32[8,128]{1,0:T(8,128)S(1)} %get-tuple-element.9, f32[8,128]{1,0:T(8,128)S(1)} %get-tuple-element.8), kind=kLoop, calls=%fused_computation.14 | loop fusion | flops 786432 | bytes 1056768 | tf_op jit(solution)/shard_map/convert_element_type | solution.py:146
  158.9 4.9 %add_negate_fusion.ctf_ref = f32[16,128,128]{2,1,0:T(8,128)} fusion(f32[128,128]{1,0:T(8,128)S(1)} %get-tuple-element.11, f32[128,128]{1,0:T(8,128)S(1)} %get-tuple-element.10, f32[16]{0:T(128)S(1)} %multiply_bitcast_fusion), kind=kLoop, calls=%fused_computation.9 | loop fusion | flops 1572864 | bytes 1179712 | tf_op jit(solution)/shard_map/neg | solution.py:42
  163.8 22.7 %shard_map.81 = (f32[16,64,1]{2,1,0:T(8,128)}, bf16[64,128,256]{2,1,0:T(8,128)(2,1)}) custom-call(s32[64]{0:T(128)} %reshape_squeeze.3.orient_ref, s32[64]{0:T(128)} %gather_fusion, bf16[64,128,256]{2,1,0:T(8,128)(2,1)} %bitcast.50, bf16[16,128,256]{2,1,0:T(8,128)(2,1)} %bitcast.53, f32[16,128,128]{2,1,0:T(8,128)} %add_negate_fusion.ctf_ref, ...), custom_call_target="tpu_custom_call" | custom-call | tf_op jit(solution)/shard_map/pallas_call | solution.py:163
  186.5 5.1 %shard_map.82.x_ref = bf16[32,128,256]{2,1,0:T(8,128)(2,1)S(1)} custom-call(bf16[64,128,256]{2,1,0:T(8,128)(2,1)} %get-tuple-element.4.x_ref), custom_call_target="tpu_custom_call" | custom-call | tf_op jit(solution)/shard_map/pallas_call | solution.py:205
  191.7 0.0 copy-start.1
  191.7 27.5 %shard_map.83.x_ref = bf16[8,128,256]{2,1,0:T(8,128)(2,1)S(1)} custom-call(bf16[32,128,256]{2,1,0:T(8,128)(2,1)S(1)} %shard_map.82.x_ref), custom_call_target="tpu_custom_call" | custom-call | tf_op jit(solution)/shard_map/pallas_call | solution.py:274
  219.1 18.1 %shard_map.84 = bf16[1,128,256]{2,1,0:T(8,128)(2,1)S(1)} custom-call(bf16[8,128,256]{2,1,0:T(8,128)(2,1)S(1)} %shard_map.83.x_ref), custom_call_target="tpu_custom_call" | custom-call | tf_op jit(solution)/shard_map/pallas_call | solution.py:274
  237.3 0.3 fusion
  237.6 1.1 copy.27
  238.7 8.2 %all-to-all-start = ((bf16[64,16,256]{2,1,0:T(8,128)(2,1)}), bf16[64,16,256]{2,1,0:T(8,128)(2,1)S(1)}, u32[]{:S(2)}, u32[]{:S(2)}) async-start(bf16[64,16,256]{2,1,0:T(8,128)(2,1)} %copy.27), calls=%async_computation | async-start | bytes 1048576 | tf_op jit(solution)/shard_map/all_to_all | solution.py:527
  246.9 0.0 copy-done.1
  246.9 0.8 reduce
  247.7 15.9 %all-to-all-done = bf16[64,16,256]{2,1,0:T(8,128)(2,1)S(1)} async-done(((bf16[64,16,256]{2,1,0:T(8,128)(2,1)}), bf16[64,16,256]{2,1,0:T(8,128)(2,1)S(1)}, u32[]{:S(2)}, u32[]{:S(2)}) %all-to-all-start) | async-done | bytes 524320 | tf_op jit(solution)/shard_map/all_to_all | solution.py:527
  263.6 1.3 convolution_bitcast_fusion.x_ref
  264.9 21.3 %shard_map.85 = f32[4,128,256]{2,1,0:T(8,128)} custom-call(f32[512,256]{1,0:T(8,128)} %convolution_bitcast_fusion.x_ref), custom_call_target="tpu_custom_call" | custom-call | tf_op jit(solution)/shard_map/pallas_call | solution.py:396
  286.3 1.9 broadcast_multiply_fusion
  (5 shorter events, 0.0 us)
Async XLA Ops:
  0.6 3.2 %copy-start = (bf16[1,64,16,512]{3,2,1,0:T(8,128)(2,1)S(1)}, bf16[1,64,16,512]{3,2,1,0:T(8,128)(2,1)}, u32[]{:S(2)}) copy-start(bf16[1,64,16,512]{3,2,1,0:T(8,128)(2,1)} %param.7) | copy-start | bytes 3145732
  191.7 55.2 %copy-start.1 = (f32[16,64,1]{2,1,0:T(8,128)S(1)}, f32[16,64,1]{2,1,0:T(8,128)}, u32[]{:S(2)}) copy-start(f32[16,64,1]{2,1,0:T(8,128)} %get-tuple-element.5) | copy-start | bytes 12292
  238.7 24.9 %all-to-all-start = ((bf16[64,16,256]{2,1,0:T(8,128)(2,1)}), bf16[64,16,256]{2,1,0:T(8,128)(2,1)S(1)}, u32[]{:S(2)}, u32[]{:S(2)}) async-start(bf16[64,16,256]{2,1,0:T(8,128)(2,1)} %copy.27), calls=%async_computation | async-start | bytes 1048576 | tf_op jit(solution)/shard_map/all_to_all | solution.py:527

commit v16 on v15

--- a/solution.py
+++ b/solution.py
@@ -508,8 +508,13 @@
         preferred_element_type=jnp.float32,
     ).reshape(ori_dev, fourier, 2 * fourier)
     panels = summed.astype(jnp.bfloat16)
-    for cid, axis in ((5, SLAB[1]), (6, SLAB[0]), (7, SLAB[2])):
-        panels = axis_gather(panels, axis, cid)
+    panels = axis_gather(panels, SLAB[1], 5)
+    for axis in (SLAB[0], SLAB[2]):
+        parts = lax.axis_size(axis)
+        panels = lax.all_to_all(
+            jnp.broadcast_to(panels[None], (parts,) + panels.shape),
+            axis, split_axis=0, concat_axis=0, tiled=True,
+        ).reshape((-1,) + panels.shape[1:])
     sizes = tuple(lax.axis_size(a) for a in SLAB)
     inv_perm = jnp.arange(orient_count, dtype=jnp.int32).reshape(
         (sizes[2], sizes[0], sizes[1], ori_dev)

time: 289 us -> 226 us (0.78)
  Pallas kernels: 239 us -> 148 us
  waiting for transfers between devices: 15.9 us -> 29.2 us
  blocking collectives: 0 us -> 8.16 us
  starting transfers between devices: 8.19 us -> 13.2 us
  local copies, waits for them, and re-layouts: 5.35 us -> 9.23 us
    pallas_call x3 -> x1, Pallas kernels: 111 us -> 19.6 us  [axis_gather(): pl.pallas_call(functools.partial(_axis_gather_kernel, axis), out_shape=ja...]
    all_to_all x0 -> x1, waiting for transfers between devices: none -> 13.3 us  [on_device(): lax.all_to_all(jnp.broadcast_to(panels[None], (parts,) + panels.shape), a...]
    all_to_all x0 -> x1, blocking collectives: none -> 8.16 us  [on_device(): lax.all_to_all(jnp.broadcast_to(panels[None], (parts,) + panels.shape), a...]
    all_to_all x0 -> x1, starting transfers between devices: none -> 4.5 us  [on_device(): lax.all_to_all(jnp.broadcast_to(panels[None], (parts,) + panels.shape), a...]
    broadcast_in_dim x0 -> x2, local copies, waits for them, and re-layouts: none -> 3.31 us  [on_device(): jnp.broadcast_to(panels[None], (parts,) + panels.shape)]
  transfers between devices with their start and end apart: 1 -> 2, of which waited for: 1 -> 2; matrix products, arithmetic and copies ran while one was open for 0% -> 5% of each run, Pallas kernels for 0% -> 0%
where the time goes in v16:
time: 226 us; the launch traced here: 225 us
  Pallas kernels  148 us (65%)
  waiting for transfers between devices  29.2 us (13%)
  starting transfers between devices  13.2 us (6%)
  other arithmetic  10.8 us (5%)
  local copies, waits for them, and re-layouts  9.23 us (4%)
  blocking collectives  8.16 us (4%)
  matrix products  6.24 us (3%)
    pallas_call x2, Pallas kernels, axis_sum(): pl.pallas_call(functools.partial(_axis_sum_kernel, axis), out_shape=jax.S...  44.9 us
    pallas_call x1, Pallas kernels, slab_all_to_all(): pl.pallas_call(_a2a_kernel, out_shape=jax.ShapeDtypeStruct(x.shape, x.dty...  34.1 us
    pallas_call x1, Pallas kernels, correlate_all(): pl.pallas_call(_correlate_kernel, grid_spec=grid_spec, out_shape=[jax.Sha...  22.7 us
    pallas_call x1, Pallas kernels, img_sum(): pl.pallas_call(_img_sum_kernel, out_shape=jax.ShapeDtypeStruct((count, ro...  21.3 us
    pallas_call x1, Pallas kernels, axis_gather(): pl.pallas_call(functools.partial(_axis_gather_kernel, axis), out_shape=ja...  19.6 us
    all_to_all x1, waiting for transfers between devices, on_device(): lax.all_to_all(outgoing, SLAB, split_axis=0, concat_axis=0, tiled=True)  15.9 us
    all_to_all x1, waiting for transfers between devices, on_device(): lax.all_to_all(jnp.broadcast_to(panels[None], (parts,) + panels.shape), a...  13.3 us
    all_to_all x1, starting transfers between devices, on_device(): lax.all_to_all(outgoing, SLAB, split_axis=0, concat_axis=0, tiled=True)  8.74 us
  transfers between devices with their start and end apart: 2, of which 2 were waited for; matrix products, arithmetic and copies ran while one was open for 5% of the time, Pallas kernels for 0%

profile of v16, /device:TPU:6, one launch (start us, length us, event | category | flops | bytes accessed | tf_op | source)
XLA Modules:
  0.0 225.3 jit_solution(7477276931764300331)
XLA Ops:
  0.6 0.0 copy-start
  0.7 1.2 copy-done
  1.9 2.4 %fusion.2.x_ref = f32[64,16,256]{2,1,0:T(8,128)} fusion(bf16[1,64,16,512]{3,2,1,0:T(8,128)(2,1)S(1)} %copy-done, bf16[512,256]{1,0:T(8,128)(2,1)} %param.6), kind=kOutput, calls=%fused_computation.6 | convolution fusion | flops 268435456 | bytes 2359296 | tf_op jit(solution)/shard_map/jpr,rx->jpx/dot_general | solution.py:500
  4.2 34.1 %shard_map.77 = f32[64,16,256]{2,1,0:T(8,128)} custom-call(f32[64,16,256]{2,1,0:T(8,128)} %fusion.2.x_ref), custom_call_target="tpu_custom_call" | custom-call | tf_op jit(solution)/shard_map/pallas_call | solution.py:475
  38.3 0.7 dynamic-slice_bitcast_fusion
  39.0 0.0 copy-start.2
  39.0 2.2 convolution_convert_fusion.1
  41.3 0.6 copy.25
  41.9 19.6 %shard_map.78 = bf16[8,1,128,256]{3,2,1,0:T(8,128)(2,1)} custom-call(bf16[1,128,256]{2,1,0:T(8,128)(2,1)} %bitcast.55), custom_call_target="tpu_custom_call" | custom-call | tf_op jit(solution)/shard_map/pallas_call | solution.py:328
  61.5 2.6 %broadcast_in_dim.9 = bf16[4,8,128,256]{3,2,1,0:T(8,128)(2,1)} broadcast(bf16[8,128,256]{2,1,0:T(8,128)(2,1)} %bitcast.52), dimensions={1,2,3} | broadcast | bytes 2621440 | tf_op jit(solution)/shard_map/broadcast_in_dim | solution.py:515
  64.2 4.5 %all-to-all-start = ((bf16[4,8,128,256]{3,2,1,0:T(8,128)(2,1)}), bf16[4,8,128,256]{3,2,1,0:T(8,128)(2,1)S(1)}, u32[]{:S(2)}, u32[]{:S(2)}) async-start(bf16[4,8,128,256]{3,2,1,0:T(8,128)(2,1)} %broadcast_in_dim.9), calls=%async_computation | async-start | bytes 4194304 | tf_op jit(solution)/shard_map/all_to_all | solution.py:514
  68.7 0.0 copy-done.2
  68.7 0.1 copy.23
  68.8 0.1 reshape.382
  68.9 0.1 copy.22
  69.0 0.6 reshape_squeeze.3.orient_ref
  69.6 0.1 reshape.375
  69.7 0.0 copy-start.3
  69.7 1.3 gather_fusion
  71.0 0.0 copy-done.3
  71.0 0.1 broadcast_multiply_fusion.2
  71.1 0.1 add_multiply_fusion.2
  71.2 3.1 %fusion.6 = (f32[8,128,128]{2,1,0:T(8,128)}, f32[8,128,128]{2,1,0:T(8,128)}) fusion(f32[8,128]{1,0:T(8,128)S(1)} %get-tuple-element.9, f32[8,128]{1,0:T(8,128)S(1)} %get-tuple-element.8), kind=kLoop, calls=%fused_computation.14 | loop fusion | flops 786432 | bytes 1056768 | tf_op jit(solution)/shard_map/convert_element_type | solution.py:146
  74.2 4.9 %add_negate_fusion.ctf_ref = f32[16,128,128]{2,1,0:T(8,128)} fusion(f32[128,128]{1,0:T(8,128)S(1)} %get-tuple-element.11, f32[128,128]{1,0:T(8,128)S(1)} %get-tuple-element.10, f32[16]{0:T(128)S(1)} %multiply_bitcast_fusion), kind=kLoop, calls=%fused_computation.9 | loop fusion | flops 1572864 | bytes 1179712 | tf_op jit(solution)/shard_map/neg | solution.py:42
  79.1 13.3 %all-to-all-done = bf16[4,8,128,256]{3,2,1,0:T(8,128)(2,1)S(1)} async-done(((bf16[4,8,128,256]{3,2,1,0:T(8,128)(2,1)}), bf16[4,8,128,256]{3,2,1,0:T(8,128)(2,1)S(1)}, u32[]{:S(2)}, u32[]{:S(2)}) %all-to-all-start) | async-done | bytes 2097184 | tf_op jit(solution)/shard_map/all_to_all | solution.py:514
  92.4 0.7 broadcast_in_dim.11
  93.1 8.2 %all_to_all.15 = bf16[2,32,128,256]{3,2,1,0:T(8,128)(2,1)} all-to-all(bf16[2,32,128,256]{3,2,1,0:T(8,128)(2,1)S(1)} %broadcast_in_dim.11), channel_id=1, replica_groups=mesh['sx'=4,'sz'=8,'sc'=2,'img'=4] {'sc'}, dimensions={0} | all-to-all | bytes 8388608 | tf_op jit(solution)/shard_map/all_to_all | solution.py:514
  101.3 22.7 %shard_map.79 = (f32[16,64,1]{2,1,0:T(8,128)}, bf16[64,128,256]{2,1,0:T(8,128)(2,1)}) custom-call(s32[64]{0:T(128)} %reshape_squeeze.3.orient_ref, s32[64]{0:T(128)} %gather_fusion, bf16[64,128,256]{2,1,0:T(8,128)(2,1)} %bitcast.50, bf16[16,128,256]{2,1,0:T(8,128)(2,1)} %bitcast.53, f32[16,128,128]{2,1,0:T(8,128)} %add_negate_fusion.ctf_ref, ...), custom_call_target="tpu_custom_call" | custom-call | tf_op jit(solution)/shard_map/pallas_call | solution.py:163
  124.0 5.0 %shard_map.80.x_ref = bf16[32,128,256]{2,1,0:T(8,128)(2,1)S(1)} custom-call(bf16[64,128,256]{2,1,0:T(8,128)(2,1)} %get-tuple-element.4.x_ref), custom_call_target="tpu_custom_call" | custom-call | tf_op jit(solution)/shard_map/pallas_call | solution.py:205
  129.0 0.0 copy-start.1
  129.0 27.0 %shard_map.81.x_ref = bf16[8,128,256]{2,1,0:T(8,128)(2,1)S(1)} custom-call(bf16[32,128,256]{2,1,0:T(8,128)(2,1)S(1)} %shard_map.80.x_ref), custom_call_target="tpu_custom_call" | custom-call | tf_op jit(solution)/shard_map/pallas_call | solution.py:274
  156.0 17.9 %shard_map.82 = bf16[1,128,256]{2,1,0:T(8,128)(2,1)S(1)} custom-call(bf16[8,128,256]{2,1,0:T(8,128)(2,1)S(1)} %shard_map.81.x_ref), custom_call_target="tpu_custom_call" | custom-call | tf_op jit(solution)/shard_map/pallas_call | solution.py:274
  173.9 0.3 fusion
  174.3 1.1 copy.27
  175.3 8.7 %all-to-all-start.2 = ((bf16[64,16,256]{2,1,0:T(8,128)(2,1)}), bf16[64,16,256]{2,1,0:T(8,128)(2,1)S(1)}, u32[]{:S(2)}, u32[]{:S(2)}) async-start(bf16[64,16,256]{2,1,0:T(8,128)(2,1)} %copy.27), calls=%async_computation.2 | async-start | bytes 1048576 | tf_op jit(solution)/shard_map/all_to_all | solution.py:532
  184.1 0.0 copy-done.1
  184.1 0.8 reduce
  184.9 15.9 %all-to-all-done.2 = bf16[64,16,256]{2,1,0:T(8,128)(2,1)S(1)} async-done(((bf16[64,16,256]{2,1,0:T(8,128)(2,1)}), bf16[64,16,256]{2,1,0:T(8,128)(2,1)S(1)}, u32[]{:S(2)}, u32[]{:S(2)}) %all-to-all-start.2) | async-done | bytes 524320 | tf_op jit(solution)/shard_map/all_to_all | solution.py:532
  200.8 1.3 convolution_bitcast_fusion.x_ref
  202.1 21.3 %shard_map.83 = f32[4,128,256]{2,1,0:T(8,128)} custom-call(f32[512,256]{1,0:T(8,128)} %convolution_bitcast_fusion.x_ref), custom_call_target="tpu_custom_call" | custom-call | tf_op jit(solution)/shard_map/pallas_call | solution.py:396
  223.4 1.9 broadcast_multiply_fusion
  (7 shorter events, 0.0 us)
Async XLA Ops:
  0.6 1.2 copy-start
  39.0 29.6 %copy-start.2 = (s32[1,16,4]{1,2,0:T(4,128)S(1)}, s32[1,16,4]{1,2,0:T(4,128)}, u32[]{:S(2)}) copy-start(s32[1,16,4]{1,2,0:T(4,128)} %param.11) | copy-start | bytes 772
  64.2 28.3 %all-to-all-start = ((bf16[4,8,128,256]{3,2,1,0:T(8,128)(2,1)}), bf16[4,8,128,256]{3,2,1,0:T(8,128)(2,1)S(1)}, u32[]{:S(2)}, u32[]{:S(2)}) async-start(bf16[4,8,128,256]{3,2,1,0:T(8,128)(2,1)} %broadcast_in_dim.9), calls=%async_computation | async-start | bytes 4194304 | tf_op jit(solution)/shard_map/all_to_all | solution.py:514
  69.7 1.3 copy-start.3
  129.0 55.1 %copy-start.1 = (f32[16,64,1]{2,1,0:T(8,128)S(1)}, f32[16,64,1]{2,1,0:T(8,128)}, u32[]{:S(2)}) copy-start(f32[16,64,1]{2,1,0:T(8,128)} %get-tuple-element.5) | copy-start | bytes 12292
  175.3 25.5 %all-to-all-start.2 = ((bf16[64,16,256]{2,1,0:T(8,128)(2,1)}), bf16[64,16,256]{2,1,0:T(8,128)(2,1)S(1)}, u32[]{:S(2)}, u32[]{:S(2)}) async-start(bf16[64,16,256]{2,1,0:T(8,128)(2,1)} %copy.27), calls=%async_computation.2 | async-start | bytes 1048576 | tf_op jit(solution)/shard_map/all_to_all | solution.py:532

commit v17 on v16

--- a/solution.py
+++ b/solution.py
@@ -529,7 +529,7 @@
         "osb,obpx->sopx", chosen_back, back_own, preferred_element_type=jnp.float32
     )
     outgoing = outgoing.astype(jnp.bfloat16).reshape(slab_count * ori_dev, block_rows, 2 * fourier)
-    incoming = lax.all_to_all(outgoing, SLAB, split_axis=0, concat_axis=0, tiled=True)
+    incoming = slab_all_to_all(outgoing, 8)
     column = jnp.einsum("jpr,jpx->rx", interp[0], incoming, preferred_element_type=jnp.float32)
     summed_cols = img_sum(column, lax.axis_size("img"), 0)
     update = summed_cols / math.sqrt(img_dev * slab_count)

time: 226 us -> 223 us (0.987)
  Pallas kernels: 148 us -> 169 us
  waiting for transfers between devices: 29.2 us -> 13.3 us
  starting transfers between devices: 13.2 us -> 4.5 us
    pallas_call x1 -> x2, Pallas kernels: 34.1 us -> 55.9 us  [slab_all_to_all(): pl.pallas_call(_a2a_kernel, out_shape=jax.ShapeDtypeStruct(x.shape, x.dty...]
    all_to_all x1 -> x0, waiting for transfers between devices: 15.9 us -> none  [on_device(): lax.all_to_all(outgoing, SLAB, split_axis=0, concat_axis=0, tiled=True)]
    all_to_all x1 -> x0, starting transfers between devices: 8.74 us -> none  [on_device(): lax.all_to_all(outgoing, SLAB, split_axis=0, concat_axis=0, tiled=True)]
  transfers between devices with their start and end apart: 2 -> 1, of which waited for: 2 -> 1; matrix products, arithmetic and copies ran while one was open for 5% -> 5% of each run, Pallas kernels for 0% -> 0%
where the time goes in v17:
time: 223 us
  Pallas kernels  169 us (76%)
  waiting for transfers between devices  13.3 us (6%)
  other arithmetic  10.8 us (5%)
  local copies, waits for them, and re-layouts  9.23 us (4%)
  blocking collectives  8.17 us (4%)
  matrix products  7.27 us (3%)
  starting transfers between devices  4.5 us (2%)
    pallas_call x2, Pallas kernels, slab_all_to_all(): pl.pallas_call(_a2a_kernel, out_shape=jax.ShapeDtypeStruct(x.shape, x.dty...  55.9 us
    pallas_call x2, Pallas kernels, axis_sum(): pl.pallas_call(functools.partial(_axis_sum_kernel, axis), out_shape=jax.S...  44.9 us
    pallas_call x1, Pallas kernels, correlate_all(): pl.pallas_call(_correlate_kernel, grid_spec=grid_spec, out_shape=[jax.Sha...  22.7 us
    pallas_call x1, Pallas kernels, img_sum(): pl.pallas_call(_img_sum_kernel, out_shape=jax.ShapeDtypeStruct((count, ro...  20.5 us
    pallas_call x1, Pallas kernels, axis_gather(): pl.pallas_call(functools.partial(_axis_gather_kernel, axis), out_shape=ja...  19.6 us
    all_to_all x1, waiting for transfers between devices, on_device(): lax.all_to_all(jnp.broadcast_to(panels[None], (parts,) + panels.shape), a...  13.3 us
    all_to_all x1, blocking collectives, on_device(): lax.all_to_all(jnp.broadcast_to(panels[None], (parts,) + panels.shape), a...  8.17 us
    pallas_call x1, Pallas kernels, pair_sum(): pl.pallas_call(_pair_sum_kernel, out_shape=jax.ShapeDtypeStruct((half,) +...  5 us
  transfers between devices with their start and end apart: 1, of which 1 were waited for; matrix products, arithmetic and copies ran while one was open for 5% of the time, Pallas kernels for 0%

profile of v17, /device:TPU:6, one launch (start us, length us, event | category | flops | bytes accessed | tf_op | source)
XLA Modules:
  0.0 222.8 jit_solution(12181995393012471021)
XLA Ops:
  0.6 0.0 copy-start
  0.7 1.2 copy-done
  1.9 2.3 %fusion.1.x_ref = f32[64,16,256]{2,1,0:T(8,128)} fusion(bf16[1,64,16,512]{3,2,1,0:T(8,128)(2,1)S(1)} %copy-done, bf16[512,256]{1,0:T(8,128)(2,1)} %param.6), kind=kOutput, calls=%fused_computation.4 | convolution fusion | flops 268435456 | bytes 2359296 | tf_op jit(solution)/shard_map/jpr,rx->jpx/dot_general | solution.py:500
  4.2 34.1 %shard_map.77 = f32[64,16,256]{2,1,0:T(8,128)} custom-call(f32[64,16,256]{2,1,0:T(8,128)} %fusion.1.x_ref), custom_call_target="tpu_custom_call" | custom-call | tf_op jit(solution)/shard_map/pallas_call | solution.py:475
  38.3 0.7 dynamic-slice_bitcast_fusion
  39.0 0.0 copy-start.2
  39.0 2.2 convolution_convert_fusion
  41.3 0.6 copy.20
  41.9 19.6 %shard_map.78 = bf16[8,1,128,256]{3,2,1,0:T(8,128)(2,1)} custom-call(bf16[1,128,256]{2,1,0:T(8,128)(2,1)} %bitcast.57), custom_call_target="tpu_custom_call" | custom-call | tf_op jit(solution)/shard_map/pallas_call | solution.py:328
  61.5 2.6 %broadcast_in_dim.9 = bf16[4,8,128,256]{3,2,1,0:T(8,128)(2,1)} broadcast(bf16[8,128,256]{2,1,0:T(8,128)(2,1)} %bitcast.53), dimensions={1,2,3} | broadcast | bytes 2621440 | tf_op jit(solution)/shard_map/broadcast_in_dim | solution.py:515
  64.2 4.5 %all-to-all-start = ((bf16[4,8,128,256]{3,2,1,0:T(8,128)(2,1)}), bf16[4,8,128,256]{3,2,1,0:T(8,128)(2,1)S(1)}, u32[]{:S(2)}, u32[]{:S(2)}) async-start(bf16[4,8,128,256]{3,2,1,0:T(8,128)(2,1)} %broadcast_in_dim.9), calls=%async_computation | async-start | bytes 4194304 | tf_op jit(solution)/shard_map/all_to_all | solution.py:514
  68.7 0.0 copy-done.2
  68.7 0.1 copy.18
  68.8 0.1 reshape.382
  68.9 0.1 copy.17
  69.0 0.6 reshape_squeeze.3.orient_ref
  69.6 0.1 reshape.375
  69.7 0.0 copy-start.3
  69.7 1.3 gather_fusion
  71.0 0.0 copy-done.3
  71.0 0.1 broadcast_multiply_fusion.2
  71.1 0.1 add_multiply_fusion.2
  71.2 3.1 %fusion.6 = (f32[8,128,128]{2,1,0:T(8,128)}, f32[8,128,128]{2,1,0:T(8,128)}) fusion(f32[8,128]{1,0:T(8,128)S(1)} %get-tuple-element.9, f32[8,128]{1,0:T(8,128)S(1)} %get-tuple-element.8), kind=kLoop, calls=%fused_computation.14 | loop fusion | flops 786432 | bytes 1056768 | tf_op jit(solution)/shard_map/convert_element_type | solution.py:146
  74.2 4.9 %add_negate_fusion.ctf_ref = f32[16,128,128]{2,1,0:T(8,128)} fusion(f32[128,128]{1,0:T(8,128)S(1)} %get-tuple-element.11, f32[128,128]{1,0:T(8,128)S(1)} %get-tuple-element.10, f32[16]{0:T(128)S(1)} %multiply_bitcast_fusion), kind=kLoop, calls=%fused_computation.8 | loop fusion | flops 1572864 | bytes 1179712 | tf_op jit(solution)/shard_map/neg | solution.py:42
  79.1 13.3 %all-to-all-done = bf16[4,8,128,256]{3,2,1,0:T(8,128)(2,1)S(1)} async-done(((bf16[4,8,128,256]{3,2,1,0:T(8,128)(2,1)}), bf16[4,8,128,256]{3,2,1,0:T(8,128)(2,1)S(1)}, u32[]{:S(2)}, u32[]{:S(2)}) %all-to-all-start) | async-done | bytes 2097184 | tf_op jit(solution)/shard_map/all_to_all | solution.py:514
  92.4 0.7 broadcast_in_dim.11
  93.1 8.2 %all_to_all.10 = bf16[2,32,128,256]{3,2,1,0:T(8,128)(2,1)} all-to-all(bf16[2,32,128,256]{3,2,1,0:T(8,128)(2,1)S(1)} %broadcast_in_dim.11), channel_id=1, replica_groups=mesh['sx'=4,'sz'=8,'sc'=2,'img'=4] {'sc'}, dimensions={0} | all-to-all | bytes 8388608 | tf_op jit(solution)/shard_map/all_to_all | solution.py:514
  101.3 22.7 %shard_map.79 = (f32[16,64,1]{2,1,0:T(8,128)}, bf16[64,128,256]{2,1,0:T(8,128)(2,1)}) custom-call(s32[64]{0:T(128)} %reshape_squeeze.3.orient_ref, s32[64]{0:T(128)} %gather_fusion, bf16[64,128,256]{2,1,0:T(8,128)(2,1)} %bitcast.51, bf16[16,128,256]{2,1,0:T(8,128)(2,1)} %bitcast.55, f32[16,128,128]{2,1,0:T(8,128)} %add_negate_fusion.ctf_ref, ...), custom_call_target="tpu_custom_call" | custom-call | tf_op jit(solution)/shard_map/pallas_call | solution.py:163
  124.0 5.0 %shard_map.80.x_ref = bf16[32,128,256]{2,1,0:T(8,128)(2,1)S(1)} custom-call(bf16[64,128,256]{2,1,0:T(8,128)(2,1)} %get-tuple-element.4.x_ref), custom_call_target="tpu_custom_call" | custom-call | tf_op jit(solution)/shard_map/pallas_call | solution.py:205
  129.0 27.0 %shard_map.81.x_ref = bf16[8,128,256]{2,1,0:T(8,128)(2,1)S(1)} custom-call(bf16[32,128,256]{2,1,0:T(8,128)(2,1)S(1)} %shard_map.80.x_ref), custom_call_target="tpu_custom_call" | custom-call | tf_op jit(solution)/shard_map/pallas_call | solution.py:274
  156.0 0.0 copy-start.1
  156.0 17.9 %shard_map.82 = bf16[1,128,256]{2,1,0:T(8,128)(2,1)S(1)} custom-call(bf16[8,128,256]{2,1,0:T(8,128)(2,1)S(1)} %shard_map.81.x_ref), custom_call_target="tpu_custom_call" | custom-call | tf_op jit(solution)/shard_map/pallas_call | solution.py:274
  173.9 0.3 fusion.9
  174.3 1.1 copy.37
  175.4 21.8 %shard_map.83 = bf16[64,16,256]{2,1,0:T(8,128)(2,1)} custom-call(bf16[64,16,256]{2,1,0:T(8,128)(2,1)} %bitcast.54), custom_call_target="tpu_custom_call" | custom-call | tf_op jit(solution)/shard_map/pallas_call | solution.py:475
  197.2 2.4 %convolution_bitcast_fusion.x_ref = f32[512,256]{1,0:T(8,128)} fusion(bf16[64,16,256]{2,1,0:T(8,128)(2,1)} %shard_map.83, bf16[1,64,16,512]{3,2,1,0:T(8,128)(2,1)S(1)} %copy-done), kind=kOutput, calls=%fused_computation.1 | convolution fusion | flops 268435456 | bytes 2097152 | tf_op jit(solution)/shard_map/jpr,jpx->rx/dot_general | solution.py:533
  199.5 20.5 %shard_map.84 = f32[4,128,256]{2,1,0:T(8,128)} custom-call(f32[512,256]{1,0:T(8,128)} %convolution_bitcast_fusion.x_ref), custom_call_target="tpu_custom_call" | custom-call | tf_op jit(solution)/shard_map/pallas_call | solution.py:396
  220.1 1.9 broadcast_multiply_fusion
  222.0 0.0 copy-done.1
  222.0 0.8 reduce
  (7 shorter events, 0.0 us)
Async XLA Ops:
  0.6 1.2 copy-start
  39.0 29.6 %copy-start.2 = (s32[1,16,4]{1,2,0:T(4,128)S(1)}, s32[1,16,4]{1,2,0:T(4,128)}, u32[]{:S(2)}) copy-start(s32[1,16,4]{1,2,0:T(4,128)} %param.11) | copy-start | bytes 772
  64.2 28.3 %all-to-all-start = ((bf16[4,8,128,256]{3,2,1,0:T(8,128)(2,1)}), bf16[4,8,128,256]{3,2,1,0:T(8,128)(2,1)S(1)}, u32[]{:S(2)}, u32[]{:S(2)}) async-start(bf16[4,8,128,256]{3,2,1,0:T(8,128)(2,1)} %broadcast_in_dim.9), calls=%async_computation | async-start | bytes 4194304 | tf_op jit(solution)/shard_map/all_to_all | solution.py:514
  69.7 1.3 copy-start.3
  156.0 65.9 %copy-start.1 = (f32[16,64,1]{2,1,0:T(8,128)S(1)}, f32[16,64,1]{2,1,0:T(8,128)}, u32[]{:S(2)}) copy-start(f32[16,64,1]{2,1,0:T(8,128)} %get-tuple-element.5) | copy-start | bytes 12292

commit v18 on v15

--- a/solution.py
+++ b/solution.py
@@ -340,6 +340,48 @@
     return out.reshape((-1,) + x.shape[1:])
 
 
+def _pair_gather_kernel(x_ref, o_ref, recv, send_sem, recv_sem, local_sem, move_sem):
+    me = lax.axis_index(SLAB[2])
+    mate = 1 - me
+    where = (lax.axis_index(SLAB[0]), lax.axis_index(SLAB[1]), mate, lax.axis_index("img"))
+    mesh_ids = pl.DeviceIdType.MESH
+    barrier = pltpu.get_barrier_semaphore()
+    pl.semaphore_signal(barrier, inc=1, device_id=where, device_id_type=mesh_ids)
+    pl.semaphore_wait(barrier, 1)
+    local = pltpu.make_async_copy(x_ref, o_ref.at[me], local_sem)
+    local.start()
+    copy = pltpu.make_async_remote_copy(
+        src_ref=x_ref, dst_ref=recv, send_sem=send_sem,
+        recv_sem=recv_sem, device_id=where, device_id_type=mesh_ids,
+    )
+    copy.start()
+    copy.wait()
+    move = pltpu.make_async_copy(recv, o_ref.at[mate], move_sem)
+    move.start()
+    local.wait()
+    move.wait()
+
+
+def pair_gather(x, cid):
+    out = pl.pallas_call(
+        _pair_gather_kernel,
+        out_shape=jax.ShapeDtypeStruct((2,) + x.shape, x.dtype),
+        in_specs=[pl.BlockSpec(memory_space=pl.ANY)],
+        out_specs=pl.BlockSpec(memory_space=pltpu.VMEM),
+        scratch_shapes=[
+            pltpu.VMEM(x.shape, x.dtype),
+            pltpu.SemaphoreType.DMA,
+            pltpu.SemaphoreType.DMA,
+            pltpu.SemaphoreType.DMA,
+            pltpu.SemaphoreType.DMA,
+        ],
+        compiler_params=pltpu.CompilerParams(
+            collective_id=cid, has_side_effects=True, vmem_limit_bytes=48 * 1024 * 1024
+        ),
+    )(x)
+    return out.reshape((-1,) + x.shape[1:])
+
+
 def _img_sum_kernel(x_ref, o_ref, gat, qbuf, s1, r1, s2, r2, l1, l2):
     count, rows = gat.shape[0], gat.shape[1]
     me = lax.axis_index("img")
@@ -508,8 +550,13 @@
         preferred_element_type=jnp.float32,
     ).reshape(ori_dev, fourier, 2 * fourier)
     panels = summed.astype(jnp.bfloat16)
-    for cid, axis in ((5, SLAB[1]), (6, SLAB[0]), (7, SLAB[2])):
-        panels = axis_gather(panels, axis, cid)
+    panels = axis_gather(panels, SLAB[1], 5)
+    parts = lax.axis_size(SLAB[0])
+    panels = lax.all_to_all(
+        jnp.broadcast_to(panels[None], (parts,) + panels.shape),
+        SLAB[0], split_axis=0, concat_axis=0, tiled=True,
+    ).reshape((-1,) + panels.shape[1:])
+    panels = pair_gather(panels, 9)
     sizes = tuple(lax.axis_size(a) for a in SLAB)
     inv_perm = jnp.arange(orient_count, dtype=jnp.int32).reshape(
         (sizes[2], sizes[0], sizes[1], ori_dev)
@@ -524,7 +571,7 @@
         "osb,obpx->sopx", chosen_back, back_own, preferred_element_type=jnp.float32
     )
     outgoing = outgoing.astype(jnp.bfloat16).reshape(slab_count * ori_dev, block_rows, 2 * fourier)
-    incoming = lax.all_to_all(outgoing, SLAB, split_axis=0, concat_axis=0, tiled=True)
+    incoming = slab_all_to_all(outgoing, 8)
     column = jnp.einsum("jpr,jpx->rx", interp[0], incoming, preferred_element_type=jnp.float32)
     summed_cols = img_sum(column, lax.axis_size("img"), 0)
     update = summed_cols / math.sqrt(img_dev * slab_count)

time: 289 us -> 221 us (0.76)
  Pallas kernels: 239 us -> 175 us
  starting transfers between devices: 8.19 us -> 4.64 us
  local copies, waits for them, and re-layouts: 5.35 us -> 8.55 us
    pallas_call x3 -> x1, Pallas kernels: 111 us -> 19.6 us  [axis_gather(): pl.pallas_call(functools.partial(_axis_gather_kernel, axis), out_shape=ja...]
    pallas_call x1 -> x2, Pallas kernels: 34.2 us -> 55.9 us  [slab_all_to_all(): pl.pallas_call(_a2a_kernel, out_shape=jax.ShapeDtypeStruct(x.shape, x.dty...]
    pallas_call x0 -> x1, Pallas kernels: none -> 6.41 us  [pair_gather(): pl.pallas_call(_pair_gather_kernel, out_shape=jax.ShapeDtypeStruct((2,) +...]
    all_to_all x1, starting transfers between devices: 8.19 us -> 4.64 us  [on_device(): lax.all_to_all(jnp.broadcast_to(panels[None], (parts,) + panels.shape), S...]
  transfers between devices with their start and end apart: 1 -> 1, of which waited for: 1 -> 1; matrix products, arithmetic and copies ran while one was open for 0% -> 5% of each run, Pallas kernels for 0% -> 0%
where the time goes in v18:
time: 221 us
  Pallas kernels  175 us (79%)
  waiting for transfers between devices  13.3 us (6%)
  other arithmetic  10.8 us (5%)
  local copies, waits for them, and re-layouts  8.55 us (4%)
  matrix products  7.32 us (3%)
  starting transfers between devices  4.64 us (2%)
    pallas_call x2, Pallas kernels, slab_all_to_all(): pl.pallas_call(_a2a_kernel, out_shape=jax.ShapeDtypeStruct(x.shape, x.dty...  55.9 us
    pallas_call x2, Pallas kernels, axis_sum(): pl.pallas_call(functools.partial(_axis_sum_kernel, axis), out_shape=jax.S...  44.9 us
    pallas_call x1, Pallas kernels, correlate_all(): pl.pallas_call(_correlate_kernel, grid_spec=grid_spec, out_shape=[jax.Sha...  22.7 us
    pallas_call x1, Pallas kernels, img_sum(): pl.pallas_call(_img_sum_kernel, out_shape=jax.ShapeDtypeStruct((count, ro...  20.5 us
    pallas_call x1, Pallas kernels, axis_gather(): pl.pallas_call(functools.partial(_axis_gather_kernel, axis), out_shape=ja...  19.6 us
    all_to_all x1, waiting for transfers between devices, on_device(): lax.all_to_all(jnp.broadcast_to(panels[None], (parts,) + panels.shape), S...  13.3 us
    pallas_call x1, Pallas kernels, pair_gather(): pl.pallas_call(_pair_gather_kernel, out_shape=jax.ShapeDtypeStruct((2,) +...  6.41 us
    pallas_call x1, Pallas kernels, pair_sum(): pl.pallas_call(_pair_sum_kernel, out_shape=jax.ShapeDtypeStruct((half,) +...  5 us
  transfers between devices with their start and end apart: 1, of which 1 were waited for; matrix products, arithmetic and copies ran while one was open for 5% of the time, Pallas kernels for 0%

profile of v18, /device:TPU:6, one launch (start us, length us, event | category | flops | bytes accessed | tf_op | source)
XLA Modules:
  0.0 220.5 jit_solution(18171873684387323607)
XLA Ops:
  0.6 0.0 copy-start
  0.7 1.2 copy-done
  1.9 2.3 %fusion.1.x_ref = f32[64,16,256]{2,1,0:T(8,128)} fusion(bf16[1,64,16,512]{3,2,1,0:T(8,128)(2,1)S(1)} %copy-done, bf16[512,256]{1,0:T(8,128)(2,1)} %param.6), kind=kOutput, calls=%fused_computation.4 | convolution fusion | flops 268435456 | bytes 2359296 | tf_op jit(solution)/shard_map/jpr,rx->jpx/dot_general | solution.py:542
  4.2 34.1 %shard_map.77 = f32[64,16,256]{2,1,0:T(8,128)} custom-call(f32[64,16,256]{2,1,0:T(8,128)} %fusion.1.x_ref), custom_call_target="tpu_custom_call" | custom-call | tf_op jit(solution)/shard_map/pallas_call | solution.py:517
  38.3 0.7 dynamic-slice_bitcast_fusion
  39.0 2.2 convolution_convert_fusion
  41.2 0.6 copy.20
  41.9 19.6 %shard_map.78 = bf16[8,1,128,256]{3,2,1,0:T(8,128)(2,1)} custom-call(bf16[1,128,256]{2,1,0:T(8,128)(2,1)} %bitcast.57), custom_call_target="tpu_custom_call" | custom-call | tf_op jit(solution)/shard_map/pallas_call | solution.py:328
  61.5 2.6 %broadcast_in_dim.5 = bf16[4,8,128,256]{3,2,1,0:T(8,128)(2,1)} broadcast(bf16[8,128,256]{2,1,0:T(8,128)(2,1)} %bitcast.53), dimensions={1,2,3} | broadcast | bytes 2621440 | tf_op jit(solution)/shard_map/broadcast_in_dim | solution.py:556
  64.2 0.0 copy-start.2
  64.2 4.6 %all-to-all-start = ((bf16[4,8,128,256]{3,2,1,0:T(8,128)(2,1)}), bf16[4,8,128,256]{3,2,1,0:T(8,128)(2,1)S(1)}, u32[]{:S(2)}, u32[]{:S(2)}) async-start(bf16[4,8,128,256]{3,2,1,0:T(8,128)(2,1)} %broadcast_in_dim.5), calls=%async_computation | async-start | bytes 4194304 | tf_op jit(solution)/shard_map/all_to_all | solution.py:555
  68.8 0.0 copy-done.2
  68.8 0.1 copy.18
  68.9 0.1 reshape.385
  69.0 0.1 copy.17
  69.1 0.6 reshape_squeeze.3.orient_ref
  69.7 0.1 reshape.377
  69.8 0.0 copy-start.3
  69.8 1.3 gather_fusion
  71.1 0.0 copy-done.3
  71.1 0.1 broadcast_multiply_fusion.2
  71.2 0.1 add_multiply_fusion.2
  71.3 3.1 %fusion.6 = (f32[8,128,128]{2,1,0:T(8,128)}, f32[8,128,128]{2,1,0:T(8,128)}) fusion(f32[8,128]{1,0:T(8,128)S(1)} %get-tuple-element.9, f32[8,128]{1,0:T(8,128)S(1)} %get-tuple-element.8), kind=kLoop, calls=%fused_computation.14 | loop fusion | flops 786432 | bytes 1056768 | tf_op jit(solution)/shard_map/convert_element_type | solution.py:146
  74.4 4.9 %add_negate_fusion.ctf_ref = f32[16,128,128]{2,1,0:T(8,128)} fusion(f32[128,128]{1,0:T(8,128)S(1)} %get-tuple-element.11, f32[128,128]{1,0:T(8,128)S(1)} %get-tuple-element.10, f32[16]{0:T(128)S(1)} %multiply_bitcast_fusion), kind=kLoop, calls=%fused_computation.8 | loop fusion | flops 1572864 | bytes 1179712 | tf_op jit(solution)/shard_map/neg | solution.py:42
  79.2 13.3 %all-to-all-done = bf16[4,8,128,256]{3,2,1,0:T(8,128)(2,1)S(1)} async-done(((bf16[4,8,128,256]{3,2,1,0:T(8,128)(2,1)}), bf16[4,8,128,256]{3,2,1,0:T(8,128)(2,1)S(1)}, u32[]{:S(2)}, u32[]{:S(2)}) %all-to-all-start) | async-done | bytes 2097184 | tf_op jit(solution)/shard_map/all_to_all | solution.py:555
  92.6 6.4 %shard_map.79 = bf16[2,32,128,256]{3,2,1,0:T(8,128)(2,1)} custom-call(bf16[32,128,256]{2,1,0:T(8,128)(2,1)S(1)} %bitcast.50), custom_call_target="tpu_custom_call" | custom-call | tf_op jit(solution)/shard_map/pallas_call | solution.py:366
  99.0 22.7 %shard_map.80 = (f32[16,64,1]{2,1,0:T(8,128)}, bf16[64,128,256]{2,1,0:T(8,128)(2,1)}) custom-call(s32[64]{0:T(128)} %reshape_squeeze.3.orient_ref, s32[64]{0:T(128)} %gather_fusion, bf16[64,128,256]{2,1,0:T(8,128)(2,1)} %bitcast.52, bf16[16,128,256]{2,1,0:T(8,128)(2,1)} %bitcast.55, f32[16,128,128]{2,1,0:T(8,128)} %add_negate_fusion.ctf_ref, ...), custom_call_target="tpu_custom_call" | custom-call | tf_op jit(solution)/shard_map/pallas_call | solution.py:163
  121.7 5.0 %shard_map.81.x_ref = bf16[32,128,256]{2,1,0:T(8,128)(2,1)S(1)} custom-call(bf16[64,128,256]{2,1,0:T(8,128)(2,1)} %get-tuple-element.4.x_ref), custom_call_target="tpu_custom_call" | custom-call | tf_op jit(solution)/shard_map/pallas_call | solution.py:205
  126.7 27.0 %shard_map.82.x_ref = bf16[8,128,256]{2,1,0:T(8,128)(2,1)S(1)} custom-call(bf16[32,128,256]{2,1,0:T(8,128)(2,1)S(1)} %shard_map.81.x_ref), custom_call_target="tpu_custom_call" | custom-call | tf_op jit(solution)/shard_map/pallas_call | solution.py:274
  153.7 17.9 %shard_map.83 = bf16[1,128,256]{2,1,0:T(8,128)(2,1)S(1)} custom-call(bf16[8,128,256]{2,1,0:T(8,128)(2,1)S(1)} %shard_map.82.x_ref), custom_call_target="tpu_custom_call" | custom-call | tf_op jit(solution)/shard_map/pallas_call | solution.py:274
  171.6 0.3 fusion.9
  172.0 1.1 copy.37
  173.0 21.8 %shard_map.84 = bf16[64,16,256]{2,1,0:T(8,128)(2,1)} custom-call(bf16[64,16,256]{2,1,0:T(8,128)(2,1)} %bitcast.54), custom_call_target="tpu_custom_call" | custom-call | tf_op jit(solution)/shard_map/pallas_call | solution.py:517
  194.8 0.0 copy-start.1
  194.9 2.4 %convolution_bitcast_fusion.x_ref = f32[512,256]{1,0:T(8,128)} fusion(bf16[64,16,256]{2,1,0:T(8,128)(2,1)} %shard_map.84, bf16[1,64,16,512]{3,2,1,0:T(8,128)(2,1)S(1)} %copy-done), kind=kOutput, calls=%fused_computation.1 | convolution fusion | flops 268435456 | bytes 2097152 | tf_op jit(solution)/shard_map/jpr,jpx->rx/dot_general | solution.py:575
  197.3 20.5 %shard_map.85 = f32[4,128,256]{2,1,0:T(8,128)} custom-call(f32[512,256]{1,0:T(8,128)} %convolution_bitcast_fusion.x_ref), custom_call_target="tpu_custom_call" | custom-call | tf_op jit(solution)/shard_map/pallas_call | solution.py:438
  217.8 1.9 broadcast_multiply_fusion
  219.7 0.0 copy-done.1
  219.7 0.8 reduce
  (7 shorter events, 0.0 us)
Async XLA Ops:
  0.6 1.2 copy-start
  64.2 4.6 %copy-start.2 = (s32[1,16,4]{1,2,0:T(4,128)S(1)}, s32[1,16,4]{1,2,0:T(4,128)}, u32[]{:S(2)}) copy-start(s32[1,16,4]{1,2,0:T(4,128)} %param.11) | copy-start | bytes 772
  64.2 28.4 %all-to-all-start = ((bf16[4,8,128,256]{3,2,1,0:T(8,128)(2,1)}), bf16[4,8,128,256]{3,2,1,0:T(8,128)(2,1)S(1)}, u32[]{:S(2)}, u32[]{:S(2)}) async-start(bf16[4,8,128,256]{3,2,1,0:T(8,128)(2,1)} %broadcast_in_dim.5), calls=%async_computation | async-start | bytes 4194304 | tf_op jit(solution)/shard_map/all_to_all | solution.py:555
  69.8 1.3 copy-start.3
  194.8 24.9 %copy-start.1 = (f32[16,64,1]{2,1,0:T(8,128)S(1)}, f32[16,64,1]{2,1,0:T(8,128)}, u32[]{:S(2)}) copy-start(f32[16,64,1]{2,1,0:T(8,128)} %get-tuple-element.5) | copy-start | bytes 12292

commit v19 on v18

--- a/solution.py
+++ b/solution.py
@@ -517,7 +517,7 @@
     return pl.pallas_call(
         _a2a_kernel,
         out_shape=jax.ShapeDtypeStruct(x.shape, x.dtype),
-        in_specs=[pl.BlockSpec(memory_space=pl.ANY)],
+        in_specs=[pl.BlockSpec(memory_space=pltpu.VMEM)],
         out_specs=pl.BlockSpec(memory_space=pl.ANY),
         scratch_shapes=[
             pltpu.SemaphoreType.DMA((count,)),

time: 221 us -> 223 us (level)
  no operation moved by 1% of the time
where the time goes in v19:
time: 223 us; the launch traced here: 222 us
  Pallas kernels  177 us (79%)
  waiting for transfers between devices  13.3 us (6%)
  other arithmetic  10.8 us (5%)
  local copies, waits for them, and re-layouts  8.55 us (4%)
  matrix products  7.32 us (3%)
  starting transfers between devices  4.64 us (2%)
    pallas_call x2, Pallas kernels, slab_all_to_all(): pl.pallas_call(_a2a_kernel, out_shape=jax.ShapeDtypeStruct(x.shape, x.dty...  57.6 us
    pallas_call x2, Pallas kernels, axis_sum(): pl.pallas_call(functools.partial(_axis_sum_kernel, axis), out_shape=jax.S...  44.9 us
    pallas_call x1, Pallas kernels, correlate_all(): pl.pallas_call(_correlate_kernel, grid_spec=grid_spec, out_shape=[jax.Sha...  22.7 us
    pallas_call x1, Pallas kernels, img_sum(): pl.pallas_call(_img_sum_kernel, out_shape=jax.ShapeDtypeStruct((count, ro...  20.5 us
    pallas_call x1, Pallas kernels, axis_gather(): pl.pallas_call(functools.partial(_axis_gather_kernel, axis), out_shape=ja...  19.6 us
    all_to_all x1, waiting for transfers between devices, on_device(): lax.all_to_all(jnp.broadcast_to(panels[None], (parts,) + panels.shape), S...  13.3 us
    pallas_call x1, Pallas kernels, pair_gather(): pl.pallas_call(_pair_gather_kernel, out_shape=jax.ShapeDtypeStruct((2,) +...  6.41 us
    pallas_call x1, Pallas kernels, pair_sum(): pl.pallas_call(_pair_sum_kernel, out_shape=jax.ShapeDtypeStruct((half,) +...  5 us
  transfers between devices with their start and end apart: 1, of which 1 were waited for; matrix products, arithmetic and copies ran while one was open for 5% of the time, Pallas kernels for 0%

profile of v19, /device:TPU:6, one launch (start us, length us, event | category | flops | bytes accessed | tf_op | source)
XLA Modules:
  0.0 222.2 jit_solution(6846447656386064838)
XLA Ops:
  0.6 0.0 copy-start
  0.7 1.2 copy-done
  1.9 2.3 %fusion.1.x_ref = f32[64,16,256]{2,1,0:T(8,128)} fusion(bf16[1,64,16,512]{3,2,1,0:T(8,128)(2,1)S(1)} %copy-done, bf16[512,256]{1,0:T(8,128)(2,1)} %param.6), kind=kOutput, calls=%fused_computation.4 | convolution fusion | flops 268435456 | bytes 2359296 | tf_op jit(solution)/shard_map/jpr,rx->jpx/dot_general | solution.py:542
  4.2 35.0 %shard_map.77 = f32[64,16,256]{2,1,0:T(8,128)} custom-call(f32[64,16,256]{2,1,0:T(8,128)} %fusion.1.x_ref), custom_call_target="tpu_custom_call" | custom-call | tf_op jit(solution)/shard_map/pallas_call | solution.py:517
  39.2 0.7 dynamic-slice_bitcast_fusion
  39.9 2.2 convolution_convert_fusion
  42.1 0.6 copy.20
  42.8 19.6 %shard_map.78 = bf16[8,1,128,256]{3,2,1,0:T(8,128)(2,1)} custom-call(bf16[1,128,256]{2,1,0:T(8,128)(2,1)} %bitcast.57), custom_call_target="tpu_custom_call" | custom-call | tf_op jit(solution)/shard_map/pallas_call | solution.py:328
  62.4 2.6 %broadcast_in_dim.5 = bf16[4,8,128,256]{3,2,1,0:T(8,128)(2,1)} broadcast(bf16[8,128,256]{2,1,0:T(8,128)(2,1)} %bitcast.53), dimensions={1,2,3} | broadcast | bytes 2621440 | tf_op jit(solution)/shard_map/broadcast_in_dim | solution.py:556
  65.1 0.0 copy-start.2
  65.1 4.6 %all-to-all-start = ((bf16[4,8,128,256]{3,2,1,0:T(8,128)(2,1)}), bf16[4,8,128,256]{3,2,1,0:T(8,128)(2,1)S(1)}, u32[]{:S(2)}, u32[]{:S(2)}) async-start(bf16[4,8,128,256]{3,2,1,0:T(8,128)(2,1)} %broadcast_in_dim.5), calls=%async_computation | async-start | bytes 4194304 | tf_op jit(solution)/shard_map/all_to_all | solution.py:555
  69.7 0.0 copy-done.2
  69.7 0.1 copy.18
  69.8 0.1 reshape.385
  69.9 0.1 copy.17
  70.0 0.6 reshape_squeeze.3.orient_ref
  70.6 0.1 reshape.377
  70.7 0.0 copy-start.3
  70.7 1.3 gather_fusion
  72.0 0.0 copy-done.3
  72.0 0.1 broadcast_multiply_fusion.2
  72.1 0.1 add_multiply_fusion.2
  72.2 3.1 %fusion.6 = (f32[8,128,128]{2,1,0:T(8,128)}, f32[8,128,128]{2,1,0:T(8,128)}) fusion(f32[8,128]{1,0:T(8,128)S(1)} %get-tuple-element.9, f32[8,128]{1,0:T(8,128)S(1)} %get-tuple-element.8), kind=kLoop, calls=%fused_computation.14 | loop fusion | flops 786432 | bytes 1056768 | tf_op jit(solution)/shard_map/convert_element_type | solution.py:146
  75.3 4.9 %add_negate_fusion.ctf_ref = f32[16,128,128]{2,1,0:T(8,128)} fusion(f32[128,128]{1,0:T(8,128)S(1)} %get-tuple-element.11, f32[128,128]{1,0:T(8,128)S(1)} %get-tuple-element.10, f32[16]{0:T(128)S(1)} %multiply_bitcast_fusion), kind=kLoop, calls=%fused_computation.8 | loop fusion | flops 1572864 | bytes 1179712 | tf_op jit(solution)/shard_map/neg | solution.py:42
  80.1 13.3 %all-to-all-done = bf16[4,8,128,256]{3,2,1,0:T(8,128)(2,1)S(1)} async-done(((bf16[4,8,128,256]{3,2,1,0:T(8,128)(2,1)}), bf16[4,8,128,256]{3,2,1,0:T(8,128)(2,1)S(1)}, u32[]{:S(2)}, u32[]{:S(2)}) %all-to-all-start) | async-done | bytes 2097184 | tf_op jit(solution)/shard_map/all_to_all | solution.py:555
  93.4 6.4 %shard_map.79 = bf16[2,32,128,256]{3,2,1,0:T(8,128)(2,1)} custom-call(bf16[32,128,256]{2,1,0:T(8,128)(2,1)S(1)} %bitcast.50), custom_call_target="tpu_custom_call" | custom-call | tf_op jit(solution)/shard_map/pallas_call | solution.py:366
  99.9 22.7 %shard_map.80 = (f32[16,64,1]{2,1,0:T(8,128)}, bf16[64,128,256]{2,1,0:T(8,128)(2,1)}) custom-call(s32[64]{0:T(128)} %reshape_squeeze.3.orient_ref, s32[64]{0:T(128)} %gather_fusion, bf16[64,128,256]{2,1,0:T(8,128)(2,1)} %bitcast.52, bf16[16,128,256]{2,1,0:T(8,128)(2,1)} %bitcast.55, f32[16,128,128]{2,1,0:T(8,128)} %add_negate_fusion.ctf_ref, ...), custom_call_target="tpu_custom_call" | custom-call | tf_op jit(solution)/shard_map/pallas_call | solution.py:163
  122.6 5.0 %shard_map.81.x_ref = bf16[32,128,256]{2,1,0:T(8,128)(2,1)S(1)} custom-call(bf16[64,128,256]{2,1,0:T(8,128)(2,1)} %get-tuple-element.4.x_ref), custom_call_target="tpu_custom_call" | custom-call | tf_op jit(solution)/shard_map/pallas_call | solution.py:205
  127.6 27.0 %shard_map.82.x_ref = bf16[8,128,256]{2,1,0:T(8,128)(2,1)S(1)} custom-call(bf16[32,128,256]{2,1,0:T(8,128)(2,1)S(1)} %shard_map.81.x_ref), custom_call_target="tpu_custom_call" | custom-call | tf_op jit(solution)/shard_map/pallas_call | solution.py:274
  154.6 17.9 %shard_map.83 = bf16[1,128,256]{2,1,0:T(8,128)(2,1)S(1)} custom-call(bf16[8,128,256]{2,1,0:T(8,128)(2,1)S(1)} %shard_map.82.x_ref), custom_call_target="tpu_custom_call" | custom-call | tf_op jit(solution)/shard_map/pallas_call | solution.py:274
  172.5 0.3 fusion.9
  172.9 1.1 copy.37
  173.9 22.5 %shard_map.84 = bf16[64,16,256]{2,1,0:T(8,128)(2,1)} custom-call(bf16[64,16,256]{2,1,0:T(8,128)(2,1)} %bitcast.54), custom_call_target="tpu_custom_call" | custom-call | tf_op jit(solution)/shard_map/pallas_call | solution.py:517
  196.5 0.0 copy-start.1
  196.5 2.4 %convolution_bitcast_fusion.x_ref = f32[512,256]{1,0:T(8,128)} fusion(bf16[64,16,256]{2,1,0:T(8,128)(2,1)} %shard_map.84, bf16[1,64,16,512]{3,2,1,0:T(8,128)(2,1)S(1)} %copy-done), kind=kOutput, calls=%fused_computation.1 | convolution fusion | flops 268435456 | bytes 2097152 | tf_op jit(solution)/shard_map/jpr,jpx->rx/dot_general | solution.py:575
  198.9 20.5 %shard_map.85 = f32[4,128,256]{2,1,0:T(8,128)} custom-call(f32[512,256]{1,0:T(8,128)} %convolution_bitcast_fusion.x_ref), custom_call_target="tpu_custom_call" | custom-call | tf_op jit(solution)/shard_map/pallas_call | solution.py:438
  219.5 1.9 broadcast_multiply_fusion
  221.3 0.0 copy-done.1
  221.4 0.8 reduce
  (7 shorter events, 0.0 us)
Async XLA Ops:
  0.6 1.2 copy-start
  65.1 4.6 %copy-start.2 = (s32[1,16,4]{1,2,0:T(4,128)S(1)}, s32[1,16,4]{1,2,0:T(4,128)}, u32[]{:S(2)}) copy-start(s32[1,16,4]{1,2,0:T(4,128)} %param.11) | copy-start | bytes 772
  65.1 28.4 %all-to-all-start = ((bf16[4,8,128,256]{3,2,1,0:T(8,128)(2,1)}), bf16[4,8,128,256]{3,2,1,0:T(8,128)(2,1)S(1)}, u32[]{:S(2)}, u32[]{:S(2)}) async-start(bf16[4,8,128,256]{3,2,1,0:T(8,128)(2,1)} %broadcast_in_dim.5), calls=%async_computation | async-start | bytes 4194304 | tf_op jit(solution)/shard_map/all_to_all | solution.py:555
  70.7 1.3 copy-start.3
  196.5 24.9 %copy-start.1 = (f32[16,64,1]{2,1,0:T(8,128)S(1)}, f32[16,64,1]{2,1,0:T(8,128)}, u32[]{:S(2)}) copy-start(f32[16,64,1]{2,1,0:T(8,128)} %get-tuple-element.5) | copy-start | bytes 12292

commit v20 on v18

--- a/solution.py
+++ b/solution.py
@@ -11,6 +11,7 @@
 BOX = 256
 NS = 16
 SLAB = ("sx", "sz", "sc")
+STEP = 2
 
 
 wave_length = 0.0197
@@ -87,43 +88,45 @@
     def _():
         acc_ref[...] = jnp.zeros_like(acc_ref)
 
-    ctf = ctf_ref[0]
-    image = image_ref[0].astype(jnp.float32)
-    ur = ctf * image[:, :half]
-    ui = ctf * image[:, half:]
-    rows = []
-    for k in range(picks):
-        panel = panels_ref[row_ref[i * picks + k]].astype(jnp.float32)
-        pr = panel[:, :half]
-        pi = panel[:, half:]
-        prod_re = (pr * ur + pi * ui).astype(jnp.bfloat16).astype(jnp.float32)
-        prod_im = (pr * ui - pi * ur).astype(jnp.bfloat16).astype(jnp.float32)
-        even = []
-        odd = []
-        for t in range(mirror):
-            even.append(jnp.sum(prod_re * cos_ref[t], axis=0, keepdims=True))
-            odd.append(jnp.sum(prod_im * sin_ref[t], axis=0, keepdims=True))
-        rows.extend(even[t] + odd[t] for t in range(mirror))
-        rows.extend(even[shifts - 1 - t] - odd[shifts - 1 - t] for t in range(mirror, shifts))
-    scores = jnp.sum(jnp.concatenate(rows, axis=0), axis=1, keepdims=True) / half
-    squared = scores * scores
-    mean = jnp.sum(squared, axis=0, keepdims=True) / squared.shape[0]
-    weights = squared / (mean + 1e-05)
-    w_ref[0] = weights
-    wround = weights.astype(jnp.bfloat16).astype(jnp.float32)
-    for k in range(picks):
-        er = jnp.zeros_like(ur)
-        ei = jnp.zeros_like(ur)
-        for t in range(mirror):
-            wt = wround[k * shifts + t : k * shifts + t + 1, :]
-            wm = wround[k * shifts + shifts - 1 - t : k * shifts + shifts - t, :]
-            er = er + (wt + wm) * cos_ref[t]
-            ei = ei - (wt - wm) * sin_ref[t]
-        slice_re = (ur * er - ui * ei).astype(jnp.bfloat16).astype(jnp.float32)
-        slice_im = (ur * ei + ui * er).astype(jnp.bfloat16).astype(jnp.float32)
-        j = row_ref[i * picks + k]
-        acc_ref[j, :, :half] += slice_re
-        acc_ref[j, :, half:] += slice_im
+    for m in range(image_ref.shape[0]):
+        n = i * image_ref.shape[0] + m
+        ctf = ctf_ref[m]
+        image = image_ref[m].astype(jnp.float32)
+        ur = ctf * image[:, :half]
+        ui = ctf * image[:, half:]
+        rows = []
+        for k in range(picks):
+            panel = panels_ref[row_ref[n * picks + k]].astype(jnp.float32)
+            pr = panel[:, :half]
+            pi = panel[:, half:]
+            prod_re = (pr * ur + pi * ui).astype(jnp.bfloat16).astype(jnp.float32)
+            prod_im = (pr * ui - pi * ur).astype(jnp.bfloat16).astype(jnp.float32)
+            even = []
+            odd = []
+            for t in range(mirror):
+                even.append(jnp.sum(prod_re * cos_ref[t], axis=0, keepdims=True))
+                odd.append(jnp.sum(prod_im * sin_ref[t], axis=0, keepdims=True))
+            rows.extend(even[t] + odd[t] for t in range(mirror))
+            rows.extend(even[shifts - 1 - t] - odd[shifts - 1 - t] for t in range(mirror, shifts))
+        scores = jnp.sum(jnp.concatenate(rows, axis=0), axis=1, keepdims=True) / half
+        squared = scores * scores
+        mean = jnp.sum(squared, axis=0, keepdims=True) / squared.shape[0]
+        weights = squared / (mean + 1e-05)
+        w_ref[m] = weights
+        wround = weights.astype(jnp.bfloat16).astype(jnp.float32)
+        for k in range(picks):
+            er = jnp.zeros_like(ur)
+            ei = jnp.zeros_like(ur)
+            for t in range(mirror):
+                wt = wround[k * shifts + t : k * shifts + t + 1, :]
+                wm = wround[k * shifts + shifts - 1 - t : k * shifts + shifts - t, :]
+                er = er + (wt + wm) * cos_ref[t]
+                ei = ei - (wt - wm) * sin_ref[t]
+            slice_re = (ur * er - ui * ei).astype(jnp.bfloat16).astype(jnp.float32)
+            slice_im = (ur * ei + ui * er).astype(jnp.bfloat16).astype(jnp.float32)
+            j = row_ref[n * picks + k]
+            acc_ref[j, :, :half] += slice_re
+            acc_ref[j, :, half:] += slice_im
 
     @pl.when(i == pl.num_programs(0) - 1)
     def _():
@@ -146,16 +149,16 @@
     sin_t = jnp.sin(angle).astype(jnp.bfloat16).astype(jnp.float32)
     grid_spec = pltpu.PrefetchScalarGridSpec(
         num_scalar_prefetch=2,
-        grid=(count,),
+        grid=(count // STEP,),
         in_specs=[
             pl.BlockSpec((orient_count, fourier, width), lambda i, o, w: (0, 0, 0)),
-            pl.BlockSpec((1, fourier, width), lambda i, o, w: (i, 0, 0)),
-            pl.BlockSpec((1, fourier, fourier), lambda i, o, w: (i, 0, 0)),
+            pl.BlockSpec((STEP, fourier, width), lambda i, o, w: (i, 0, 0)),
+            pl.BlockSpec((STEP, fourier, fourier), lambda i, o, w: (i, 0, 0)),
             pl.BlockSpec((NS // 2, fourier, fourier), lambda i, o, w: (0, 0, 0)),
             pl.BlockSpec((NS // 2, fourier, fourier), lambda i, o, w: (0, 0, 0)),
         ],
         out_specs=[
-            pl.BlockSpec((1, picks * NS, 1), lambda i, o, w: (i, 0, 0)),
+            pl.BlockSpec((STEP, picks * NS, 1), lambda i, o, w: (i, 0, 0)),
             pl.BlockSpec((orient_count, fourier, width), lambda i, o, w: (0, 0, 0)),
         ],
         scratch_shapes=[pltpu.VMEM((orient_count, fourier, width), jnp.float32)],

time: 221 us -> 219 us (level)
  no operation moved by 1% of the time
where the time goes in v20:
time: 219 us
  Pallas kernels  173 us (79%)
  waiting for transfers between devices  13.3 us (6%)
  other arithmetic  10.8 us (5%)
  local copies, waits for them, and re-layouts  8.55 us (4%)
  matrix products  7.32 us (3%)
  starting transfers between devices  4.64 us (2%)
    pallas_call x2, Pallas kernels, slab_all_to_all(): pl.pallas_call(_a2a_kernel, out_shape=jax.ShapeDtypeStruct(x.shape, x.dty...  55.9 us
    pallas_call x2, Pallas kernels, axis_sum(): pl.pallas_call(functools.partial(_axis_sum_kernel, axis), out_shape=jax.S...  44.9 us
    pallas_call x1, Pallas kernels, correlate_all(): pl.pallas_call(_correlate_kernel, grid_spec=grid_spec, out_shape=[jax.Sha...  21.1 us
    pallas_call x1, Pallas kernels, img_sum(): pl.pallas_call(_img_sum_kernel, out_shape=jax.ShapeDtypeStruct((count, ro...  20.5 us
    pallas_call x1, Pallas kernels, axis_gather(): pl.pallas_call(functools.partial(_axis_gather_kernel, axis), out_shape=ja...  19.6 us
    all_to_all x1, waiting for transfers between devices, on_device(): lax.all_to_all(jnp.broadcast_to(panels[None], (parts,) + panels.shape), S...  13.3 us
    pallas_call x1, Pallas kernels, pair_gather(): pl.pallas_call(_pair_gather_kernel, out_shape=jax.ShapeDtypeStruct((2,) +...  6.41 us
    pallas_call x1, Pallas kernels, pair_sum(): pl.pallas_call(_pair_sum_kernel, out_shape=jax.ShapeDtypeStruct((half,) +...  5 us
  transfers between devices with their start and end apart: 1, of which 1 were waited for; matrix products, arithmetic and copies ran while one was open for 5% of the time, Pallas kernels for 0%

profile of v20, /device:TPU:6, one launch (start us, length us, event | category | flops | bytes accessed | tf_op | source)
XLA Modules:
  0.0 218.9 jit_solution(15825168724177966041)
XLA Ops:
  0.6 0.0 copy-start
  0.7 1.2 copy-done
  1.9 2.3 %fusion.1.x_ref = f32[64,16,256]{2,1,0:T(8,128)} fusion(bf16[1,64,16,512]{3,2,1,0:T(8,128)(2,1)S(1)} %copy-done, bf16[512,256]{1,0:T(8,128)(2,1)} %param.6), kind=kOutput, calls=%fused_computation.4 | convolution fusion | flops 268435456 | bytes 2359296 | tf_op jit(solution)/shard_map/jpr,rx->jpx/dot_general | solution.py:545
  4.2 34.1 %shard_map.77 = f32[64,16,256]{2,1,0:T(8,128)} custom-call(f32[64,16,256]{2,1,0:T(8,128)} %fusion.1.x_ref), custom_call_target="tpu_custom_call" | custom-call | tf_op jit(solution)/shard_map/pallas_call | solution.py:520
  38.3 0.7 dynamic-slice_bitcast_fusion
  39.0 2.2 %convolution_convert_fusion = bf16[8,16,256]{2,0,1:T(8,128)(2,1)S(1)} fusion(f32[64,16,256]{2,1,0:T(8,128)} %shard_map.77, s32[64]{0:T(128)S(1)} %dynamic-slice_bitcast_fusion), kind=kOutput, calls=%fused_computation.2 | convolution fusion | flops 25199104 | bytes 1114368 | tf_op jit(solution)/shard_map/osb,sopx->obpx/dot_general | solution.py:551
  41.2 0.6 copy.20
  41.9 19.6 %shard_map.78 = bf16[8,1,128,256]{3,2,1,0:T(8,128)(2,1)} custom-call(bf16[1,128,256]{2,1,0:T(8,128)(2,1)} %bitcast.57), custom_call_target="tpu_custom_call" | custom-call | tf_op jit(solution)/shard_map/pallas_call | solution.py:331
  61.5 2.6 %broadcast_in_dim.5 = bf16[4,8,128,256]{3,2,1,0:T(8,128)(2,1)} broadcast(bf16[8,128,256]{2,1,0:T(8,128)(2,1)} %bitcast.53), dimensions={1,2,3} | broadcast | bytes 2621440 | tf_op jit(solution)/shard_map/broadcast_in_dim | solution.py:559
  64.2 0.0 copy-start.2
  64.2 4.6 %all-to-all-start = ((bf16[4,8,128,256]{3,2,1,0:T(8,128)(2,1)}), bf16[4,8,128,256]{3,2,1,0:T(8,128)(2,1)S(1)}, u32[]{:S(2)}, u32[]{:S(2)}) async-start(bf16[4,8,128,256]{3,2,1,0:T(8,128)(2,1)} %broadcast_in_dim.5), calls=%async_computation | async-start | bytes 4194304 | tf_op jit(solution)/shard_map/all_to_all | solution.py:558
  68.8 0.0 copy-done.2
  68.8 0.1 copy.18
  68.9 0.1 reshape.385
  69.0 0.1 copy.17
  69.1 0.6 reshape_squeeze.3.orient_ref
  69.7 0.1 reshape.377
  69.8 0.0 copy-start.3
  69.8 1.3 gather_fusion
  71.1 0.0 copy-done.3
  71.1 0.1 broadcast_multiply_fusion.2
  71.2 0.1 add_multiply_fusion.2
  71.3 3.1 %fusion.6 = (f32[8,128,128]{2,1,0:T(8,128)}, f32[8,128,128]{2,1,0:T(8,128)}) fusion(f32[8,128]{1,0:T(8,128)S(1)} %get-tuple-element.9, f32[8,128]{1,0:T(8,128)S(1)} %get-tuple-element.8), kind=kLoop, calls=%fused_computation.14 | loop fusion | flops 786432 | bytes 1056768 | tf_op jit(solution)/shard_map/convert_element_type | solution.py:149
  74.4 4.9 %add_negate_fusion.ctf_ref = f32[16,128,128]{2,1,0:T(8,128)} fusion(f32[128,128]{1,0:T(8,128)S(1)} %get-tuple-element.11, f32[128,128]{1,0:T(8,128)S(1)} %get-tuple-element.10, f32[16]{0:T(128)S(1)} %multiply_bitcast_fusion), kind=kLoop, calls=%fused_computation.8 | loop fusion | flops 1572864 | bytes 1179712 | tf_op jit(solution)/shard_map/neg | solution.py:43
  79.2 13.3 %all-to-all-done = bf16[4,8,128,256]{3,2,1,0:T(8,128)(2,1)S(1)} async-done(((bf16[4,8,128,256]{3,2,1,0:T(8,128)(2,1)}), bf16[4,8,128,256]{3,2,1,0:T(8,128)(2,1)S(1)}, u32[]{:S(2)}, u32[]{:S(2)}) %all-to-all-start) | async-done | bytes 2097184 | tf_op jit(solution)/shard_map/all_to_all | solution.py:558
  92.6 6.4 %shard_map.79 = bf16[2,32,128,256]{3,2,1,0:T(8,128)(2,1)} custom-call(bf16[32,128,256]{2,1,0:T(8,128)(2,1)S(1)} %bitcast.50), custom_call_target="tpu_custom_call" | custom-call | tf_op jit(solution)/shard_map/pallas_call | solution.py:369
  99.0 21.1 %shard_map.80 = (f32[16,64,1]{2,1,0:T(8,128)}, bf16[64,128,256]{2,1,0:T(8,128)(2,1)}) custom-call(s32[64]{0:T(128)} %reshape_squeeze.3.orient_ref, s32[64]{0:T(128)} %gather_fusion, bf16[64,128,256]{2,1,0:T(8,128)(2,1)} %bitcast.52, bf16[16,128,256]{2,1,0:T(8,128)(2,1)} %bitcast.55, f32[16,128,128]{2,1,0:T(8,128)} %add_negate_fusion.ctf_ref, ...), custom_call_target="tpu_custom_call" | custom-call | tf_op jit(solution)/shard_map/pallas_call | solution.py:166
  120.1 5.0 %shard_map.81.x_ref = bf16[32,128,256]{2,1,0:T(8,128)(2,1)S(1)} custom-call(bf16[64,128,256]{2,1,0:T(8,128)(2,1)} %get-tuple-element.4.x_ref), custom_call_target="tpu_custom_call" | custom-call | tf_op jit(solution)/shard_map/pallas_call | solution.py:208
  125.1 27.0 %shard_map.82.x_ref = bf16[8,128,256]{2,1,0:T(8,128)(2,1)S(1)} custom-call(bf16[32,128,256]{2,1,0:T(8,128)(2,1)S(1)} %shard_map.81.x_ref), custom_call_target="tpu_custom_call" | custom-call | tf_op jit(solution)/shard_map/pallas_call | solution.py:277
  152.1 17.9 %shard_map.83 = bf16[1,128,256]{2,1,0:T(8,128)(2,1)S(1)} custom-call(bf16[8,128,256]{2,1,0:T(8,128)(2,1)S(1)} %shard_map.82.x_ref), custom_call_target="tpu_custom_call" | custom-call | tf_op jit(solution)/shard_map/pallas_call | solution.py:277
  170.0 0.3 fusion.9
  170.3 1.1 copy.37
  171.4 21.8 %shard_map.84 = bf16[64,16,256]{2,1,0:T(8,128)(2,1)} custom-call(bf16[64,16,256]{2,1,0:T(8,128)(2,1)} %bitcast.54), custom_call_target="tpu_custom_call" | custom-call | tf_op jit(solution)/shard_map/pallas_call | solution.py:520
  193.2 0.0 copy-start.1
  193.2 2.4 %convolution_bitcast_fusion.x_ref = f32[512,256]{1,0:T(8,128)} fusion(bf16[64,16,256]{2,1,0:T(8,128)(2,1)} %shard_map.84, bf16[1,64,16,512]{3,2,1,0:T(8,128)(2,1)S(1)} %copy-done), kind=kOutput, calls=%fused_computation.1 | convolution fusion | flops 268435456 | bytes 2097152 | tf_op jit(solution)/shard_map/jpr,jpx->rx/dot_general | solution.py:578
  195.6 20.5 %shard_map.85 = f32[4,128,256]{2,1,0:T(8,128)} custom-call(f32[512,256]{1,0:T(8,128)} %convolution_bitcast_fusion.x_ref), custom_call_target="tpu_custom_call" | custom-call | tf_op jit(solution)/shard_map/pallas_call | solution.py:441
  216.2 1.9 broadcast_multiply_fusion
  218.1 0.0 copy-done.1
  218.1 0.8 reduce
  (7 shorter events, 0.0 us)
Async XLA Ops:
  0.6 1.2 copy-start
  64.2 4.6 %copy-start.2 = (s32[1,16,4]{1,2,0:T(4,128)S(1)}, s32[1,16,4]{1,2,0:T(4,128)}, u32[]{:S(2)}) copy-start(s32[1,16,4]{1,2,0:T(4,128)} %param.11) | copy-start | bytes 772
  64.2 28.4 %all-to-all-start = ((bf16[4,8,128,256]{3,2,1,0:T(8,128)(2,1)}), bf16[4,8,128,256]{3,2,1,0:T(8,128)(2,1)S(1)}, u32[]{:S(2)}, u32[]{:S(2)}) async-start(bf16[4,8,128,256]{3,2,1,0:T(8,128)(2,1)} %broadcast_in_dim.5), calls=%async_computation | async-start | bytes 4194304 | tf_op jit(solution)/shard_map/all_to_all | solution.py:558
  69.8 1.3 copy-start.3
  193.2 24.9 %copy-start.1 = (f32[16,64,1]{2,1,0:T(8,128)S(1)}, f32[16,64,1]{2,1,0:T(8,128)}, u32[]{:S(2)}) copy-start(f32[16,64,1]{2,1,0:T(8,128)} %get-tuple-element.5) | copy-start | bytes 12292

commit v21 on v20

--- a/solution.py
+++ b/solution.py
@@ -11,7 +11,7 @@
 BOX = 256
 NS = 16
 SLAB = ("sx", "sz", "sc")
-STEP = 2
+STEP = 4
 
 
 wave_length = 0.0197

time: 219 us -> 219 us (level)
  no operation moved by 1% of the time
where the time goes in v21:
time: 219 us
  Pallas kernels  173 us (79%)
  waiting for transfers between devices  13.3 us (6%)
  other arithmetic  10.8 us (5%)
  local copies, waits for them, and re-layouts  8.55 us (4%)
  matrix products  7.32 us (3%)
  starting transfers between devices  4.64 us (2%)
    pallas_call x2, Pallas kernels, slab_all_to_all(): pl.pallas_call(_a2a_kernel, out_shape=jax.ShapeDtypeStruct(x.shape, x.dty...  56 us
    pallas_call x2, Pallas kernels, axis_sum(): pl.pallas_call(functools.partial(_axis_sum_kernel, axis), out_shape=jax.S...  44.9 us
    pallas_call x1, Pallas kernels, correlate_all(): pl.pallas_call(_correlate_kernel, grid_spec=grid_spec, out_shape=[jax.Sha...  20.9 us
    pallas_call x1, Pallas kernels, img_sum(): pl.pallas_call(_img_sum_kernel, out_shape=jax.ShapeDtypeStruct((count, ro...  20.6 us
    pallas_call x1, Pallas kernels, axis_gather(): pl.pallas_call(functools.partial(_axis_gather_kernel, axis), out_shape=ja...  19.5 us
    all_to_all x1, waiting for transfers between devices, on_device(): lax.all_to_all(jnp.broadcast_to(panels[None], (parts,) + panels.shape), S...  13.3 us
    pallas_call x1, Pallas kernels, pair_gather(): pl.pallas_call(_pair_gather_kernel, out_shape=jax.ShapeDtypeStruct((2,) +...  6.41 us
    pallas_call x1, Pallas kernels, pair_sum(): pl.pallas_call(_pair_sum_kernel, out_shape=jax.ShapeDtypeStruct((half,) +...  5 us
  transfers between devices with their start and end apart: 1, of which 1 were waited for; matrix products, arithmetic and copies ran while one was open for 5% of the time, Pallas kernels for 0%

profile of v21, /device:TPU:6, one launch (start us, length us, event | category | flops | bytes accessed | tf_op | source)
XLA Modules:
  0.0 218.7 jit_solution(9486316859115921926)
XLA Ops:
  0.6 0.0 copy-start
  0.7 1.2 copy-done
  1.9 2.4 %fusion.1.x_ref = f32[64,16,256]{2,1,0:T(8,128)} fusion(bf16[1,64,16,512]{3,2,1,0:T(8,128)(2,1)S(1)} %copy-done, bf16[512,256]{1,0:T(8,128)(2,1)} %param.6), kind=kOutput, calls=%fused_computation.4 | convolution fusion | flops 268435456 | bytes 2359296 | tf_op jit(solution)/shard_map/jpr,rx->jpx/dot_general | solution.py:545
  4.2 34.2 %shard_map.77 = f32[64,16,256]{2,1,0:T(8,128)} custom-call(f32[64,16,256]{2,1,0:T(8,128)} %fusion.1.x_ref), custom_call_target="tpu_custom_call" | custom-call | tf_op jit(solution)/shard_map/pallas_call | solution.py:520
  38.4 0.7 dynamic-slice_bitcast_fusion
  39.1 2.2 %convolution_convert_fusion = bf16[8,16,256]{2,0,1:T(8,128)(2,1)S(1)} fusion(f32[64,16,256]{2,1,0:T(8,128)} %shard_map.77, s32[64]{0:T(128)S(1)} %dynamic-slice_bitcast_fusion), kind=kOutput, calls=%fused_computation.2 | convolution fusion | flops 25199104 | bytes 1114368 | tf_op jit(solution)/shard_map/osb,sopx->obpx/dot_general | solution.py:551
  41.3 0.6 copy.20
  42.0 19.5 %shard_map.78 = bf16[8,1,128,256]{3,2,1,0:T(8,128)(2,1)} custom-call(bf16[1,128,256]{2,1,0:T(8,128)(2,1)} %bitcast.57), custom_call_target="tpu_custom_call" | custom-call | tf_op jit(solution)/shard_map/pallas_call | solution.py:331
  61.5 2.6 %broadcast_in_dim.5 = bf16[4,8,128,256]{3,2,1,0:T(8,128)(2,1)} broadcast(bf16[8,128,256]{2,1,0:T(8,128)(2,1)} %bitcast.53), dimensions={1,2,3} | broadcast | bytes 2621440 | tf_op jit(solution)/shard_map/broadcast_in_dim | solution.py:559
  64.2 0.0 copy-start.2
  64.2 4.6 %all-to-all-start = ((bf16[4,8,128,256]{3,2,1,0:T(8,128)(2,1)}), bf16[4,8,128,256]{3,2,1,0:T(8,128)(2,1)S(1)}, u32[]{:S(2)}, u32[]{:S(2)}) async-start(bf16[4,8,128,256]{3,2,1,0:T(8,128)(2,1)} %broadcast_in_dim.5), calls=%async_computation | async-start | bytes 4194304 | tf_op jit(solution)/shard_map/all_to_all | solution.py:558
  68.8 0.0 copy-done.2
  68.8 0.1 copy.18
  68.9 0.1 reshape.385
  69.0 0.1 copy.17
  69.1 0.6 reshape_squeeze.3.orient_ref
  69.7 0.1 reshape.377
  69.8 0.0 copy-start.3
  69.8 1.3 gather_fusion
  71.1 0.0 copy-done.3
  71.1 0.1 broadcast_multiply_fusion.2
  71.2 0.1 add_multiply_fusion.2
  71.3 3.1 %fusion.6 = (f32[8,128,128]{2,1,0:T(8,128)}, f32[8,128,128]{2,1,0:T(8,128)}) fusion(f32[8,128]{1,0:T(8,128)S(1)} %get-tuple-element.9, f32[8,128]{1,0:T(8,128)S(1)} %get-tuple-element.8), kind=kLoop, calls=%fused_computation.14 | loop fusion | flops 786432 | bytes 1056768 | tf_op jit(solution)/shard_map/convert_element_type | solution.py:149
  74.4 4.9 %add_negate_fusion.ctf_ref = f32[16,128,128]{2,1,0:T(8,128)} fusion(f32[128,128]{1,0:T(8,128)S(1)} %get-tuple-element.11, f32[128,128]{1,0:T(8,128)S(1)} %get-tuple-element.10, f32[16]{0:T(128)S(1)} %multiply_bitcast_fusion), kind=kLoop, calls=%fused_computation.8 | loop fusion | flops 1572864 | bytes 1179712 | tf_op jit(solution)/shard_map/neg | solution.py:43
  79.2 13.3 %all-to-all-done = bf16[4,8,128,256]{3,2,1,0:T(8,128)(2,1)S(1)} async-done(((bf16[4,8,128,256]{3,2,1,0:T(8,128)(2,1)}), bf16[4,8,128,256]{3,2,1,0:T(8,128)(2,1)S(1)}, u32[]{:S(2)}, u32[]{:S(2)}) %all-to-all-start) | async-done | bytes 2097184 | tf_op jit(solution)/shard_map/all_to_all | solution.py:558
  92.6 6.4 %shard_map.79 = bf16[2,32,128,256]{3,2,1,0:T(8,128)(2,1)} custom-call(bf16[32,128,256]{2,1,0:T(8,128)(2,1)S(1)} %bitcast.50), custom_call_target="tpu_custom_call" | custom-call | tf_op jit(solution)/shard_map/pallas_call | solution.py:369
  99.0 20.9 %shard_map.80 = (f32[16,64,1]{2,1,0:T(8,128)}, bf16[64,128,256]{2,1,0:T(8,128)(2,1)}) custom-call(s32[64]{0:T(128)} %reshape_squeeze.3.orient_ref, s32[64]{0:T(128)} %gather_fusion, bf16[64,128,256]{2,1,0:T(8,128)(2,1)} %bitcast.52, bf16[16,128,256]{2,1,0:T(8,128)(2,1)} %bitcast.55, f32[16,128,128]{2,1,0:T(8,128)} %add_negate_fusion.ctf_ref, ...), custom_call_target="tpu_custom_call" | custom-call | tf_op jit(solution)/shard_map/pallas_call | solution.py:166
  119.8 5.0 %shard_map.81.x_ref = bf16[32,128,256]{2,1,0:T(8,128)(2,1)S(1)} custom-call(bf16[64,128,256]{2,1,0:T(8,128)(2,1)} %get-tuple-element.4.x_ref), custom_call_target="tpu_custom_call" | custom-call | tf_op jit(solution)/shard_map/pallas_call | solution.py:208
  124.9 27.0 %shard_map.82.x_ref = bf16[8,128,256]{2,1,0:T(8,128)(2,1)S(1)} custom-call(bf16[32,128,256]{2,1,0:T(8,128)(2,1)S(1)} %shard_map.81.x_ref), custom_call_target="tpu_custom_call" | custom-call | tf_op jit(solution)/shard_map/pallas_call | solution.py:277
  151.9 17.9 %shard_map.83 = bf16[1,128,256]{2,1,0:T(8,128)(2,1)S(1)} custom-call(bf16[8,128,256]{2,1,0:T(8,128)(2,1)S(1)} %shard_map.82.x_ref), custom_call_target="tpu_custom_call" | custom-call | tf_op jit(solution)/shard_map/pallas_call | solution.py:277
  169.7 0.3 fusion.9
  170.1 1.1 copy.37
  171.2 21.8 %shard_map.84 = bf16[64,16,256]{2,1,0:T(8,128)(2,1)} custom-call(bf16[64,16,256]{2,1,0:T(8,128)(2,1)} %bitcast.54), custom_call_target="tpu_custom_call" | custom-call | tf_op jit(solution)/shard_map/pallas_call | solution.py:520
  193.0 0.0 copy-start.1
  193.0 2.4 %convolution_bitcast_fusion.x_ref = f32[512,256]{1,0:T(8,128)} fusion(bf16[64,16,256]{2,1,0:T(8,128)(2,1)} %shard_map.84, bf16[1,64,16,512]{3,2,1,0:T(8,128)(2,1)S(1)} %copy-done), kind=kOutput, calls=%fused_computation.1 | convolution fusion | flops 268435456 | bytes 2097152 | tf_op jit(solution)/shard_map/jpr,jpx->rx/dot_general | solution.py:578
  195.4 20.6 %shard_map.85 = f32[4,128,256]{2,1,0:T(8,128)} custom-call(f32[512,256]{1,0:T(8,128)} %convolution_bitcast_fusion.x_ref), custom_call_target="tpu_custom_call" | custom-call | tf_op jit(solution)/shard_map/pallas_call | solution.py:441
  216.0 1.9 broadcast_multiply_fusion
  217.9 0.0 copy-done.1
  217.9 0.8 reduce
  (7 shorter events, 0.0 us)
Async XLA Ops:
  0.6 1.2 copy-start
  64.2 4.6 %copy-start.2 = (s32[1,16,4]{1,2,0:T(4,128)S(1)}, s32[1,16,4]{1,2,0:T(4,128)}, u32[]{:S(2)}) copy-start(s32[1,16,4]{1,2,0:T(4,128)} %param.11) | copy-start | bytes 772
  64.2 28.4 %all-to-all-start = ((bf16[4,8,128,256]{3,2,1,0:T(8,128)(2,1)}), bf16[4,8,128,256]{3,2,1,0:T(8,128)(2,1)S(1)}, u32[]{:S(2)}, u32[]{:S(2)}) async-start(bf16[4,8,128,256]{3,2,1,0:T(8,128)(2,1)} %broadcast_in_dim.5), calls=%async_computation | async-start | bytes 4194304 | tf_op jit(solution)/shard_map/all_to_all | solution.py:558
  69.8 1.3 copy-start.3
  193.0 24.9 %copy-start.1 = (f32[16,64,1]{2,1,0:T(8,128)S(1)}, f32[16,64,1]{2,1,0:T(8,128)}, u32[]{:S(2)}) copy-start(f32[16,64,1]{2,1,0:T(8,128)} %get-tuple-element.5) | copy-start | bytes 12292

commit v22 on v21

--- a/solution.py
+++ b/solution.py
@@ -11,7 +11,7 @@
 BOX = 256
 NS = 16
 SLAB = ("sx", "sz", "sc")
-STEP = 4
+STEP = 8
 
 
 wave_length = 0.0197

time: 219 us -> 219 us (level)
  no operation moved by 1% of the time
where the time goes in v22:
time: 219 us
  Pallas kernels  173 us (79%)
  waiting for transfers between devices  13.3 us (6%)
  other arithmetic  10.8 us (5%)
  local copies, waits for them, and re-layouts  8.55 us (4%)
  matrix products  7.32 us (3%)
  starting transfers between devices  4.64 us (2%)
    pallas_call x2, Pallas kernels, slab_all_to_all(): pl.pallas_call(_a2a_kernel, out_shape=jax.ShapeDtypeStruct(x.shape, x.dty...  56 us
    pallas_call x2, Pallas kernels, axis_sum(): pl.pallas_call(functools.partial(_axis_sum_kernel, axis), out_shape=jax.S...  44.9 us
    pallas_call x1, Pallas kernels, correlate_all(): pl.pallas_call(_correlate_kernel, grid_spec=grid_spec, out_shape=[jax.Sha...  21 us
    pallas_call x1, Pallas kernels, img_sum(): pl.pallas_call(_img_sum_kernel, out_shape=jax.ShapeDtypeStruct((count, ro...  20.6 us
    pallas_call x1, Pallas kernels, axis_gather(): pl.pallas_call(functools.partial(_axis_gather_kernel, axis), out_shape=ja...  19.5 us
    all_to_all x1, waiting for transfers between devices, on_device(): lax.all_to_all(jnp.broadcast_to(panels[None], (parts,) + panels.shape), S...  13.3 us
    pallas_call x1, Pallas kernels, pair_gather(): pl.pallas_call(_pair_gather_kernel, out_shape=jax.ShapeDtypeStruct((2,) +...  6.41 us
    pallas_call x1, Pallas kernels, pair_sum(): pl.pallas_call(_pair_sum_kernel, out_shape=jax.ShapeDtypeStruct((half,) +...  5 us
  transfers between devices with their start and end apart: 1, of which 1 were waited for; matrix products, arithmetic and copies ran while one was open for 5% of the time, Pallas kernels for 0%

profile of v22, /device:TPU:6, one launch (start us, length us, event | category | flops | bytes accessed | tf_op | source)
XLA Modules:
  0.0 218.8 jit_solution(14225377396471835057)
XLA Ops:
  0.6 0.0 copy-start
  0.7 1.2 copy-done
  1.9 2.4 %fusion.1.x_ref = f32[64,16,256]{2,1,0:T(8,128)} fusion(bf16[1,64,16,512]{3,2,1,0:T(8,128)(2,1)S(1)} %copy-done, bf16[512,256]{1,0:T(8,128)(2,1)} %param.6), kind=kOutput, calls=%fused_computation.4 | convolution fusion | flops 268435456 | bytes 2359296 | tf_op jit(solution)/shard_map/jpr,rx->jpx/dot_general | solution.py:545
  4.2 34.2 %shard_map.77 = f32[64,16,256]{2,1,0:T(8,128)} custom-call(f32[64,16,256]{2,1,0:T(8,128)} %fusion.1.x_ref), custom_call_target="tpu_custom_call" | custom-call | tf_op jit(solution)/shard_map/pallas_call | solution.py:520
  38.4 0.7 dynamic-slice_bitcast_fusion
  39.1 2.2 %convolution_convert_fusion = bf16[8,16,256]{2,0,1:T(8,128)(2,1)S(1)} fusion(f32[64,16,256]{2,1,0:T(8,128)} %shard_map.77, s32[64]{0:T(128)S(1)} %dynamic-slice_bitcast_fusion), kind=kOutput, calls=%fused_computation.2 | convolution fusion | flops 25199104 | bytes 1114368 | tf_op jit(solution)/shard_map/osb,sopx->obpx/dot_general | solution.py:551
  41.3 0.6 copy.20
  42.0 19.5 %shard_map.78 = bf16[8,1,128,256]{3,2,1,0:T(8,128)(2,1)} custom-call(bf16[1,128,256]{2,1,0:T(8,128)(2,1)} %bitcast.57), custom_call_target="tpu_custom_call" | custom-call | tf_op jit(solution)/shard_map/pallas_call | solution.py:331
  61.5 2.6 %broadcast_in_dim.5 = bf16[4,8,128,256]{3,2,1,0:T(8,128)(2,1)} broadcast(bf16[8,128,256]{2,1,0:T(8,128)(2,1)} %bitcast.53), dimensions={1,2,3} | broadcast | bytes 2621440 | tf_op jit(solution)/shard_map/broadcast_in_dim | solution.py:559
  64.2 0.0 copy-start.2
  64.2 4.6 %all-to-all-start = ((bf16[4,8,128,256]{3,2,1,0:T(8,128)(2,1)}), bf16[4,8,128,256]{3,2,1,0:T(8,128)(2,1)S(1)}, u32[]{:S(2)}, u32[]{:S(2)}) async-start(bf16[4,8,128,256]{3,2,1,0:T(8,128)(2,1)} %broadcast_in_dim.5), calls=%async_computation | async-start | bytes 4194304 | tf_op jit(solution)/shard_map/all_to_all | solution.py:558
  68.8 0.0 copy-done.2
  68.8 0.1 copy.18
  68.9 0.1 reshape.385
  69.0 0.1 copy.17
  69.1 0.6 reshape_squeeze.3.orient_ref
  69.7 0.1 reshape.377
  69.8 0.0 copy-start.3
  69.8 1.3 gather_fusion
  71.1 0.0 copy-done.3
  71.1 0.1 broadcast_multiply_fusion.2
  71.2 0.1 add_multiply_fusion.2
  71.3 3.1 %fusion.6 = (f32[8,128,128]{2,1,0:T(8,128)}, f32[8,128,128]{2,1,0:T(8,128)}) fusion(f32[8,128]{1,0:T(8,128)S(1)} %get-tuple-element.9, f32[8,128]{1,0:T(8,128)S(1)} %get-tuple-element.8), kind=kLoop, calls=%fused_computation.14 | loop fusion | flops 786432 | bytes 1056768 | tf_op jit(solution)/shard_map/convert_element_type | solution.py:149
  74.4 4.9 %add_negate_fusion.ctf_ref = f32[16,128,128]{2,1,0:T(8,128)} fusion(f32[128,128]{1,0:T(8,128)S(1)} %get-tuple-element.11, f32[128,128]{1,0:T(8,128)S(1)} %get-tuple-element.10, f32[16]{0:T(128)S(1)} %multiply_bitcast_fusion), kind=kLoop, calls=%fused_computation.8 | loop fusion | flops 1572864 | bytes 1179712 | tf_op jit(solution)/shard_map/neg | solution.py:43
  79.2 13.3 %all-to-all-done = bf16[4,8,128,256]{3,2,1,0:T(8,128)(2,1)S(1)} async-done(((bf16[4,8,128,256]{3,2,1,0:T(8,128)(2,1)}), bf16[4,8,128,256]{3,2,1,0:T(8,128)(2,1)S(1)}, u32[]{:S(2)}, u32[]{:S(2)}) %all-to-all-start) | async-done | bytes 2097184 | tf_op jit(solution)/shard_map/all_to_all | solution.py:558
  92.6 6.4 %shard_map.79 = bf16[2,32,128,256]{3,2,1,0:T(8,128)(2,1)} custom-call(bf16[32,128,256]{2,1,0:T(8,128)(2,1)S(1)} %bitcast.50), custom_call_target="tpu_custom_call" | custom-call | tf_op jit(solution)/shard_map/pallas_call | solution.py:369
  99.0 21.0 %shard_map.80 = (f32[16,64,1]{2,1,0:T(8,128)}, bf16[64,128,256]{2,1,0:T(8,128)(2,1)}) custom-call(s32[64]{0:T(128)} %reshape_squeeze.3.orient_ref, s32[64]{0:T(128)} %gather_fusion, bf16[64,128,256]{2,1,0:T(8,128)(2,1)} %bitcast.52, bf16[16,128,256]{2,1,0:T(8,128)(2,1)} %bitcast.55, f32[16,128,128]{2,1,0:T(8,128)} %add_negate_fusion.ctf_ref, ...), custom_call_target="tpu_custom_call" | custom-call | tf_op jit(solution)/shard_map/pallas_call | solution.py:166
  120.0 5.0 %shard_map.81.x_ref = bf16[32,128,256]{2,1,0:T(8,128)(2,1)S(1)} custom-call(bf16[64,128,256]{2,1,0:T(8,128)(2,1)} %get-tuple-element.4.x_ref), custom_call_target="tpu_custom_call" | custom-call | tf_op jit(solution)/shard_map/pallas_call | solution.py:208
  125.0 27.0 %shard_map.82.x_ref = bf16[8,128,256]{2,1,0:T(8,128)(2,1)S(1)} custom-call(bf16[32,128,256]{2,1,0:T(8,128)(2,1)S(1)} %shard_map.81.x_ref), custom_call_target="tpu_custom_call" | custom-call | tf_op jit(solution)/shard_map/pallas_call | solution.py:277
  152.0 17.9 %shard_map.83 = bf16[1,128,256]{2,1,0:T(8,128)(2,1)S(1)} custom-call(bf16[8,128,256]{2,1,0:T(8,128)(2,1)S(1)} %shard_map.82.x_ref), custom_call_target="tpu_custom_call" | custom-call | tf_op jit(solution)/shard_map/pallas_call | solution.py:277
  169.9 0.3 fusion.9
  170.2 1.1 copy.37
  171.3 21.8 %shard_map.84 = bf16[64,16,256]{2,1,0:T(8,128)(2,1)} custom-call(bf16[64,16,256]{2,1,0:T(8,128)(2,1)} %bitcast.54), custom_call_target="tpu_custom_call" | custom-call | tf_op jit(solution)/shard_map/pallas_call | solution.py:520
  193.1 0.0 copy-start.1
  193.1 2.4 %convolution_bitcast_fusion.x_ref = f32[512,256]{1,0:T(8,128)} fusion(bf16[64,16,256]{2,1,0:T(8,128)(2,1)} %shard_map.84, bf16[1,64,16,512]{3,2,1,0:T(8,128)(2,1)S(1)} %copy-done), kind=kOutput, calls=%fused_computation.1 | convolution fusion | flops 268435456 | bytes 2097152 | tf_op jit(solution)/shard_map/jpr,jpx->rx/dot_general | solution.py:578
  195.5 20.6 %shard_map.85 = f32[4,128,256]{2,1,0:T(8,128)} custom-call(f32[512,256]{1,0:T(8,128)} %convolution_bitcast_fusion.x_ref), custom_call_target="tpu_custom_call" | custom-call | tf_op jit(solution)/shard_map/pallas_call | solution.py:441
  216.1 1.9 broadcast_multiply_fusion
  218.0 0.0 copy-done.1
  218.0 0.8 reduce
  (7 shorter events, 0.0 us)
Async XLA Ops:
  0.6 1.2 copy-start
  64.2 4.6 %copy-start.2 = (s32[1,16,4]{1,2,0:T(4,128)S(1)}, s32[1,16,4]{1,2,0:T(4,128)}, u32[]{:S(2)}) copy-start(s32[1,16,4]{1,2,0:T(4,128)} %param.11) | copy-start | bytes 772
  64.2 28.4 %all-to-all-start = ((bf16[4,8,128,256]{3,2,1,0:T(8,128)(2,1)}), bf16[4,8,128,256]{3,2,1,0:T(8,128)(2,1)S(1)}, u32[]{:S(2)}, u32[]{:S(2)}) async-start(bf16[4,8,128,256]{3,2,1,0:T(8,128)(2,1)} %broadcast_in_dim.5), calls=%async_computation | async-start | bytes 4194304 | tf_op jit(solution)/shard_map/all_to_all | solution.py:558
  69.8 1.3 copy-start.3
  193.1 24.9 %copy-start.1 = (f32[16,64,1]{2,1,0:T(8,128)S(1)}, f32[16,64,1]{2,1,0:T(8,128)}, u32[]{:S(2)}) copy-start(f32[16,64,1]{2,1,0:T(8,128)} %get-tuple-element.5) | copy-start | bytes 12292
